TPU v7x, 256 devices: a whole 4x4x8 slice. The times are simulated.
256 devices in a mesh: dp: 8 (over z), frame: 8 (over x, core), audio: 4 (over y).
Axes of the slice: x: 4, y: 4, z: 8, core: 2. Of those that a mesh axis runs over, the one named last changes fastest.
Arguments:
- video_query: bfloat16 [8, 4096, 3072], P('dp', ('frame', 'audio')), may hold values from -72 to 72
- out_grad: bfloat16 [8, 4096, 3072], P('dp', ('frame', 'audio')), may hold values from -6 to 6
- audio_latents: bfloat16 [8, 1024, 3072], P('dp', 'audio'), may hold values from -6 to 6
- kv_weight: bfloat16 [3072, 2, 3072], P(None, None, 'frame'), may hold values from -0.4375 to 0.4375
- video_length: int32 [8], P('dp'), may hold values from 1024 to 4096, as said below
- audio_length: int32 [8], P('dp'), may hold values from 128 to 1024, as said below
- align_list: int32 [8, 32, 2], P('dp'), may hold values from 0 to 15, as said below
Outputs:
- attended: bfloat16 [8, 4096, 3072], P('dp', ('frame', 'audio'))
- query_grad: bfloat16 [8, 4096, 3072], P('dp', ('frame', 'audio'))
- kv_weight_grad: float32 [3072, 2, 3072], P(('dp', 'audio'), None, 'frame')
Inputs may be any that keep to these rules, and one draw needn't show every extreme that they name: `video_length`: one clip of every draw has all 4096 tokens live. `audio_length`: one clip of every draw has all 1024 latents live. `align_list`: for clip c and query block b the 2 entries are distinct and each is below ceil(audio_length[c] / 64); the first is b * ceil(audio_length[c] / 64) // 32.
All inputs are finite; a program needn't handle non-finite values.
Results may differ from a plain program's by a relative error of at most 0.004.
The roundings to bfloat16 on the way count: a program that leaves them out, or rounds other values in their place, can miss the bound.
Values may be sent and summed in bfloat16 or wider, within the bound.
No kernel may reach another device: no remote copies, remote signals or barrier semaphores. Data moves between devices by JAX's collectives and lax.ppermute only.
A program may use at most 128 MiB of HBM per device.

v0:
```python
import jax
import jax.numpy as jnp
from jax import lax
from jax.sharding import PartitionSpec as P

D = 3072
HD = 128
QB = 128
KB = 64
NLIST = 2


def from_everyone(array, axis):
    copies = jnp.broadcast_to(array, (lax.axis_size(axis), *array.shape))
    return lax.all_to_all(copies, axis, split_axis=0, concat_axis=0, tiled=True)


def joined_along(pieces, dim):
    pieces = jnp.moveaxis(pieces, 0, dim)
    lengths = pieces.shape
    return pieces.reshape(*lengths[:dim], lengths[dim] * lengths[dim + 1], *lengths[dim + 2 :])


def gathered_copies(array, axis, dim):
    pieces = from_everyone(array, axis)
    return joined_along(pieces, dim)


def in_blocks(array, dim, count):
    before, after = (array.shape[:dim], array.shape[dim + 1 :])
    return jnp.moveaxis(array.reshape(*before, count, -1, *after), dim, 0)


def sum_at_owner(array, axis, dim):
    pieces = in_blocks(array, dim, lax.axis_size(axis))
    arrived = lax.all_to_all(pieces, axis, split_axis=0, concat_axis=0, tiled=True)
    return arrived.sum(axis=0)


def summed_rows(so_far, axes):
    for axis in axes:
        so_far = lax.psum_scatter(so_far, axis, scatter_dimension=0, tiled=True)
    return so_far


def softmax_core(query_rows, grad_rows, key_rows, value_rows, allowed, live_rows):
    scaling = HD ** (-0.5)
    scores = (
        jnp.einsum("bqhd,bkhd->bhqk", query_rows, key_rows, preferred_element_type=jnp.float32)
        * scaling
    )
    scores = jnp.where(allowed[:, None], scores, -1e30)
    scores = scores - jnp.max(scores, axis=-1, keepdims=True)
    weights = jnp.exp(scores)
    probability = weights / jnp.sum(weights, axis=-1, keepdims=True)
    probability = jnp.where(live_rows[:, None, :, None], probability, 0.0)
    prob_low = probability.astype(jnp.bfloat16)
    output = jnp.einsum(
        "bhqk,bkhd->bqhd", prob_low, value_rows, preferred_element_type=jnp.float32
    ).astype(jnp.bfloat16)
    prob_grad = jnp.einsum(
        "bqhd,bkhd->bhqk", grad_rows, value_rows, preferred_element_type=jnp.float32
    )
    row_dot = jnp.sum(probability * prob_grad, axis=-1, keepdims=True)
    score_grad = (probability * (prob_grad - row_dot)).astype(jnp.bfloat16)
    query_part = (
        jnp.einsum("bhqk,bkhd->bqhd", score_grad, key_rows, preferred_element_type=jnp.float32)
        * scaling
    )
    key_part = (
        jnp.einsum("bhqk,bqhd->bkhd", score_grad, query_rows, preferred_element_type=jnp.float32)
        * scaling
    )
    value_part = jnp.einsum(
        "bhqk,bqhd->bkhd", prob_low, grad_rows, preferred_element_type=jnp.float32
    )
    return (output, query_part.astype(jnp.bfloat16), jnp.stack([key_part, value_part], axis=2))


def attend_listed(
    queries, cotangent, positions, key_table, block_lists, video_live, audio_live, heads
):
    row_total = queries.shape[0]
    key_count = key_table.shape[0]
    block_count = key_count // KB
    head_width = heads * HD
    query_count = row_total // QB
    blocks = key_table.reshape(block_count, KB, 2, heads, HD)
    row_index = positions.reshape(query_count, QB)
    listed = block_lists[row_index[:, 0] // QB]
    chosen = jnp.take(blocks, listed, axis=0).reshape(query_count, NLIST * KB, 2, heads, HD)
    key_index = (listed[:, :, None] * KB + jnp.arange(KB)[None, None, :]).reshape(
        query_count, NLIST * KB
    )
    allowed = jnp.broadcast_to((key_index < audio_live)[:, None, :], (query_count, QB, NLIST * KB))
    output, query_part, grad_part = softmax_core(
        queries.reshape(query_count, QB, heads, HD),
        cotangent.reshape(query_count, QB, heads, HD),
        chosen[:, :, 0],
        chosen[:, :, 1],
        allowed,
        row_index < video_live,
    )
    onehot = (listed.reshape(-1)[:, None] == jnp.arange(block_count)[None, :]).astype(jnp.float32)
    grad_part = grad_part.reshape(query_count * NLIST, KB, 2 * head_width)
    summed = jnp.einsum("sn,skx->nkx", onehot, grad_part, precision=lax.Precision.HIGHEST)
    return (
        output.reshape(row_total, head_width),
        query_part.reshape(row_total, head_width),
        summed.reshape(key_count, 2 * head_width),
    )


def attend(queries, cotangent, positions, key_table, block_lists, video_live, audio_live, heads):
    return attend_listed(
        queries, cotangent, positions, key_table, block_lists, video_live, audio_live, heads
    )


def per_device(
    video_query, out_grad, audio_latents, kv_weight, video_length, audio_length, align_list
):
    frames = lax.axis_size("frame")
    audio_count = lax.axis_size("audio")
    audio_at = lax.axis_index("audio")
    queries = video_query[0]
    cotangent = out_grad[0]
    latents = audio_latents[0]
    shard_rows = queries.shape[0]
    local_width = kv_weight.shape[2]
    video_live = video_length[0]
    audio_live = audio_length[0]
    block_lists = align_list[0]
    projected = jnp.dot(
        latents, kv_weight.reshape(D, 2 * local_width), preferred_element_type=jnp.float32
    ).astype(jnp.bfloat16)
    head_queries, head_cotangent = (
        lax.all_to_all(queries, "frame", split_axis=1, concat_axis=0, tiled=True),
        lax.all_to_all(cotangent, "frame", split_axis=1, concat_axis=0, tiled=True),
    )
    key_table = gathered_copies(projected, "audio", 0)
    source = jnp.arange(frames * shard_rows) // shard_rows
    offset = jnp.arange(frames * shard_rows) % shard_rows
    positions = (source * audio_count + audio_at) * shard_rows + offset
    attended, query_grad, key_part = attend(
        head_queries,
        head_cotangent,
        positions,
        key_table,
        block_lists,
        video_live,
        audio_live,
        local_width // HD,
    )
    attended, query_grad = (
        lax.all_to_all(attended, "frame", split_axis=0, concat_axis=1, tiled=True),
        lax.all_to_all(query_grad, "frame", split_axis=0, concat_axis=1, tiled=True),
    )
    key_grad = sum_at_owner(key_part, "audio", 0)
    key_grad = key_grad.astype(jnp.bfloat16)
    clip_count = lax.axis_size("dp")
    weight_rows = D // (clip_count * audio_count)
    product = lax.dot_general(
        latents, key_grad, (((0,), (0,)), ((), ())), preferred_element_type=jnp.float32
    )
    weight_grad = summed_rows(product * (1.0 / clip_count), ("dp", "audio"))
    return (attended[None], query_grad[None], weight_grad.reshape(weight_rows, 2, local_width))


def solution(mesh):
    return jax.shard_map(
        per_device,
        mesh=mesh,
        in_specs=(
            P("dp", ("frame", "audio"), None),
            P("dp", ("frame", "audio"), None),
            P("dp", "audio", None),
            P(None, None, "frame"),
            P("dp"),
            P("dp"),
            P("dp", None, None),
        ),
        out_specs=(
            P("dp", ("frame", "audio"), None),
            P("dp", ("frame", "audio"), None),
            P(("dp", "audio"), None, "frame"),
        ),
        check_vma=False,
    )
```

profile of v0, /device:TPU:1, one launch (start us, length us, event | category | flops | bytes accessed | tf_op | source)
XLA Modules:
  0.0 298.6 jit_solution(10806674023518532897)
XLA Ops:
  7.2 2.4 copy.49
  9.6 6.6 %all-to-all-start.1 = ((bf16[128,8,384]{0,2,1:T(8,128)(2,1)}), bf16[128,8,384]{0,2,1:T(8,128)(2,1)S(1)}, u32[]{:S(2)}, u32[]{:S(2)}) async-start(bf16[128,8,384]{0,2,1:T(8,128)(2,1)} %bitcast.9), calls=%async_computation.1 | async-start | bytes 1572864 | tf_op jit(solution)/shard_map/all_to_all | solution.py:138
  16.2 3.1 %copy.79 = bf16[384,8,2,384]{3,1,2,0:T(8,128)(2,1)S(1)} copy(bf16[384,8,2,384]{3,2,1,0:T(2,128)(2,1)} %bitcast.100) | data formatting | bytes 9437184
  19.5 1.4 fusion.14
  20.9 7.5 %all-to-all-done.1 = bf16[128,8,384]{0,2,1:T(8,128)(2,1)S(1)} async-done(((bf16[128,8,384]{0,2,1:T(8,128)(2,1)}), bf16[128,8,384]{0,2,1:T(8,128)(2,1)S(1)}, u32[]{:S(2)}, u32[]{:S(2)}) %all-to-all-start.1) | async-done | bytes 786464 | tf_op jit(solution)/shard_map/all_to_all | solution.py:138
  28.4 1.3 broadcast_in_dim.59
  29.8 3.6 %all-to-all-start = ((bf16[4,256,768]{2,1,0:T(8,128)(2,1)}), bf16[4,256,768]{2,1,0:T(8,128)(2,1)S(1)}, u32[]{:S(2)}, u32[]{:S(2)}) async-start(bf16[4,256,768]{2,1,0:T(8,128)(2,1)} %broadcast_in_dim.59), calls=%async_computation | async-start | bytes 3145728 | tf_op jit(solution)/shard_map/all_to_all | solution.py:15
  36.3 2.3 copy.54
  38.6 14.5 %all-to-all-done = bf16[4,256,768]{2,1,0:T(8,128)(2,1)S(1)} async-done(((bf16[4,256,768]{2,1,0:T(8,128)(2,1)}), bf16[4,256,768]{2,1,0:T(8,128)(2,1)S(1)}, u32[]{:S(2)}, u32[]{:S(2)}) %all-to-all-start) | async-done | bytes 1572896 | tf_op jit(solution)/shard_map/all_to_all | solution.py:15
  53.2 5.9 %all-to-all-start.3 = ((bf16[128,8,384]{0,2,1:T(8,128)(2,1)}), bf16[128,8,384]{0,2,1:T(8,128)(2,1)}, u32[]{:S(2)}, u32[]{:S(2)}) async-start(bf16[128,8,384]{0,2,1:T(8,128)(2,1)} %bitcast.102), calls=%async_computation.3 | async-start | bytes 1572864 | tf_op jit(solution)/shard_map/all_to_all | solution.py:139
  59.1 2.2 reshape_reshape.6
  61.3 5.1 %gather_fusion.1 = bf16[16,64,2,3,128]{4,3,2,1,0:T(4,128)(2,1)} fusion(bf16[16,64,2,3,128]{4,3,2,1,0:T(4,128)(2,1)} %reshape_reshape.6, s32[1024]{0:T(1024)S(1)} %pad_clamp_fusion), kind=kCustom, calls=%fused_computation.1 | custom fusion | bytes 3145792 | tf_op jit(solution)/shard_map/jit(_take)/gather | solution.py:91
  66.4 1.9 copy_select_fusion
  68.3 3.5 %fusion.34 = (f32[8,3,128]{2,1,0:T(4,128)S(1)}, f32[8,3,128,128]{2,3,1,0:T(8,128)}) fusion(bf16[8,128,3,128]{1,3,2,0:T(8,128)(2,1)} %bitcast.105, bf16[8,128,2,3,128]{4,1,3,0,2:T(8,128)(2,1)S(1)} %copy_select_fusion, pred[8,128]{1,0:T(8,128)(4,1)S(1)} %add_compare_fusion), kind=kOutput, calls=%fused_computation.66 | convolution fusion | flops 102236288 | bytes 3159040 | tf_op jit(solution)/shard_map/sub | solution.py:53
  71.8 2.4 convolution_bitcast_fusion
  74.2 1.6 fusion.4
  77.9 4.1 %copy.61 = f32[8,128,2,3,128]{4,3,2,1,0:T(4,128)} copy(f32[8,128,2,3,128]{4,1,3,0,2:T(8,128)S(1)} %pad_maximum_fusion) | data formatting | bytes 6291456 | tf_op jit(solution)/shard_map/stack | solution.py:77
  82.0 6.0 %reshape.132 = f32[16,64,768]{2,1,0:T(8,128)} reshape(f32[8,128,2,3,128]{4,3,2,1,0:T(4,128)} %copy.61) | data formatting | bytes 6291456 | tf_op jit(solution)/shard_map/reshape | solution.py:105
  88.0 5.2 %fusion.1 = f32[16,64,768]{2,0,1:T(8,128)S(1)} fusion(f32[16,64,768]{2,1,0:T(8,128)} %reshape.132, s32[16]{0:T(128)S(1)} %eq.17), kind=kOutput, calls=%fused_computation.5 | convolution fusion | flops 150995200 | bytes 6291520 | tf_op jit(solution)/shard_map/sn,skx->nkx/dot_general | solution.py:106
  93.2 1.8 copy.63
  95.0 40.5 %all_to_all.74 = f32[4,256,768]{2,1,0:T(8,128)} all-to-all(f32[4,256,768]{2,1,0:T(8,128)S(1)} %bitcast.98), channel_id=1, replica_groups=mesh['dp'=8,'frame'=8,'audio'=4] {'audio'}, dimensions={0} | all-to-all | bytes 6291456 | tf_op jit(solution)/shard_map/all_to_all | solution.py:36
  135.5 2.1 reduce_sum.29
  137.6 5.0 %multiply_bitcast_fusion = f32[3072,768]{0,1:T(8,128)} fusion(bf16[1,256,3072]{2,1,0:T(8,128)(2,1)S(1)} %copy-done, bf16[256,768]{1,0:T(8,128)(2,1)S(1)} %reduce_sum.29), kind=kOutput, calls=%fused_computation.3 | convolution fusion | flops 1210318848 | bytes 11403264 | tf_op jit(solution)/shard_map/dot_general | solution.py:163
  142.7 106.5 %reduce-scatter.5.cloned.1.call-done = f32[384,768]{0,1:T(8,128)} async-done(((f32[3072,768]{0,1:T(8,128)}), f32[384,768]{0,1:T(8,128)}) %reduce-scatter.5.cloned.1.call-update) | async-done | bytes 1179664 | tf_op jit(solution)/shard_map/reduce_scatter | solution.py:42
  249.2 2.7 copy.77
  251.9 3.0 convolution_convert_fusion
  254.8 5.0 %all-to-all-start.2 = ((bf16[8,128,384]{1,2,0:T(8,128)(2,1)}), bf16[8,128,384]{1,2,0:T(8,128)(2,1)S(1)}, u32[]{:S(2)}, u32[]{:S(2)}) async-start(bf16[8,128,384]{1,2,0:T(8,128)(2,1)} %bitcast.109), calls=%async_computation.2 | async-start | bytes 1572864 | tf_op jit(solution)/shard_map/all_to_all | solution.py:156
  259.8 2.5 multiply_convert_fusion
  262.4 9.6 %all-to-all-done.2 = bf16[8,128,384]{1,2,0:T(8,128)(2,1)S(1)} async-done(((bf16[8,128,384]{1,2,0:T(8,128)(2,1)}), bf16[8,128,384]{1,2,0:T(8,128)(2,1)S(1)}, u32[]{:S(2)}, u32[]{:S(2)}) %all-to-all-start.2) | async-done | bytes 786464 | tf_op jit(solution)/shard_map/all_to_all | solution.py:156
  272.0 4.4 %all-to-all-start.4 = ((bf16[8,128,384]{1,2,0:T(8,128)(2,1)}), bf16[8,128,384]{1,2,0:T(8,128)(2,1)S(1)}, u32[]{:S(2)}, u32[]{:S(2)}) async-start(bf16[8,128,384]{1,2,0:T(8,128)(2,1)} %bitcast.107), calls=%async_computation.4 | async-start | bytes 1572864 | tf_op jit(solution)/shard_map/all_to_all | solution.py:157
  277.6 11.0 %all-to-all-done.4 = bf16[8,128,384]{1,2,0:T(8,128)(2,1)S(1)} async-done(((bf16[8,128,384]{1,2,0:T(8,128)(2,1)}), bf16[8,128,384]{1,2,0:T(8,128)(2,1)S(1)}, u32[]{:S(2)}, u32[]{:S(2)}) %all-to-all-start.4) | async-done | bytes 786464 | tf_op jit(solution)/shard_map/all_to_all | solution.py:157
  288.6 1.2 copy.76
  (46 shorter events, 7.0 us)
Async XLA Ops:
  7.2 12.3 %copy-start = (bf16[1,256,3072]{2,1,0:T(8,128)(2,1)S(1)}, bf16[1,256,3072]{2,1,0:T(8,128)(2,1)}, u32[]{:S(2)}) copy-start(bf16[1,256,3072]{2,1,0:T(8,128)(2,1)} %param.9) | copy-start | bytes 4718596
  9.6 18.8 %all-to-all-start.1 = ((bf16[128,8,384]{0,2,1:T(8,128)(2,1)}), bf16[128,8,384]{0,2,1:T(8,128)(2,1)S(1)}, u32[]{:S(2)}, u32[]{:S(2)}) async-start(bf16[128,8,384]{0,2,1:T(8,128)(2,1)} %bitcast.9), calls=%async_computation.1 | async-start | bytes 1572864 | tf_op jit(solution)/shard_map/all_to_all | solution.py:138
  28.4 1.4 copy-start.2
  29.8 3.6 %copy-start.5 = (s32[1,32,2]{1,2,0:T(2,128)S(1)}, s32[1,32,2]{1,2,0:T(2,128)}, u32[]{:S(2)}) copy-start(s32[1,32,2]{1,2,0:T(2,128)} %param.13) | copy-start | bytes 772
  29.8 23.3 %all-to-all-start = ((bf16[4,256,768]{2,1,0:T(8,128)(2,1)}), bf16[4,256,768]{2,1,0:T(8,128)(2,1)S(1)}, u32[]{:S(2)}, u32[]{:S(2)}) async-start(bf16[4,256,768]{2,1,0:T(8,128)(2,1)} %broadcast_in_dim.59), calls=%async_computation | async-start | bytes 3145728 | tf_op jit(solution)/shard_map/all_to_all | solution.py:15
  53.2 18.6 %all-to-all-start.3 = ((bf16[128,8,384]{0,2,1:T(8,128)(2,1)}), bf16[128,8,384]{0,2,1:T(8,128)(2,1)}, u32[]{:S(2)}, u32[]{:S(2)}) async-start(bf16[128,8,384]{0,2,1:T(8,128)(2,1)} %bitcast.102), calls=%async_computation.3 | async-start | bytes 1572864 | tf_op jit(solution)/shard_map/all_to_all | solution.py:139
  59.1 190.1 %reduce-scatter.5.cloned.1.call-start = ((), (), s32[]{:S(2)}) async-start(), calls=%async_computation.8 | async-start | bytes 10616832 | tf_op jit(solution)/shard_map/reduce_scatter | solution.py:42
  68.3 5.9 %copy-start.1 = (bf16[8,128,2,3,128]{4,1,3,0,2:T(8,128)(2,1)}, bf16[8,128,2,3,128]{4,1,3,0,2:T(8,128)(2,1)S(1)}, u32[]{:S(2)}) copy-start(bf16[8,128,2,3,128]{4,1,3,0,2:T(8,128)(2,1)S(1)} %copy_select_fusion) | copy-start | bytes 4718596
  71.8 2.4 copy-start.4
  75.8 1.1 copy-start.3
  142.7 147.1 %reduce-scatter.7.cloned.1.call-start = ((), (), s32[]{:S(2)}) async-start(), calls=%async_computation.9 | async-start | bytes 1474560
  254.8 17.2 %all-to-all-start.2 = ((bf16[8,128,384]{1,2,0:T(8,128)(2,1)}), bf16[8,128,384]{1,2,0:T(8,128)(2,1)S(1)}, u32[]{:S(2)}, u32[]{:S(2)}) async-start(bf16[8,128,384]{1,2,0:T(8,128)(2,1)} %bitcast.109), calls=%async_computation.2 | async-start | bytes 1572864 | tf_op jit(solution)/shard_map/all_to_all | solution.py:156
  272.0 16.6 %all-to-all-start.4 = ((bf16[8,128,384]{1,2,0:T(8,128)(2,1)}), bf16[8,128,384]{1,2,0:T(8,128)(2,1)S(1)}, u32[]{:S(2)}, u32[]{:S(2)}) async-start(bf16[8,128,384]{1,2,0:T(8,128)(2,1)} %bitcast.107), calls=%async_computation.4 | async-start | bytes 1572864 | tf_op jit(solution)/shard_map/all_to_all | solution.py:157
Sparse Core Ops, SparseCore 0:
  142.8 106.3 reduce-scatter.4
  252.0 23.8 reduce-scatter.6
where the time goes:
time: 300 us; the launch traced here: 299 us
  waiting for transfers between devices  149 us (50%)
  blocking collectives  40.5 us (14%)
  local copies, waits for them, and re-layouts  37.7 us (13%)
  starting transfers between devices  25.6 us (9%)
  matrix products  25.3 us (8%)
  between operations  15.5 us (5%)
  other arithmetic  4.87 us (2%)
    reduce_scatter x1, waiting for transfers between devices, summed_rows(): so_far = lax.psum_scatter(so_far, axis, scatter_dimension=0, tiled=True)  106 us
    all_to_all x1, blocking collectives, sum_at_owner(): lax.all_to_all(pieces, axis, split_axis=0, concat_axis=0, tiled=True)  40.5 us
    all_to_all x1, waiting for transfers between devices, from_everyone(): return lax.all_to_all(copies, axis, split_axis=0, concat_axis=0, tiled=True)  14.5 us
    unnamed x18, local copies, waits for them, and re-layouts  13.3 us
    all_to_all x1, waiting for transfers between devices, per_device(): lax.all_to_all(query_grad, 'frame', split_axis=0, concat_axis=1, tiled=True)  11 us
    all_to_all x1, waiting for transfers between devices, per_device(): lax.all_to_all(attended, 'frame', split_axis=0, concat_axis=1, tiled=True)  9.64 us
    all_to_all x1, waiting for transfers between devices, per_device(): lax.all_to_all(queries, 'frame', split_axis=1, concat_axis=0, tiled=True)  7.53 us
    all_to_all x1, starting transfers between devices, per_device(): lax.all_to_all(queries, 'frame', split_axis=1, concat_axis=0, tiled=True)  6.65 us
  transfers between devices with their start and end apart: 7, of which 5 were waited for; matrix products, arithmetic and copies ran while one was open for 10% of the time, Pallas kernels for 0%

commit v1 on v0

v1 whole, which is shorter than its diff:
```python
import jax
import jax.numpy as jnp
from jax import lax
from jax.experimental import pallas as pl
from jax.experimental.pallas import tpu as pltpu
from jax.sharding import PartitionSpec as P


D = 3072
HD = 128
QB = 128
KB = 64
NLIST = 2
SCALING = HD ** (-0.5)
LOG2_E = 1.4426950408889634
BF16 = jnp.bfloat16
F32 = jnp.float32


VMEM = pl.BlockSpec(memory_space=pltpu.VMEM)
SMEM = pl.BlockSpec(memory_space=pltpu.SMEM)
ANY = pl.BlockSpec(memory_space=pl.ANY)


def shifted(array, axis, by):
    count = lax.axis_size(axis)
    return lax.ppermute(array, axis, [(i, (i + by) % count) for i in range(count)])


def pack_kernel(query, grad, out):
    width = out.shape[3]
    for j in range(out.shape[0]):
        out[j, 0] = query[:, j * width : (j + 1) * width]
        out[j, 1] = grad[:, j * width : (j + 1) * width]


def pack(query, grad, frames):
    rows, width = query.shape
    return pl.pallas_call(
        pack_kernel,
        out_shape=jax.ShapeDtypeStruct((frames, 2, rows, width // frames), query.dtype),
        in_specs=[VMEM, VMEM],
        out_specs=VMEM,
        name="pack",
    )(query, grad)


def unpack_kernel(pieces, attended, query_grad):
    width = pieces.shape[3]
    for j in range(pieces.shape[0]):
        attended[:, j * width : (j + 1) * width] = pieces[j, 0]
        query_grad[:, j * width : (j + 1) * width] = pieces[j, 1]


def unpack(pieces):
    frames, _, rows, width = pieces.shape
    whole = jax.ShapeDtypeStruct((rows, width * frames), pieces.dtype)
    return pl.pallas_call(
        unpack_kernel,
        out_shape=[whole, whole],
        in_specs=[VMEM],
        out_specs=[VMEM, VMEM],
        name="unpack",
    )(pieces)


def turn_kernel(ids, latents, own, *refs):
    sends, turned = refs[:-1], refs[-1]
    _, count, rows, _ = own.shape
    audio_count = len(sends) + 1
    width = rows * audio_count
    parity = lax.rem(ids[1], 2)
    for group in range(2):
        for j in range(count):
            owner = 2 * j + (parity if group == 0 else 1 - parity)
            turned[...] = latents[:, pl.ds(pl.multiple_of(owner * width, HD), width)].T
            own[group, j] = turned[pl.ds(pl.multiple_of(ids[0] * rows, 16), rows), :]

            @pl.when(ids[2] == group)
            def _():
                for k in range(1, audio_count):
                    first = pl.multiple_of(lax.rem(ids[0] + k, audio_count) * rows, 16)
                    sends[k - 1][j] = turned[pl.ds(first, rows), :]


def turn(ids, latents, clips, audio_count):
    count, width = latents.shape
    rows = width // (clips * audio_count)
    shape = (clips // 2, rows, count)
    return pl.pallas_call(
        turn_kernel,
        out_shape=[jax.ShapeDtypeStruct((2, *shape), latents.dtype)]
        + [jax.ShapeDtypeStruct(shape, latents.dtype)] * (audio_count - 1),
        in_specs=[SMEM, VMEM],
        out_specs=[VMEM] * audio_count,
        scratch_shapes=[pltpu.VMEM((rows * audio_count, count), latents.dtype)],
        name="turn",
    )(ids, latents)


def dot(left, right, left_dim, right_dim):
    return lax.dot_general(
        left, right, (((left_dim,), (right_dim,)), ((), ())), preferred_element_type=F32
    )


def attend_kernel(audio_count, heads, ids, video_live, audio_live, lists, *refs):
    refs = list(refs)
    take = lambda n: [refs.pop(0) for _ in range(n)]
    (arrived,), tables = take(1), take(audio_count)
    (results,), grads = take(1), take(2 * audio_count)
    rows_in, table, rows_out = take(3)
    sums = take(2 * heads)
    in_sem, table_sem, out_sem = take(3)
    frames = arrived.shape[0]
    share = tables[0].shape[0]
    here = ids[0]

    copies = []
    for k in range(audio_count):
        at = pl.multiple_of(lax.rem(here + audio_count - k, audio_count) * share, share)
        copies.append(
            pltpu.make_async_copy(tables[k], table.at[pl.ds(at, share), :], table_sem.at[k])
        )
    copies.append(pltpu.make_async_copy(arrived, rows_in, in_sem))
    for copy in copies:
        copy.start()
    for part in sums:
        part[...] = jnp.zeros_like(part)
    for copy in copies:
        copy.wait()

    key_row = lax.broadcasted_iota(jnp.int32, (NLIST * KB, 1), 0)
    query_lane = lax.broadcasted_iota(jnp.int32, (1, QB), 1)

    def one(k):
        index = k * audio_count + here
        first = pl.multiple_of(lists[NLIST * index] * KB, KB)
        second = pl.multiple_of(lists[NLIST * index + 1] * KB, KB)
        key_index = jnp.where(key_row < KB, first + key_row, second + key_row - KB)
        allowed = key_index < audio_live[0]
        live = query_lane + index * QB < video_live[0]
        parts = []
        for h in range(heads):
            cols = slice(h * HD, (h + 1) * HD)
            vcols = slice((heads + h) * HD, (heads + h + 1) * HD)
            query = rows_in[k, 0, :, cols]
            grad = rows_in[k, 1, :, cols]
            key = jnp.concatenate(
                [table[pl.ds(first, KB), cols], table[pl.ds(second, KB), cols]], axis=0
            )
            value = jnp.concatenate(
                [table[pl.ds(first, KB), vcols], table[pl.ds(second, KB), vcols]], axis=0
            )
            scores = dot(key, query, 1, 1)
            prob_grad = dot(value, grad, 1, 1)
            scores = jnp.where(allowed, scores, -1e30)
            scores = scores - jnp.max(scores, axis=0, keepdims=True)
            weights = jnp.exp2(scores * (SCALING * LOG2_E))
            inverse = 1.0 / jnp.sum(weights, axis=0, keepdims=True)
            probability = weights * jnp.where(live, inverse, 0.0)
            prob_low = probability.astype(BF16)
            row_dot = jnp.sum(probability * prob_grad, axis=0, keepdims=True)
            score_grad = (probability * (prob_grad - row_dot)).astype(BF16)
            output = dot(prob_low, value, 0, 0).astype(BF16)
            query_part = (dot(score_grad, key, 0, 0) * SCALING).astype(BF16)
            key_part = dot(score_grad, query, 1, 0) * SCALING
            value_part = dot(prob_low, grad, 1, 0)
            parts.append((output, query_part, key_part, value_part))
        return first, second, parts

    def finish(k, first, second, parts):
        for h, (output, query_part, key_part, value_part) in enumerate(parts):
            cols = slice(h * HD, (h + 1) * HD)
            rows_out[k, 0, :, cols] = output
            rows_out[k, 1, :, cols] = query_part
            for into, part in ((sums[h], key_part), (sums[heads + h], value_part)):
                into[pl.ds(first, KB), :] += part[:KB]
                into[pl.ds(second, KB), :] += part[KB:]

    def block(step, carry):
        made = [(2 * step + i, *one(2 * step + i)) for i in range(2)]
        for entry in made:
            finish(*entry)
        return carry

    lax.fori_loop(0, frames // 2, block, 0)

    copy = pltpu.make_async_copy(rows_out, results, out_sem)
    copy.start()
    for k in range(audio_count):
        at = pl.multiple_of(lax.rem(here + k, audio_count) * share, share)
        for half in range(2):
            into = grads[2 * k + half]
            for h in range(heads):
                part = sums[half * heads + h][pl.ds(at, share), :]
                into[:, h * HD : (h + 1) * HD] = part.astype(into.dtype)
    copy.wait()


def attend(ids, video_live, audio_live, lists, arrived, tables):
    audio_count = len(tables)
    share, width = tables[0].shape
    heads = width // (2 * HD)
    total = share * audio_count

    def kernel(*refs):
        attend_kernel(audio_count, heads, *refs)

    results, *grads = pl.pallas_call(
        kernel,
        out_shape=[jax.ShapeDtypeStruct(arrived.shape, BF16)]
        + [jax.ShapeDtypeStruct((share, width // 2), F32)] * 2
        + [jax.ShapeDtypeStruct((share, width // 2), BF16)] * (2 * audio_count - 2),
        in_specs=[SMEM] * 4 + [ANY] * (1 + audio_count),
        out_specs=[ANY] + [VMEM] * (2 * audio_count),
        scratch_shapes=[
            pltpu.VMEM(arrived.shape, BF16),
            pltpu.VMEM((total, width), BF16),
            pltpu.VMEM(arrived.shape, BF16),
        ]
        + [pltpu.VMEM((total, HD), F32)] * (2 * heads)
        + [
            pltpu.SemaphoreType.DMA,
            pltpu.SemaphoreType.DMA((audio_count,)),
            pltpu.SemaphoreType.DMA,
        ],
        name="attend",
    )(ids, video_live, audio_live, lists, arrived, *tables)
    return results, grads


def product_kernel(scale, hops, ids, own, *refs):
    refs = list(refs)
    take = lambda n: [refs.pop(0) for _ in range(n)]
    mine, other, grads = take(hops), take(hops), take(hops + 1)
    kept, sent, turned, sems = take(4)
    core = ids[2]
    copies = []
    for k in range(hops):
        for i, (ref, at) in enumerate(((mine[k], core), (other[k], 1 - core))):
            copies.append(pltpu.make_async_copy(ref, turned.at[k, at], sems.at[k, i]))
    for copy in copies:
        copy.start()
    for copy in copies:
        copy.wait()
    for group, out in enumerate((kept, sent)):
        for j in range(out.shape[0]):
            total = dot(own[group, j], grads[0][...], 1, 0)
            for k in range(hops):
                total += dot(turned[k, group, j], grads[k + 1][...], 1, 0)
            out[j] = (total * scale).astype(out.dtype)


def product(ids, own, mine, other, grads, scale):
    _, count, rows, _ = own.shape
    width = grads[0].shape[1]
    hops = len(mine)

    def kernel(*refs):
        product_kernel(scale, hops, *refs)

    return pl.pallas_call(
        kernel,
        out_shape=[
            jax.ShapeDtypeStruct((count, rows, width), F32),
            jax.ShapeDtypeStruct((count, rows, width), BF16),
        ],
        in_specs=[SMEM, VMEM] + [ANY] * (2 * hops) + [VMEM] * (hops + 1),
        out_specs=[VMEM, VMEM],
        scratch_shapes=[
            pltpu.VMEM((hops, *own.shape), own.dtype),
            pltpu.SemaphoreType.DMA((hops, 2)),
        ],
        name="product",
    )(ids, own, *mine, *other, *grads)


def merge_kernel(ids, key_kept, value_kept, key_came, value_came, *outs):
    count = len(outs)
    width = key_kept.shape[2]
    for s in range(count):
        at = lax.rem(lax.div(ids[1], 2) + s, count)
        key = key_kept[at] + key_came[at].astype(F32)
        value = value_kept[at] + value_came[at].astype(F32)
        outs[s][:, :width] = key.astype(outs[s].dtype)
        outs[s][:, width:] = value.astype(outs[s].dtype)


def merge(ids, key_kept, value_kept, key_came, value_came):
    count, rows, width = key_kept.shape
    shape = (rows, 2 * width)
    return pl.pallas_call(
        merge_kernel,
        out_shape=[jax.ShapeDtypeStruct(shape, F32)]
        + [jax.ShapeDtypeStruct(shape, BF16)] * (count - 1),
        in_specs=[SMEM] + [VMEM] * 4,
        out_specs=[VMEM] * count,
        name="merge",
    )(ids, key_kept, value_kept, key_came, value_came)


def total_of(pieces):
    total = pieces[0]
    for piece in pieces[1:]:
        total = total + piece.astype(F32)
    return total


def to_owners(array, axis):
    return lax.all_to_all(array, axis, split_axis=0, concat_axis=0, tiled=True)


def per_device(
    video_query, out_grad, audio_latents, kv_weight, video_length, audio_length, align_list
):
    frames = lax.axis_size("frame")
    audio_count = lax.axis_size("audio")
    clips = lax.axis_size("dp")
    local_width = kv_weight.shape[2]
    latents = audio_latents[0]
    ids = [
        lax.axis_index("audio"),
        lax.axis_index("dp"),
        lax.rem(lax.axis_index("frame"), 2),
    ]
    ids = jnp.stack(ids).astype(jnp.int32)
    beside = [(i, i ^ 1) for i in range(frames)]
    before = [(i, i ^ 1) for i in range(clips)]
    after = [(i, (((i + 1) % clips) ^ 1) - 1) for i in range(clips)]
    after = [(i, j % clips) for i, j in after]
    hops = range(1, audio_count)

    packed = pack(video_query[0], out_grad[0], frames)
    arrived = to_owners(packed, "frame")
    projected = jnp.dot(
        latents, kv_weight.reshape(D, 2 * local_width), preferred_element_type=F32
    ).astype(BF16)
    tables = [projected]
    for k in hops:
        tables.append(shifted(projected, "audio", k))
    held, *pieces = turn(ids, latents, clips, audio_count)
    turned = []
    for k in hops:
        turned.append(shifted(pieces[k - 1], "audio", k))

    results, grads = attend(
        ids, video_length, audio_length, align_list.reshape(-1), arrived, tables
    )
    own = []
    for half in (1, 0):
        added = [grads[half]]
        for k in hops:
            added.append(shifted(grads[2 * k + half], "audio", k))
        own.append(total_of(added).astype(BF16))
    results = to_owners(results, "frame")
    swapped = []
    for k in hops:
        swapped.append(lax.ppermute(turned[k - 1], "frame", beside))
    halves = []
    for mine, partner in zip(own, (before, after)):
        shares = [mine]
        for k in hops:
            shares.append(shifted(mine, "audio", k))
        kept, sent = product(ids, held, turned, swapped, shares, 1.0 / clips)
        halves.append((kept, lax.ppermute(sent, "dp", partner)))
    (value_kept, value_came), (key_kept, key_came) = halves
    merged = merge(ids, key_kept, value_kept, key_came, value_came)
    parts = [merged[0]]
    for k in range(1, len(merged)):
        parts.append(shifted(merged[k], "dp", 2 * k))
    weight_grad = total_of(parts).reshape(-1, 2, local_width)
    attended, query_grad = unpack(results)
    return attended[None], query_grad[None], weight_grad


def solution(mesh):
    return jax.shard_map(
        per_device,
        mesh=mesh,
        in_specs=(
            P("dp", ("frame", "audio"), None),
            P("dp", ("frame", "audio"), None),
            P("dp", "audio", None),
            P(None, None, "frame"),
            P("dp"),
            P("dp"),
            P("dp", None, None),
        ),
        out_specs=(
            P("dp", ("frame", "audio"), None),
            P("dp", ("frame", "audio"), None),
            P(("dp", "audio"), None, "frame"),
        ),
        check_vma=False,
    )
```

time: 300 us -> 142 us (0.47)
  waiting for transfers between devices: 149 us -> 37 us
  blocking collectives: 40.5 us -> 0 us
  Pallas kernels: 0 us -> 33 us
  local copies, waits for them, and re-layouts: 37.7 us -> 10.2 us
  starting transfers between devices: 25.6 us -> 52.9 us
  matrix products: 25.3 us -> 1.39 us
  between operations: 15.5 us -> 2.17 us
    reduce_scatter x1 -> x0, waiting for transfers between devices: 106 us -> none  [summed_rows(): so_far = lax.psum_scatter(so_far, axis, scatter_dimension=0, tiled=True)]
    all_to_all x5 -> x2, waiting for transfers between devices: 42.8 us -> 0.01 us  [to_owners(): return lax.all_to_all(array, axis, split_axis=0, concat_axis=0, tiled=True)]
    all_to_all x1 -> x0, blocking collectives: 40.5 us -> none  [sum_at_owner(): lax.all_to_all(pieces, axis, split_axis=0, concat_axis=0, tiled=True)]
    ppermute x0 -> x26, starting transfers between devices: none -> 39.6 us  [the longest x21 32.9 us: shifted(): lax.ppermute(array, axis, [(i, (i + by) % count) for i in range(count)])]
    ppermute x0 -> x26, waiting for transfers between devices: none -> 37 us  [the longest x21 31.4 us: shifted(): lax.ppermute(array, axis, [(i, (i + by) % count) for i in range(count)])]
    pallas_call x0 -> x7, Pallas kernels: none -> 33 us  [the longest x1 12.7 us: attend(): pl.pallas_call(kernel, out_shape=[jax.ShapeDtypeStruct(arrived.shape, BF1...]
    dot_general x7 -> x0, matrix products: 20.4 us -> none  [the longest x1 5.17 us: attend_listed(): jnp.einsum('sn,skx->nkx', onehot, grad_part, precision=lax.Precision.HIGH...]
    all_to_all x5 -> x2, starting transfers between devices: 25.6 us -> 13.3 us  [to_owners(): return lax.all_to_all(array, axis, split_axis=0, concat_axis=0, tiled=True)]
  transfers between devices with their start and end apart: 7 -> 28, of which waited for: 5 -> 10; matrix products, arithmetic and copies ran while one was open for 10% -> 7% of each run, Pallas kernels for 0% -> 20%
where the time goes in v1:
time: 142 us; the launch traced here: 139 us
  starting transfers between devices  52.9 us (37%)
  waiting for transfers between devices  37 us (26%)
  Pallas kernels  33 us (23%)
  local copies, waits for them, and re-layouts  10.2 us (7%)
  other arithmetic  2.87 us (2%)
  between operations  2.17 us (2%)
    ppermute x21, starting transfers between devices, shifted(): lax.ppermute(array, axis, [(i, (i + by) % count) for i in range(count)])  32.9 us
    ppermute x21, waiting for transfers between devices, shifted(): lax.ppermute(array, axis, [(i, (i + by) % count) for i in range(count)])  31.4 us
    all_to_all x2, starting transfers between devices, to_owners(): return lax.all_to_all(array, axis, split_axis=0, concat_axis=0, tiled=True)  13.3 us
    pallas_call x1, Pallas kernels, attend(): pl.pallas_call(kernel, out_shape=[jax.ShapeDtypeStruct(arrived.shape, BF1...  12.7 us
    pallas_call x2, Pallas kernels, product(): pl.pallas_call(kernel, out_shape=[jax.ShapeDtypeStruct((count, rows, widt...  9.22 us
    unnamed x52, local copies, waits for them, and re-layouts  8.7 us
    ppermute x2, waiting for transfers between devices, per_device(): halves.append((kept, lax.ppermute(sent, 'dp', partner)))  5.58 us
    ppermute x2, starting transfers between devices, per_device(): halves.append((kept, lax.ppermute(sent, 'dp', partner)))  4.97 us
  transfers between devices with their start and end apart: 28, of which 10 were waited for; matrix products, arithmetic and copies ran while one was open for 7% of the time, Pallas kernels for 20%

profile of v1, /device:TPU:1, one launch (start us, length us, event | category | flops | bytes accessed | tf_op | source)
XLA Modules:
  0.0 139.5 jit_solution(9404774599982211095)
XLA Ops:
  0.6 2.7 %pack.1 = bf16[8,2,128,384]{3,2,1,0:T(8,128)(2,1)} custom-call(bf16[128,3072]{1,0:T(8,128)(2,1)} %bitcast.16, bf16[128,3072]{1,0:T(8,128)(2,1)} %bitcast.17), custom_call_target="tpu_custom_call" | custom-call | tf_op jit(solution)/shard_map/pack/pallas_call | solution.py:39
  3.3 6.7 %all-to-all-start = ((bf16[8,2,128,384]{3,2,1,0:T(8,128)(2,1)}), bf16[8,2,128,384]{3,2,1,0:T(8,128)(2,1)S(1)}, u32[]{:S(2)}, u32[]{:S(2)}) async-start(bf16[8,2,128,384]{3,2,1,0:T(8,128)(2,1)} %pack.1), calls=%async_computation | async-start | bytes 3145728 | tf_op jit(solution)/shard_map/all_to_all | solution.py:311
  10.0 3.3 %copy.12 = bf16[384,8,2,384]{3,1,2,0:T(8,128)(2,1)S(1)} copy(bf16[384,8,2,384]{3,2,1,0:T(2,128)(2,1)} %bitcast.13) | data formatting | bytes 9437184
  13.3 1.4 convolution_convert_fusion.refs_5_
  15.2 2.6 %collective-permute-start.1 = (bf16[256,768]{1,0:T(8,128)(2,1)S(1)}, bf16[256,768]{1,0:T(8,128)(2,1)S(1)}, u32[]{:S(2)}, u32[]{:S(2)}) collective-permute-start(bf16[256,768]{1,0:T(8,128)(2,1)S(1)} %convolution_convert_fusion.refs_5_), channel_id=1, source_target_pairs={{0,2},{1,3},{2,0},{3,1},{4,6},{5,7},{6,4},{7,5},{8,10},{9,11},{10,... | collective-permute-start | bytes 1179656 | tf_op jit(solution)/shard_map/ppermute | solution.py:27
  19.5 3.3 %turn.1 = (bf16[2,4,96,256]{3,2,1,0:T(8,128)(2,1)}, bf16[4,96,256]{2,1,0:T(8,128)(2,1)}, bf16[4,96,256]{2,1,0:T(8,128)(2,1)}, bf16[4,96,256]{2,1,0:T(8,128)(2,1)}) custom-call(s32[3]{0:T(128)} %pad_add_fusion.refs_0_.ids, bf16[256,3072]{1,0:T(8,128)(2,1)} %bitcast.15), custom_call_target="tpu_custom_call" | custom-call | tf_op jit(solution)/shard_map/turn/pallas_call | solution.py:90
  26.7 8.8 %collective-permute-done.1.refs_7_ = bf16[256,768]{1,0:T(8,128)(2,1)S(1)} collective-permute-done((bf16[256,768]{1,0:T(8,128)(2,1)S(1)}, bf16[256,768]{1,0:T(8,128)(2,1)S(1)}, u32[]{:S(2)}, u32[]{:S(2)}) %collective-permute-start.1) | collective-permute-done | bytes 393248 | tf_op jit(solution)/shard_map/ppermute | solution.py:27
  37.5 12.7 %attend.1 = (bf16[8,2,128,384]{3,2,1,0:T(8,128)(2,1)}, f32[256,384]{1,0:T(8,128)}, f32[256,384]{1,0:T(8,128)}, bf16[256,384]{1,0:T(8,128)(2,1)}, bf16[256,384]{1...) custom-call(s32[3]{0:T(128)} %pad_add_fusion.refs_0_.ids, ...), custom_call_target="tpu_custom_call" | custom-call | tf_op jit(solution)/shard_map/attend/pallas_call | solution.py:210
  50.2 2.5 %collective-permute-start.15 = (bf16[256,384]{1,0:T(8,128)(2,1)}, bf16[256,384]{1,0:T(8,128)(2,1)S(1)}, u32[]{:S(2)}, u32[]{:S(2)}) collective-permute-start(bf16[256,384]{1,0:T(8,128)(2,1)} %get-tuple-element.39), channel_id=1, source_target_pairs={{0,1},{1,2},{2,3},{3,0},{4,5},{5,6},{6,7},{7,4},{8,9},{9,10},{10,1... | collective-permute-start | bytes 589832 | tf_op jit(solution)/shard_map/ppermute | solution.py:27
  52.7 2.3 %collective-permute-start.16 = (bf16[256,384]{1,0:T(8,128)(2,1)}, bf16[256,384]{1,0:T(8,128)(2,1)S(1)}, u32[]{:S(2)}, u32[]{:S(2)}) collective-permute-start(bf16[256,384]{1,0:T(8,128)(2,1)} %get-tuple-element.40), channel_id=1, source_target_pairs={{0,2},{1,3},{2,0},{3,1},{4,6},{5,7},{6,4},{7,5},{8,10},{9,11},{10,... | collective-permute-start | bytes 589832 | tf_op jit(solution)/shard_map/ppermute | solution.py:27
  55.2 6.6 %all-to-all-start.1 = ((bf16[8,2,128,384]{3,2,1,0:T(8,128)(2,1)}), bf16[8,2,128,384]{3,2,1,0:T(8,128)(2,1)S(1)}, u32[]{:S(2)}, u32[]{:S(2)}) async-start(bf16[8,2,128,384]{3,2,1,0:T(8,128)(2,1)} %get-tuple-element.26), calls=%async_computation.1 | async-start | bytes 3145728 | tf_op jit(solution)/shard_map/all_to_all | solution.py:311
  62.7 2.2 %collective-permute-start.10 = (bf16[256,384]{1,0:T(8,128)(2,1)}, bf16[256,384]{1,0:T(8,128)(2,1)S(1)}, u32[]{:S(2)}, u32[]{:S(2)}) collective-permute-start(bf16[256,384]{1,0:T(8,128)(2,1)} %get-tuple-element.35), channel_id=1, source_target_pairs={{0,2},{1,3},{2,0},{3,1},{4,6},{5,7},{6,4},{7,5},{8,10},{9,11},{10,... | collective-permute-start | bytes 589832 | tf_op jit(solution)/shard_map/ppermute | solution.py:27
  68.6 1.3 collective-permute-start.7
  70.6 4.5 %collective-permute-start.18 = (bf16[256,384]{1,0:T(8,128)(2,1)S(1)}, bf16[256,384]{1,0:T(8,128)(2,1)S(1)}, u32[]{:S(2)}, u32[]{:S(2)}) collective-permute-start(bf16[256,384]{1,0:T(8,128)(2,1)S(1)} %add_convert_fusion.refs_8_), channel_id=1, source_target_pairs={{0,1},{1,2},{2,3},{3,0},{4,5},{5,6},{6,7},{7,4},{8,9},{9,10},{10,1... | collective-permute-start | bytes 589832 | tf_op jit(solution)/shard_map/ppermute | solution.py:27
  75.1 2.0 %collective-permute-done.11 = bf16[256,384]{1,0:T(8,128)(2,1)S(1)} collective-permute-done((bf16[256,384]{1,0:T(8,128)(2,1)}, bf16[256,384]{1,0:T(8,128)(2,1)S(1)}, u32[]{:S(2)}, u32[]{:S(2)}) %collective-permute-start.11) | collective-permute-done | bytes 196640 | tf_op jit(solution)/shard_map/ppermute | solution.py:27
  77.1 1.4 %collective-permute-start.19 = (bf16[256,384]{1,0:T(8,128)(2,1)S(1)}, bf16[256,384]{1,0:T(8,128)(2,1)S(1)}, u32[]{:S(2)}, u32[]{:S(2)}) collective-permute-start(bf16[256,384]{1,0:T(8,128)(2,1)S(1)} %add_convert_fusion.refs_8_), channel_id=1, source_target_pairs={{0,2},{1,3},{2,0},{3,1},{4,6},{5,7},{6,4},{7,5},{8,10},{9,11},{10,... | collective-permute-start | bytes 589832 | tf_op jit(solution)/shard_map/ppermute | solution.py:27
  78.5 1.8 %collective-permute-start.20 = (bf16[256,384]{1,0:T(8,128)(2,1)S(1)}, bf16[256,384]{1,0:T(8,128)(2,1)S(1)}, u32[]{:S(2)}, u32[]{:S(2)}) collective-permute-start(bf16[256,384]{1,0:T(8,128)(2,1)S(1)} %add_convert_fusion.refs_8_), channel_id=1, source_target_pairs={{0,3},{1,0},{2,1},{3,2},{4,7},{5,4},{6,5},{7,6},{8,11},{9,8},{10,9... | collective-permute-start | bytes 589832 | tf_op jit(solution)/shard_map/ppermute | solution.py:27
  80.6 1.3 collective-permute-start.13
  81.9 2.0 %collective-permute-start.14 = (bf16[256,384]{1,0:T(8,128)(2,1)S(1)}, bf16[256,384]{1,0:T(8,128)(2,1)}, u32[]{:S(2)}, u32[]{:S(2)}) collective-permute-start(bf16[256,384]{1,0:T(8,128)(2,1)S(1)} %add_convert_fusion.1.refs_8_), channel_id=1, source_target_pairs={{0,3},{1,0},{2,1},{3,2},{4,7},{5,4},{6,5},{7,6},{8,11},{9,8},{10,9... | collective-permute-start | bytes 589832 | tf_op jit(solution)/shard_map/ppermute | solution.py:27
  83.8 1.6 %collective-permute-done.19.refs_10_ = bf16[256,384]{1,0:T(8,128)(2,1)S(1)} collective-permute-done((bf16[256,384]{1,0:T(8,128)(2,1)S(1)}, bf16[256,384]{1,0:T(8,128)(2,1)S(1)}, u32[]{:S(2)}, u32[]{:S(2)}) %collective-permute-start.19) | collective-permute-done | bytes 196640 | tf_op jit(solution)/shard_map/ppermute | solution.py:27
  85.4 3.4 %collective-permute-done.20.refs_11_ = bf16[256,384]{1,0:T(8,128)(2,1)S(1)} collective-permute-done((bf16[256,384]{1,0:T(8,128)(2,1)S(1)}, bf16[256,384]{1,0:T(8,128)(2,1)S(1)}, u32[]{:S(2)}, u32[]{:S(2)}) %collective-permute-start.20) | collective-permute-done | bytes 196640 | tf_op jit(solution)/shard_map/ppermute | solution.py:27
  89.5 4.6 %product.3 = (f32[4,96,384]{2,1,0:T(8,128)}, bf16[4,96,384]{2,1,0:T(8,128)(2,1)}) custom-call(s32[3]{0:T(128)} %pad_add_fusion.refs_0_.ids, bf16[2,4,96,256]{3,2,1,0:T(8,128)(2,1)} %get-tuple-element.29.refs_1_, bf16[4,96,256]{2,1,0:T(8,128)(2,1)} %copy-done.3, bf16[4,96,256]{2,1,0:T(8,128)(2,1)} %copy-done.4, bf16[4,96,256]{2,1,0:T(8,128)(2,1)} %copy-done.5, ...), custom_call_target="tpu_custom_call" | custom-call | tf_op jit(solution)/shard_map/product/pallas_call | solution.py:263
  95.0 1.9 %collective-permute-done.14.refs_11_ = bf16[256,384]{1,0:T(8,128)(2,1)} collective-permute-done((bf16[256,384]{1,0:T(8,128)(2,1)S(1)}, bf16[256,384]{1,0:T(8,128)(2,1)}, u32[]{:S(2)}, u32[]{:S(2)}) %collective-permute-start.14) | collective-permute-done | bytes 196640 | tf_op jit(solution)/shard_map/ppermute | solution.py:27
  96.9 4.6 %product.2 = (f32[4,96,384]{2,1,0:T(8,128)}, bf16[4,96,384]{2,1,0:T(8,128)(2,1)}) custom-call(s32[3]{0:T(128)} %pad_add_fusion.refs_0_.ids, bf16[2,4,96,256]{3,2,1,0:T(8,128)(2,1)} %get-tuple-element.29.refs_1_, bf16[4,96,256]{2,1,0:T(8,128)(2,1)} %copy-done.3, bf16[4,96,256]{2,1,0:T(8,128)(2,1)} %copy-done.4, bf16[4,96,256]{2,1,0:T(8,128)(2,1)} %copy-done.5, ...), custom_call_target="tpu_custom_call" | custom-call | tf_op jit(solution)/shard_map/product/pallas_call | solution.py:263
  101.5 4.1 %collective-permute-start.21 = (bf16[4,96,384]{2,1,0:T(8,128)(2,1)}, bf16[4,96,384]{2,1,0:T(8,128)(2,1)S(1)}, u32[]{:S(2)}, u32[]{:S(2)}) collective-permute-start(bf16[4,96,384]{2,1,0:T(8,128)(2,1)} %get-tuple-element.43), channel_id=1, source_target_pairs={{0,224},{32,64},{64,32},{96,128},{128,96},{160,192},{192,160},{224... | collective-permute-start | bytes 884744 | tf_op jit(solution)/shard_map/ppermute | solution.py:366
  105.6 5.6 %collective-permute-done.21.key_came = bf16[4,96,384]{2,1,0:T(8,128)(2,1)S(1)} collective-permute-done((bf16[4,96,384]{2,1,0:T(8,128)(2,1)}, bf16[4,96,384]{2,1,0:T(8,128)(2,1)S(1)}, u32[]{:S(2)}, u32[]{:S(2)}) %collective-permute-start.21) | collective-permute-done | bytes 294944 | tf_op jit(solution)/shard_map/ppermute | solution.py:366
  111.9 2.4 %merge.1 = (f32[96,768]{1,0:T(8,128)}, bf16[96,768]{1,0:T(8,128)(2,1)}, bf16[96,768]{1,0:T(8,128)(2,1)}, bf16[96,768]{1,0:T(8,128)(2,1)}) custom-call(s32[3]{0:T(128)} %pad_add_fusion.refs_0_.ids, f32[4,96,384]{2,1,0:T(8,128)} %get-tuple-element.37.key_kept, f32[4,96,384]{2,1,0:T(8,128)} %get-tuple-element.42.value_kept, bf16[4,96,384]{2,1,0:T(8,128)(2,1)} %copy-done.18, ...), custom_call_target="tpu_custom_call" | custom-call | tf_op jit(solution)/shard_map/merge/pallas_call | solution.py:293
  114.3 3.7 %collective-permute-start.24 = (bf16[96,768]{1,0:T(8,128)(2,1)}, bf16[96,768]{1,0:T(8,128)(2,1)S(1)}, u32[]{:S(2)}, u32[]{:S(2)}) collective-permute-start(bf16[96,768]{1,0:T(8,128)(2,1)} %get-tuple-element.47), channel_id=1, source_target_pairs={{0,128},{32,160},{64,192},{96,224},{128,0},{160,32},{192,64},{224,... | collective-permute-start | bytes 442376 | tf_op jit(solution)/shard_map/ppermute | solution.py:27
  118.0 3.5 %collective-permute-start.25 = (bf16[96,768]{1,0:T(8,128)(2,1)}, bf16[96,768]{1,0:T(8,128)(2,1)S(1)}, u32[]{:S(2)}, u32[]{:S(2)}) collective-permute-start(bf16[96,768]{1,0:T(8,128)(2,1)} %get-tuple-element.48), channel_id=1, source_target_pairs={{0,192},{32,224},{64,0},{96,32},{128,64},{160,96},{192,128},{224,1... | collective-permute-start | bytes 442376 | tf_op jit(solution)/shard_map/ppermute | solution.py:27
  121.6 3.9 %collective-permute-done.24 = bf16[96,768]{1,0:T(8,128)(2,1)S(1)} collective-permute-done((bf16[96,768]{1,0:T(8,128)(2,1)}, bf16[96,768]{1,0:T(8,128)(2,1)S(1)}, u32[]{:S(2)}, u32[]{:S(2)}) %collective-permute-start.24) | collective-permute-done | bytes 147488 | tf_op jit(solution)/shard_map/ppermute | solution.py:27
  125.5 8.2 %collective-permute-done.25 = bf16[96,768]{1,0:T(8,128)(2,1)S(1)} collective-permute-done((bf16[96,768]{1,0:T(8,128)(2,1)}, bf16[96,768]{1,0:T(8,128)(2,1)S(1)}, u32[]{:S(2)}, u32[]{:S(2)}) %collective-permute-start.25) | collective-permute-done | bytes 147488 | tf_op jit(solution)/shard_map/ppermute | solution.py:27
  136.8 2.7 %unpack.1 = (bf16[128,3072]{1,0:T(8,128)(2,1)}, bf16[128,3072]{1,0:T(8,128)(2,1)}) custom-call(bf16[8,2,128,384]{3,2,1,0:T(8,128)(2,1)} %copy-done), custom_call_target="tpu_custom_call" | custom-call | tf_op jit(solution)/shard_map/unpack/pallas_call | solution.py:58
  (90 shorter events, 17.8 us)
Async XLA Ops:
  3.3 32.2 %all-to-all-start = ((bf16[8,2,128,384]{3,2,1,0:T(8,128)(2,1)}), bf16[8,2,128,384]{3,2,1,0:T(8,128)(2,1)S(1)}, u32[]{:S(2)}, u32[]{:S(2)}) async-start(bf16[8,2,128,384]{3,2,1,0:T(8,128)(2,1)} %pack.1), calls=%async_computation | async-start | bytes 3145728 | tf_op jit(solution)/shard_map/all_to_all | solution.py:311
  14.7 12.0 %collective-permute-start = (bf16[256,768]{1,0:T(8,128)(2,1)S(1)}, bf16[256,768]{1,0:T(8,128)(2,1)S(1)}, u32[]{:S(2)}, u32[]{:S(2)}) collective-permute-start(bf16[256,768]{1,0:T(8,128)(2,1)S(1)} %convolution_convert_fusion.refs_5_), channel_id=1, source_target_pairs={{0,1},{1,2},{2,3},{3,0},{4,5},{5,6},{6,7},{7,4},{8,9},{9,10},{10,1... | collective-permute-start | bytes 1179656 | tf_op jit(solution)/shard_map/ppermute | solution.py:27
  15.2 20.3 %collective-permute-start.1 = (bf16[256,768]{1,0:T(8,128)(2,1)S(1)}, bf16[256,768]{1,0:T(8,128)(2,1)S(1)}, u32[]{:S(2)}, u32[]{:S(2)}) collective-permute-start(bf16[256,768]{1,0:T(8,128)(2,1)S(1)} %convolution_convert_fusion.refs_5_), channel_id=1, source_target_pairs={{0,2},{1,3},{2,0},{3,1},{4,6},{5,7},{6,4},{7,5},{8,10},{9,11},{10,... | collective-permute-start | bytes 1179656 | tf_op jit(solution)/shard_map/ppermute | solution.py:27
  17.8 17.7 %collective-permute-start.2 = (bf16[256,768]{1,0:T(8,128)(2,1)S(1)}, bf16[256,768]{1,0:T(8,128)(2,1)S(1)}, u32[]{:S(2)}, u32[]{:S(2)}) collective-permute-start(bf16[256,768]{1,0:T(8,128)(2,1)S(1)} %convolution_convert_fusion.refs_5_), channel_id=1, source_target_pairs={{0,3},{1,0},{2,1},{3,2},{4,7},{5,4},{6,5},{7,6},{8,11},{9,8},{10,9... | collective-permute-start | bytes 1179656 | tf_op jit(solution)/shard_map/ppermute | solution.py:27
  22.8 39.1 %collective-permute-start.3 = (bf16[4,96,256]{2,1,0:T(8,128)(2,1)}, bf16[4,96,256]{2,1,0:T(8,128)(2,1)S(1)}, u32[]{:S(2)}, u32[]{:S(2)}) collective-permute-start(bf16[4,96,256]{2,1,0:T(8,128)(2,1)} %get-tuple-element.30), channel_id=1, source_target_pairs={{0,1},{1,2},{2,3},{3,0},{4,5},{5,6},{6,7},{7,4},{8,9},{9,10},{10,1... | collective-permute-start | bytes 589832 | tf_op jit(solution)/shard_map/ppermute | solution.py:27
  23.2 39.3 %collective-permute-start.4 = (bf16[4,96,256]{2,1,0:T(8,128)(2,1)}, bf16[4,96,256]{2,1,0:T(8,128)(2,1)S(1)}, u32[]{:S(2)}, u32[]{:S(2)}) collective-permute-start(bf16[4,96,256]{2,1,0:T(8,128)(2,1)} %get-tuple-element.31), channel_id=1, source_target_pairs={{0,2},{1,3},{2,0},{3,1},{4,6},{5,7},{6,4},{7,5},{8,10},{9,11},{10,... | collective-permute-start | bytes 589832 | tf_op jit(solution)/shard_map/ppermute | solution.py:27
  50.2 12.5 %collective-permute-start.15 = (bf16[256,384]{1,0:T(8,128)(2,1)}, bf16[256,384]{1,0:T(8,128)(2,1)S(1)}, u32[]{:S(2)}, u32[]{:S(2)}) collective-permute-start(bf16[256,384]{1,0:T(8,128)(2,1)} %get-tuple-element.39), channel_id=1, source_target_pairs={{0,1},{1,2},{2,3},{3,0},{4,5},{5,6},{6,7},{7,4},{8,9},{9,10},{10,1... | collective-permute-start | bytes 589832 | tf_op jit(solution)/shard_map/ppermute | solution.py:27
  52.7 12.2 %collective-permute-start.16 = (bf16[256,384]{1,0:T(8,128)(2,1)}, bf16[256,384]{1,0:T(8,128)(2,1)S(1)}, u32[]{:S(2)}, u32[]{:S(2)}) collective-permute-start(bf16[256,384]{1,0:T(8,128)(2,1)} %get-tuple-element.40), channel_id=1, source_target_pairs={{0,2},{1,3},{2,0},{3,1},{4,6},{5,7},{6,4},{7,5},{8,10},{9,11},{10,... | collective-permute-start | bytes 589832 | tf_op jit(solution)/shard_map/ppermute | solution.py:27
  55.0 11.1 %collective-permute-start.17 = (bf16[256,384]{1,0:T(8,128)(2,1)}, bf16[256,384]{1,0:T(8,128)(2,1)}, u32[]{:S(2)}, u32[]{:S(2)}) collective-permute-start(bf16[256,384]{1,0:T(8,128)(2,1)} %get-tuple-element.41), channel_id=1, source_target_pairs={{0,3},{1,0},{2,1},{3,2},{4,7},{5,4},{6,5},{7,6},{8,11},{9,8},{10,9... | collective-permute-start | bytes 589832 | tf_op jit(solution)/shard_map/ppermute | solution.py:27
  55.2 25.1 %copy-start.11 = (f32[256,384]{1,0:T(8,128)S(1)}, f32[256,384]{1,0:T(8,128)}, u32[]{:S(2)}) copy-start(f32[256,384]{1,0:T(8,128)} %get-tuple-element.33) | copy-start | bytes 1179652
  55.2 80.4 %all-to-all-start.1 = ((bf16[8,2,128,384]{3,2,1,0:T(8,128)(2,1)}), bf16[8,2,128,384]{3,2,1,0:T(8,128)(2,1)S(1)}, u32[]{:S(2)}, u32[]{:S(2)}) async-start(bf16[8,2,128,384]{3,2,1,0:T(8,128)(2,1)} %get-tuple-element.26), calls=%async_computation.1 | async-start | bytes 3145728 | tf_op jit(solution)/shard_map/all_to_all | solution.py:311
  61.9 27.6 %copy-start.3 = (bf16[4,96,256]{2,1,0:T(8,128)(2,1)}, bf16[4,96,256]{2,1,0:T(8,128)(2,1)S(1)}, u32[]{:S(2)}) copy-start(bf16[4,96,256]{2,1,0:T(8,128)(2,1)S(1)} %collective-permute-done.3.refs_2_) | copy-start | bytes 589828
  61.9 6.7 %collective-permute-start.5 = (bf16[4,96,256]{2,1,0:T(8,128)(2,1)}, bf16[4,96,256]{2,1,0:T(8,128)(2,1)S(1)}, u32[]{:S(2)}, u32[]{:S(2)}) collective-permute-start(bf16[4,96,256]{2,1,0:T(8,128)(2,1)} %get-tuple-element.32), channel_id=1, source_target_pairs={{0,3},{1,0},{2,1},{3,2},{4,7},{5,4},{6,5},{7,6},{8,11},{9,8},{10,9... | collective-permute-start | bytes 589832 | tf_op jit(solution)/shard_map/ppermute | solution.py:27
  62.4 27.0 %copy-start.4 = (bf16[4,96,256]{2,1,0:T(8,128)(2,1)}, bf16[4,96,256]{2,1,0:T(8,128)(2,1)S(1)}, u32[]{:S(2)}) copy-start(bf16[4,96,256]{2,1,0:T(8,128)(2,1)S(1)} %collective-permute-done.4.refs_3_) | copy-start | bytes 589828
  62.4 7.5 %collective-permute-start.6 = (bf16[4,96,256]{2,1,0:T(8,128)(2,1)S(1)}, bf16[4,96,256]{2,1,0:T(8,128)(2,1)S(1)}, u32[]{:S(2)}, u32[]{:S(2)}) collective-permute-start(bf16[4,96,256]{2,1,0:T(8,128)(2,1)S(1)} %collective-permute-done.3.refs_2_), channel_id=1, source_target_pairs={{0,4},{4,0},{8,12},{12,8},{16,20},{20,16},{24,28},{28,24},{1,5},{5... | collective-permute-start | bytes 589832 | tf_op jit(solution)/shard_map/ppermute | solution.py:359
  62.7 7.9 %collective-permute-start.10 = (bf16[256,384]{1,0:T(8,128)(2,1)}, bf16[256,384]{1,0:T(8,128)(2,1)S(1)}, u32[]{:S(2)}, u32[]{:S(2)}) collective-permute-start(bf16[256,384]{1,0:T(8,128)(2,1)} %get-tuple-element.35), channel_id=1, source_target_pairs={{0,2},{1,3},{2,0},{3,1},{4,6},{5,7},{6,4},{7,5},{8,10},{9,11},{10,... | collective-permute-start | bytes 589832 | tf_op jit(solution)/shard_map/ppermute | solution.py:27
  64.9 12.1 %collective-permute-start.11 = (bf16[256,384]{1,0:T(8,128)(2,1)}, bf16[256,384]{1,0:T(8,128)(2,1)S(1)}, u32[]{:S(2)}, u32[]{:S(2)}) collective-permute-start(bf16[256,384]{1,0:T(8,128)(2,1)} %get-tuple-element.36), channel_id=1, source_target_pairs={{0,3},{1,0},{2,1},{3,2},{4,7},{5,4},{6,5},{7,6},{8,11},{9,8},{10,9... | collective-permute-start | bytes 589832 | tf_op jit(solution)/shard_map/ppermute | solution.py:27
  66.1 12.4 %collective-permute-start.9 = (bf16[256,384]{1,0:T(8,128)(2,1)}, bf16[256,384]{1,0:T(8,128)(2,1)S(1)}, u32[]{:S(2)}, u32[]{:S(2)}) collective-permute-start(bf16[256,384]{1,0:T(8,128)(2,1)} %get-tuple-element.34), channel_id=1, source_target_pairs={{0,1},{1,2},{2,3},{3,0},{4,5},{5,6},{6,7},{7,4},{8,9},{9,10},{10,1... | collective-permute-start | bytes 589832 | tf_op jit(solution)/shard_map/ppermute | solution.py:27
  67.5 21.9 %copy-start.9 = (bf16[256,384]{1,0:T(8,128)(2,1)}, bf16[256,384]{1,0:T(8,128)(2,1)S(1)}, u32[]{:S(2)}) copy-start(bf16[256,384]{1,0:T(8,128)(2,1)S(1)} %add_convert_fusion.refs_8_) | copy-start | bytes 589828
  68.6 11.8 %collective-permute-start.7 = (bf16[4,96,256]{2,1,0:T(8,128)(2,1)S(1)}, bf16[4,96,256]{2,1,0:T(8,128)(2,1)S(1)}, u32[]{:S(2)}, u32[]{:S(2)}) collective-permute-start(bf16[4,96,256]{2,1,0:T(8,128)(2,1)S(1)} %collective-permute-done.4.refs_3_), channel_id=1, source_target_pairs={{0,4},{4,0},{8,12},{12,8},{16,20},{20,16},{24,28},{28,24},{1,5},{5... | collective-permute-start | bytes 589832 | tf_op jit(solution)/shard_map/ppermute | solution.py:359
  70.0 10.6 %collective-permute-start.8 = (bf16[4,96,256]{2,1,0:T(8,128)(2,1)S(1)}, bf16[4,96,256]{2,1,0:T(8,128)(2,1)S(1)}, u32[]{:S(2)}, u32[]{:S(2)}) collective-permute-start(bf16[4,96,256]{2,1,0:T(8,128)(2,1)S(1)} %collective-permute-done.5.refs_4_), channel_id=1, source_target_pairs={{0,4},{4,0},{8,12},{12,8},{16,20},{20,16},{24,28},{28,24},{1,5},{5... | collective-permute-start | bytes 589832 | tf_op jit(solution)/shard_map/ppermute | solution.py:359
  70.6 11.2 %collective-permute-start.18 = (bf16[256,384]{1,0:T(8,128)(2,1)S(1)}, bf16[256,384]{1,0:T(8,128)(2,1)S(1)}, u32[]{:S(2)}, u32[]{:S(2)}) collective-permute-start(bf16[256,384]{1,0:T(8,128)(2,1)S(1)} %add_convert_fusion.refs_8_), channel_id=1, source_target_pairs={{0,1},{1,2},{2,3},{3,0},{4,5},{5,6},{6,7},{7,4},{8,9},{9,10},{10,1... | collective-permute-start | bytes 589832 | tf_op jit(solution)/shard_map/ppermute | solution.py:27
  77.1 8.3 %collective-permute-start.19 = (bf16[256,384]{1,0:T(8,128)(2,1)S(1)}, bf16[256,384]{1,0:T(8,128)(2,1)S(1)}, u32[]{:S(2)}, u32[]{:S(2)}) collective-permute-start(bf16[256,384]{1,0:T(8,128)(2,1)S(1)} %add_convert_fusion.refs_8_), channel_id=1, source_target_pairs={{0,2},{1,3},{2,0},{3,1},{4,6},{5,7},{6,4},{7,5},{8,10},{9,11},{10,... | collective-permute-start | bytes 589832 | tf_op jit(solution)/shard_map/ppermute | solution.py:27
  78.5 10.2 %collective-permute-start.20 = (bf16[256,384]{1,0:T(8,128)(2,1)S(1)}, bf16[256,384]{1,0:T(8,128)(2,1)S(1)}, u32[]{:S(2)}, u32[]{:S(2)}) collective-permute-start(bf16[256,384]{1,0:T(8,128)(2,1)S(1)} %add_convert_fusion.refs_8_), channel_id=1, source_target_pairs={{0,3},{1,0},{2,1},{3,2},{4,7},{5,4},{6,5},{7,6},{8,11},{9,8},{10,9... | collective-permute-start | bytes 589832 | tf_op jit(solution)/shard_map/ppermute | solution.py:27
  80.5 14.5 %collective-permute-start.12 = (bf16[256,384]{1,0:T(8,128)(2,1)S(1)}, bf16[256,384]{1,0:T(8,128)(2,1)S(1)}, u32[]{:S(2)}, u32[]{:S(2)}) collective-permute-start(bf16[256,384]{1,0:T(8,128)(2,1)S(1)} %add_convert_fusion.1.refs_8_), channel_id=1, source_target_pairs={{0,1},{1,2},{2,3},{3,0},{4,5},{5,6},{6,7},{7,4},{8,9},{9,10},{10,1... | collective-permute-start | bytes 589832 | tf_op jit(solution)/shard_map/ppermute | solution.py:27
  80.6 14.4 %collective-permute-start.13 = (bf16[256,384]{1,0:T(8,128)(2,1)S(1)}, bf16[256,384]{1,0:T(8,128)(2,1)S(1)}, u32[]{:S(2)}, u32[]{:S(2)}) collective-permute-start(bf16[256,384]{1,0:T(8,128)(2,1)S(1)} %add_convert_fusion.1.refs_8_), channel_id=1, source_target_pairs={{0,2},{1,3},{2,0},{3,1},{4,6},{5,7},{6,4},{7,5},{8,10},{9,11},{10,... | collective-permute-start | bytes 589832 | tf_op jit(solution)/shard_map/ppermute | solution.py:27
  81.9 15.0 %collective-permute-start.14 = (bf16[256,384]{1,0:T(8,128)(2,1)S(1)}, bf16[256,384]{1,0:T(8,128)(2,1)}, u32[]{:S(2)}, u32[]{:S(2)}) collective-permute-start(bf16[256,384]{1,0:T(8,128)(2,1)S(1)} %add_convert_fusion.1.refs_8_), channel_id=1, source_target_pairs={{0,3},{1,0},{2,1},{3,2},{4,7},{5,4},{6,5},{7,6},{8,11},{9,8},{10,9... | collective-permute-start | bytes 589832 | tf_op jit(solution)/shard_map/ppermute | solution.py:27
  94.1 11.5 %collective-permute-start.22 = (bf16[4,96,384]{2,1,0:T(8,128)(2,1)}, bf16[4,96,384]{2,1,0:T(8,128)(2,1)S(1)}, u32[]{:S(2)}, u32[]{:S(2)}) collective-permute-start(bf16[4,96,384]{2,1,0:T(8,128)(2,1)} %get-tuple-element.44), channel_id=1, source_target_pairs={{0,32},{32,0},{64,96},{96,64},{128,160},{160,128},{192,224},{224,1... | collective-permute-start | bytes 884744 | tf_op jit(solution)/shard_map/ppermute | solution.py:366
  101.5 9.7 %collective-permute-start.21 = (bf16[4,96,384]{2,1,0:T(8,128)(2,1)}, bf16[4,96,384]{2,1,0:T(8,128)(2,1)S(1)}, u32[]{:S(2)}, u32[]{:S(2)}) collective-permute-start(bf16[4,96,384]{2,1,0:T(8,128)(2,1)} %get-tuple-element.43), channel_id=1, source_target_pairs={{0,224},{32,64},{64,32},{96,128},{128,96},{160,192},{192,160},{224... | collective-permute-start | bytes 884744 | tf_op jit(solution)/shard_map/ppermute | solution.py:366
  114.3 7.3 %collective-permute-start.23 = (bf16[96,768]{1,0:T(8,128)(2,1)}, bf16[96,768]{1,0:T(8,128)(2,1)S(1)}, u32[]{:S(2)}, u32[]{:S(2)}) collective-permute-start(bf16[96,768]{1,0:T(8,128)(2,1)} %get-tuple-element.46), channel_id=1, source_target_pairs={{0,64},{32,96},{64,128},{96,160},{128,192},{160,224},{192,0},{224,... | collective-permute-start | bytes 442376 | tf_op jit(solution)/shard_map/ppermute | solution.py:27
  114.3 11.2 %collective-permute-start.24 = (bf16[96,768]{1,0:T(8,128)(2,1)}, bf16[96,768]{1,0:T(8,128)(2,1)S(1)}, u32[]{:S(2)}, u32[]{:S(2)}) collective-permute-start(bf16[96,768]{1,0:T(8,128)(2,1)} %get-tuple-element.47), channel_id=1, source_target_pairs={{0,128},{32,160},{64,192},{96,224},{128,0},{160,32},{192,64},{224,... | collective-permute-start | bytes 442376 | tf_op jit(solution)/shard_map/ppermute | solution.py:27
  118.0 15.7 %collective-permute-start.25 = (bf16[96,768]{1,0:T(8,128)(2,1)}, bf16[96,768]{1,0:T(8,128)(2,1)S(1)}, u32[]{:S(2)}, u32[]{:S(2)}) collective-permute-start(bf16[96,768]{1,0:T(8,128)(2,1)} %get-tuple-element.48), channel_id=1, source_target_pairs={{0,192},{32,224},{64,0},{96,32},{128,64},{160,96},{192,128},{224,1... | collective-permute-start | bytes 442376 | tf_op jit(solution)/shard_map/ppermute | solution.py:27
  (21 other events, 145.4 us)

commit v2 on v1

v2 whole, which is shorter than its diff:
```python
import jax
import jax.numpy as jnp
from jax import lax
from jax.experimental import pallas as pl
from jax.experimental.pallas import tpu as pltpu
from jax.sharding import PartitionSpec as P


D = 3072
HD = 128
QB = 128
KB = 64
NLIST = 2
SCALING = HD ** (-0.5)
LOG2_E = 1.4426950408889634
BF16 = jnp.bfloat16
F32 = jnp.float32


VMEM = pl.BlockSpec(memory_space=pltpu.VMEM)
SMEM = pl.BlockSpec(memory_space=pltpu.SMEM)
ANY = pl.BlockSpec(memory_space=pl.ANY)


def shifted(array, axis, by):
    count = lax.axis_size(axis)
    return lax.ppermute(array, axis, [(i, (i + by) % count) for i in range(count)])


def pack_kernel(query, grad, out):
    width = out.shape[3]
    for j in range(out.shape[0]):
        out[j, 0] = query[:, j * width : (j + 1) * width]
        out[j, 1] = grad[:, j * width : (j + 1) * width]


def pack(query, grad, frames):
    rows, width = query.shape
    return pl.pallas_call(
        pack_kernel,
        out_shape=jax.ShapeDtypeStruct((frames, 2, rows, width // frames), query.dtype),
        in_specs=[VMEM, VMEM],
        out_specs=VMEM,
        name="pack",
    )(query, grad)


def unpack_kernel(pieces, attended, query_grad):
    width = pieces.shape[3]
    for j in range(pieces.shape[0]):
        attended[:, j * width : (j + 1) * width] = pieces[j, 0]
        query_grad[:, j * width : (j + 1) * width] = pieces[j, 1]


def unpack(pieces):
    frames, _, rows, width = pieces.shape
    whole = jax.ShapeDtypeStruct((rows, width * frames), pieces.dtype)
    return pl.pallas_call(
        unpack_kernel,
        out_shape=[whole, whole],
        in_specs=[VMEM],
        out_specs=[VMEM, VMEM],
        name="unpack",
    )(pieces)


def turn_kernel(audio_count, ids, latents, own, near, far, turned):
    rows = turned.shape[0] // audio_count
    count = own.shape[0] // rows
    width = rows * audio_count
    core = ids[2]

    def part(ahead):
        at = lax.rem(ids[0] + ahead, audio_count) * rows
        return turned[pl.ds(pl.multiple_of(at, 16), rows), :]

    for j in range(count):
        turned[...] = latents[:, j * width : (j + 1) * width].T
        own[j * rows : (j + 1) * rows] = part(0)
        near[j * rows : (j + 1) * rows] = part(1 + core * (audio_count - 2))
        half, place = divmod(j, count // 2)

        @pl.when(core == half)
        def _():
            far[place * rows : (place + 1) * rows] = part(2)


def turn(ids, latents, clips, audio_count):
    count, width = latents.shape
    share = width // audio_count

    def kernel(*refs):
        turn_kernel(audio_count, *refs)

    return pl.pallas_call(
        kernel,
        out_shape=[
            jax.ShapeDtypeStruct((share, count), latents.dtype),
            jax.ShapeDtypeStruct((share, count), latents.dtype),
            jax.ShapeDtypeStruct((share // 2, count), latents.dtype),
        ],
        in_specs=[SMEM, VMEM],
        out_specs=[VMEM] * 3,
        scratch_shapes=[pltpu.VMEM((width // clips, count), latents.dtype)],
        name="turn",
    )(ids, latents)


def dot(left, right, left_dim, right_dim):
    return lax.dot_general(
        left, right, (((left_dim,), (right_dim,)), ((), ())), preferred_element_type=F32
    )


def attend_kernel(audio_count, heads, ids, rows_in, *refs):
    refs = list(refs)
    take = lambda n: [refs.pop(0) for _ in range(n)]
    tables, (rows_out,), grads = take(5), take(1), take(audio_count)
    (table,), sums, (table_sem,) = take(1), take(2 * heads), take(1)
    share = tables[0].shape[0]
    here = ids[0]
    step = pl.program_id(0)
    count = rows_in.shape[0]

    @pl.when(step == 0)
    def _():
        copies = []
        places = ((0, 0), (audio_count - 1, 0), (1, 0), (2, 0), (2, share // 2))
        for i, (ahead, extra) in enumerate(places):
            at = lax.rem(here + ahead, audio_count) * share + extra
            at = pl.ds(pl.multiple_of(at, share // 2), tables[i].shape[0])
            copies.append(pltpu.make_async_copy(tables[i], table.at[at, :], table_sem.at[i]))
        for copy in copies:
            copy.start()
        for part in sums:
            part[...] = jnp.zeros_like(part)
        for copy in copies:
            copy.wait()

    key_row = lax.broadcasted_iota(jnp.int32, (NLIST * KB, 1), 0)
    query_lane = lax.broadcasted_iota(jnp.int32, (1, QB), 1)

    def one(k):
        index = (step * count + k) * audio_count + here
        first = pl.multiple_of(ids[5 + NLIST * index] * KB, KB)
        second = pl.multiple_of(ids[6 + NLIST * index] * KB, KB)
        key_index = jnp.where(key_row < KB, first + key_row, second + key_row - KB)
        allowed = key_index < ids[4]
        live = query_lane + index * QB < ids[3]
        parts = []
        for h in range(heads):
            cols = slice(h * HD, (h + 1) * HD)
            vcols = slice((heads + h) * HD, (heads + h + 1) * HD)
            query = rows_in[k, 0, :, cols]
            grad = rows_in[k, 1, :, cols]
            key = jnp.concatenate(
                [table[pl.ds(first, KB), cols], table[pl.ds(second, KB), cols]], axis=0
            )
            value = jnp.concatenate(
                [table[pl.ds(first, KB), vcols], table[pl.ds(second, KB), vcols]], axis=0
            )
            scores = dot(key, query, 1, 1)
            prob_grad = dot(value, grad, 1, 1)
            scores = jnp.where(allowed, scores, -1e30)
            scores = scores - jnp.max(scores, axis=0, keepdims=True)
            weights = jnp.exp2(scores * (SCALING * LOG2_E))
            inverse = 1.0 / jnp.sum(weights, axis=0, keepdims=True)
            probability = weights * jnp.where(live, inverse, 0.0)
            prob_low = probability.astype(BF16)
            row_dot = jnp.sum(probability * prob_grad, axis=0, keepdims=True)
            score_grad = (probability * (prob_grad - row_dot)).astype(BF16)
            output = dot(prob_low, value, 0, 0).astype(BF16)
            query_part = (dot(score_grad, key, 0, 0) * SCALING).astype(BF16)
            key_part = dot(score_grad, query, 1, 0) * SCALING
            value_part = dot(prob_low, grad, 1, 0)
            parts.append((output, query_part, key_part, value_part))
        return first, second, parts

    def finish(k, first, second, parts):
        for h, (output, query_part, key_part, value_part) in enumerate(parts):
            cols = slice(h * HD, (h + 1) * HD)
            rows_out[k, 0, :, cols] = output
            rows_out[k, 1, :, cols] = query_part
            for into, part in ((sums[h], key_part), (sums[heads + h], value_part)):
                into[pl.ds(first, KB), :] += part[:KB]
                into[pl.ds(second, KB), :] += part[KB:]

    made = [(k, *one(k)) for k in range(count)]
    for entry in made:
        finish(*entry)

    @pl.when(step == pl.num_programs(0) - 1)
    def _():
        for k in range(audio_count):
            at = pl.multiple_of(lax.rem(here + k, audio_count) * share, share)
            for c, total in enumerate(sums):
                half, h = divmod(c, heads)
                place = half + (1 - 2 * half) * (1 - lax.rem(ids[1], 2))
                cols = pl.ds(pl.multiple_of((place * heads + h) * HD, HD), HD)
                grads[k][:, cols] = total[pl.ds(at, share), :].astype(grads[k].dtype)


def attend(ids, arrived, tables, audio_count):
    share, width = tables[0].shape
    heads = width // (2 * HD)
    total = share * audio_count
    count = 2
    rows = pl.BlockSpec((count, *arrived.shape[1:]), lambda i: (i, 0, 0, 0))
    part = pl.BlockSpec((share, width), lambda i: (0, 0))

    def kernel(*refs):
        attend_kernel(audio_count, heads, *refs)

    results, *grads = pl.pallas_call(
        kernel,
        grid=(arrived.shape[0] // count,),
        out_shape=[jax.ShapeDtypeStruct(arrived.shape, BF16)]
        + [jax.ShapeDtypeStruct((share, width), F32)]
        + [jax.ShapeDtypeStruct((share, width), BF16)] * (audio_count - 1),
        in_specs=[SMEM, rows] + [ANY] * len(tables),
        out_specs=[rows] + [part] * audio_count,
        scratch_shapes=[pltpu.VMEM((total, width), BF16)]
        + [pltpu.VMEM((total, HD), F32)] * (2 * heads)
        + [pltpu.SemaphoreType.DMA((len(tables),))],
        compiler_params=pltpu.CompilerParams(dimension_semantics=("arbitrary",)),
        name="attend",
    )(ids, arrived, *tables)
    return results, grads


def assemble_kernel(ids, near, far, near_swapped, far_swapped, out):
    half, depth = far.shape
    core = ids[2]
    middle = slice(depth, 2 * depth)
    out[pl.ds(pl.multiple_of(core * half, 16), half), middle] = far[...]
    out[pl.ds(pl.multiple_of((1 - core) * half, 16), half), middle] = far_swapped[...]

    @pl.when(core == 0)
    def _():
        out[:, :depth] = near[...]
        out[:, 2 * depth :] = near_swapped[...]

    @pl.when(core == 1)
    def _():
        out[:, :depth] = near_swapped[...]
        out[:, 2 * depth :] = near[...]


def assemble(ids, near, *parts):
    rows, depth = near.shape
    return pl.pallas_call(
        assemble_kernel,
        out_shape=jax.ShapeDtypeStruct((rows, depth * 3), near.dtype),
        in_specs=[SMEM] + [VMEM] * 4,
        out_specs=VMEM,
        name="assemble",
    )(ids, near, *parts)


def first_product_kernel(held, rest, paired_held, came, *refs):
    grads, (out, table) = refs[:-2], refs[-2:]
    depth = came.shape[0]
    for k, grad in enumerate(grads[1:]):
        table[k * depth : (k + 1) * depth, :] = grad[...]
    total = dot(held[...], grads[0][...], 1, 0) + dot(paired_held[...], came[...], 1, 0)
    out[...] = total + dot(rest[...], table[...], 1, 0)


def first_product(held, rest, paired_held, came, grads):
    shape = (held.shape[0], came.shape[1])
    return pl.pallas_call(
        first_product_kernel,
        out_shape=jax.ShapeDtypeStruct(shape, F32),
        in_specs=[VMEM] * (4 + len(grads)),
        out_specs=VMEM,
        scratch_shapes=[pltpu.VMEM((rest.shape[1], shape[1]), BF16)],
        name="first_product",
    )(held, rest, paired_held, came, *grads)


def second_product_kernel(scale, hops, ids, so_far, rest, *refs):
    grads, outs, (whole, table) = refs[:hops], refs[hops:-2], refs[-2:]
    depth = grads[0].shape[0]
    for k, grad in enumerate(grads):
        table[k * depth : (k + 1) * depth, :] = grad[...]
    whole[...] = (so_far[...] + dot(rest[...], table[...], 1, 0)) * scale
    count, rows = len(outs), outs[0].shape[0]
    for k in range(count):
        at = pl.multiple_of(lax.rem(ids[1] + k, count) * rows, 16)
        outs[k][...] = whole[pl.ds(at, rows), :].astype(outs[k].dtype)


def second_product(ids, so_far, rest, grads, count, scale):
    rows, width = so_far.shape

    def kernel(*refs):
        second_product_kernel(scale, len(grads), *refs)

    shape = (rows // count, width)
    return pl.pallas_call(
        kernel,
        out_shape=[jax.ShapeDtypeStruct(shape, F32)]
        + [jax.ShapeDtypeStruct(shape, BF16)] * (count - 1),
        in_specs=[SMEM] + [VMEM] * (2 + len(grads)),
        out_specs=[VMEM] * count,
        scratch_shapes=[
            pltpu.VMEM((rows, width), F32),
            pltpu.VMEM((rest.shape[1], width), BF16),
        ],
        name="second_product",
    )(ids, so_far, rest, *grads)


def total_of(pieces):
    total = pieces[0].astype(F32)
    for piece in pieces[1:]:
        total = total + piece.astype(F32)
    return total


def to_owners(array, axis):
    return lax.all_to_all(array, axis, split_axis=0, concat_axis=0, tiled=True)


def per_device(
    video_query, out_grad, audio_latents, kv_weight, video_length, audio_length, align_list
):
    frames = lax.axis_size("frame")
    audio_count = lax.axis_size("audio")
    clips = lax.axis_size("dp")
    local_width = kv_weight.shape[2]
    latents = audio_latents[0]
    ids = jnp.stack(
        [
            lax.axis_index("audio"),
            lax.axis_index("dp"),
            lax.rem(lax.axis_index("frame"), 2),
            video_length[0],
            audio_length[0],
        ]
    )
    ids = jnp.concatenate([ids, align_list.reshape(-1)]).astype(jnp.int32)
    hops = range(1, audio_count)
    cores = range(frames)
    beside = [(f, f ^ 1) for f in cores]
    around = [
        (f * audio_count + a, f * audio_count + (a + 1 - 2 * (f % 2)) % audio_count)
        for f in cores
        for a in range(audio_count)
    ]
    paired = [
        (c * frames + f, (((c + f % 2) ^ 1) - f % 2) % clips * frames + f)
        for c in range(clips)
        for f in cores
    ]

    packed = pack(video_query[0], out_grad[0], frames)
    arrived = to_owners(packed, "frame")
    projected = jnp.dot(
        latents, kv_weight.reshape(D, 2 * local_width), preferred_element_type=F32
    ).astype(BF16)
    half_rows = projected.shape[0] // 2
    left = shifted(projected, "audio", 1)
    right = shifted(projected, "audio", -1)
    low = shifted(left[:half_rows], "audio", 1)
    high = shifted(right[half_rows:], "audio", -1)
    tables = [projected, left, right, low, high]
    held, near, far = turn(ids, latents, clips, audio_count)
    near = lax.ppermute(near, ("frame", "audio"), around)
    far = shifted(far, "audio", 2)
    paired_held = lax.ppermute(held, ("dp", "frame"), paired)

    results, grads = attend(ids, arrived, tables, audio_count)
    added = [grads[0]]
    for k in hops:
        added.append(shifted(grads[k], "audio", k))
    results = to_owners(results, "frame")
    near_swapped = lax.ppermute(near, "frame", beside)
    far_swapped = lax.ppermute(far, "frame", beside)
    rest = assemble(ids, near, far, near_swapped, far_swapped)
    paired_rest = lax.ppermute(rest, ("dp", "frame"), paired)
    total = total_of(added).astype(BF16)
    mine, theirs = total[:, :local_width], total[:, local_width:]
    came = lax.ppermute(theirs, ("dp", "frame"), paired)
    shares, paired_shares = [mine], [came]
    for k in hops:
        shares.append(shifted(mine, "audio", k))
    for k in hops:
        paired_shares.append(shifted(came, "audio", k))
    so_far = first_product(held, rest, paired_held, came, shares)
    pieces = second_product(
        ids, so_far, paired_rest, paired_shares[1:], clips, 1.0 / clips
    )
    parts = [pieces[0]]
    for k in range(1, clips):
        parts.append(shifted(pieces[k], "dp", k))
    same, other = total_of(parts[::2]), total_of(parts[1::2])
    even = ids[1] % 2 == 0
    weight_grad = jnp.stack(
        [jnp.where(even, other, same), jnp.where(even, same, other)], axis=1
    )
    attended, query_grad = unpack(results)
    return attended[None], query_grad[None], weight_grad


def solution(mesh):
    return jax.shard_map(
        per_device,
        mesh=mesh,
        in_specs=(
            P("dp", ("frame", "audio"), None),
            P("dp", ("frame", "audio"), None),
            P("dp", "audio", None),
            P(None, None, "frame"),
            P("dp"),
            P("dp"),
            P("dp", None, None),
        ),
        out_specs=(
            P("dp", ("frame", "audio"), None),
            P("dp", ("frame", "audio"), None),
            P(("dp", "audio"), None, "frame"),
        ),
        check_vma=False,
    )
```

time: 142 us -> 137 us (0.965)
  the two profiles are of different devices: /device:TPU:1 before, /device:TPU:26 now
where the time goes in v2:
time: 137 us
  starting transfers between devices  55.7 us (41%)
  waiting for transfers between devices  35.8 us (26%)
  Pallas kernels  30.4 us (22%)
  local copies, waits for them, and re-layouts  8.81 us (6%)
  other arithmetic  2.41 us (2%)
  between operations  2.14 us (2%)
  matrix products  1.39 us (1%)
    ppermute x21, starting transfers between devices, shifted(): lax.ppermute(array, axis, [(i, (i + by) % count) for i in range(count)])  38.7 us
    ppermute x21, waiting for transfers between devices, shifted(): lax.ppermute(array, axis, [(i, (i + by) % count) for i in range(count)])  32.2 us
    pallas_call x1, Pallas kernels, attend(): pl.pallas_call(kernel, grid=(arrived.shape[0] // count,), out_shape=[jax....  12 us
    all_to_all x2, starting transfers between devices, to_owners(): return lax.all_to_all(array, axis, split_axis=0, concat_axis=0, tiled=True)  11.8 us
    unnamed x37, local copies, waits for them, and re-layouts  8.06 us
    pallas_call x1, Pallas kernels, first_product(): pl.pallas_call(first_product_kernel, out_shape=jax.ShapeDtypeStruct(shape...  3.99 us
    pallas_call x1, Pallas kernels, second_product(): pl.pallas_call(kernel, out_shape=[jax.ShapeDtypeStruct(shape, F32)] + [ja...  3.41 us
    pallas_call x1, Pallas kernels, turn(): pl.pallas_call(kernel, out_shape=[jax.ShapeDtypeStruct((share, count), la...  3.32 us
  transfers between devices with their start and end apart: 29, of which 12 were waited for; matrix products, arithmetic and copies ran while one was open for 6% of the time, Pallas kernels for 18%

profile of v2, /device:TPU:26, one launch (start us, length us, event | category | flops | bytes accessed | tf_op | source)
XLA Modules:
  0.0 136.7 jit_solution(11817770493015666331)
XLA Ops:
  0.6 2.7 %pack.1 = bf16[8,2,128,384]{3,2,1,0:T(8,128)(2,1)} custom-call(bf16[128,3072]{1,0:T(8,128)(2,1)} %bitcast.20, bf16[128,3072]{1,0:T(8,128)(2,1)} %bitcast.21), custom_call_target="tpu_custom_call" | custom-call | tf_op jit(solution)/shard_map/pack/pallas_call | solution.py:39
  3.3 5.0 %all-to-all-start = ((bf16[8,2,128,384]{3,2,1,0:T(8,128)(2,1)}), bf16[8,2,128,384]{3,2,1,0:T(8,128)(2,1)S(1)}, u32[]{:S(2)}, u32[]{:S(2)}) async-start(bf16[8,2,128,384]{3,2,1,0:T(8,128)(2,1)} %pack.1), calls=%async_computation | async-start | bytes 3145728 | tf_op jit(solution)/shard_map/all_to_all | solution.py:322
  10.3 3.3 %turn.1 = (bf16[768,256]{1,0:T(8,128)(2,1)}, bf16[768,256]{1,0:T(8,128)(2,1)}, bf16[384,256]{1,0:T(8,128)(2,1)}) custom-call(s32[69]{0:T(128)} %concatenate.3.refs_0_.ids, bf16[256,3072]{1,0:T(8,128)(2,1)} %bitcast.19), custom_call_target="tpu_custom_call" | custom-call | tf_op jit(solution)/shard_map/turn/pallas_call | solution.py:95
  14.8 3.3 %copy.14 = bf16[384,8,2,384]{3,1,2,0:T(8,128)(2,1)S(1)} copy(bf16[384,8,2,384]{3,2,1,0:T(2,128)(2,1)} %bitcast.17) | data formatting | bytes 9437184
  18.0 1.4 %convolution_convert_fusion.refs_2_ = bf16[256,768]{1,0:T(8,128)(2,1)S(1)} fusion(bf16[3072,768]{1,0:T(8,128)(2,1)S(1)} %bitcast.18, bf16[1,256,3072]{2,1,0:T(8,128)(2,1)S(1)} %copy-done.2), kind=kOutput, calls=%fused_computation | convolution fusion | flops 1208156160 | bytes 6684672 | tf_op jit(solution)/shard_map/dot_general | solution.py:359
  21.6 1.7 %collective-permute-start.5 = (bf16[384,256]{1,0:T(8,128)(2,1)S(1)}, bf16[384,256]{1,0:T(8,128)(2,1)}, u32[]{:S(2)}, u32[]{:S(2)}) collective-permute-start(bf16[384,256]{1,0:T(8,128)(2,1)S(1)} %copy-done.16), channel_id=1, source_target_pairs={{0,2},{1,3},{2,0},{3,1},{4,6},{5,7},{6,4},{7,5},{8,10},{9,11},{10,... | collective-permute-start | bytes 589832 | tf_op jit(solution)/shard_map/ppermute | solution.py:27
  23.3 8.2 %collective-permute-done.refs_3_ = bf16[256,768]{1,0:T(8,128)(2,1)S(1)} collective-permute-done((bf16[256,768]{1,0:T(8,128)(2,1)S(1)}, bf16[256,768]{1,0:T(8,128)(2,1)S(1)}, u32[]{:S(2)}, u32[]{:S(2)}) %collective-permute-start) | collective-permute-done | bytes 393248 | tf_op jit(solution)/shard_map/ppermute | solution.py:27
  31.5 5.9 %collective-permute-start.2 = (bf16[128,768]{1,0:T(8,128)(2,1)S(1)}, bf16[128,768]{1,0:T(8,128)(2,1)S(1)}, u32[]{:S(2)}, u32[]{:S(2)}) collective-permute-start(bf16[128,768]{1,0:T(8,128)(2,1)S(1)} %slice.16), channel_id=1, source_target_pairs={{0,1},{1,2},{2,3},{3,0},{4,5},{5,6},{6,7},{7,4},{8,9},{9,10},{10,1... | collective-permute-start | bytes 589832 | tf_op jit(solution)/shard_map/ppermute | solution.py:27
  37.9 4.0 %collective-permute-done.2.refs_5_ = bf16[128,768]{1,0:T(8,128)(2,1)S(1)} collective-permute-done((bf16[128,768]{1,0:T(8,128)(2,1)S(1)}, bf16[128,768]{1,0:T(8,128)(2,1)S(1)}, u32[]{:S(2)}, u32[]{:S(2)}) %collective-permute-start.2) | collective-permute-done | bytes 196640 | tf_op jit(solution)/shard_map/ppermute | solution.py:27
  42.6 3.4 %collective-permute-done.3.refs_6_ = bf16[128,768]{1,0:T(8,128)(2,1)} collective-permute-done((bf16[128,768]{1,0:T(8,128)(2,1)S(1)}, bf16[128,768]{1,0:T(8,128)(2,1)}, u32[]{:S(2)}, u32[]{:S(2)}) %collective-permute-start.3) | collective-permute-done | bytes 196640 | tf_op jit(solution)/shard_map/ppermute | solution.py:27
  47.1 12.0 %attend.1 = (bf16[8,2,128,384]{3,2,1,0:T(8,128)(2,1)}, f32[256,768]{1,0:T(8,128)}, bf16[256,768]{1,0:T(8,128)(2,1)}, bf16[256,768]{1,0:T(8,128)(2,1)}, bf16[256,768]{1,0:T(8,128)(2,1)}) custom-call(s32[69]{0:T(128)} %concatenate.3.refs_0_.ids, bf16[8,2,128,384]{3,2,1,0:T(8,128)(2,1)} %copy-done.1, bf16[256,768]{1,0:T(8,128)(2,1)} %copy-done.10, ...), custom_call_target="tpu_custom_call" | custom-call | tf_op jit(solution)/shard_map/attend/pallas_call | solution.py:214
  60.4 2.1 %collective-permute-start.9 = (bf16[256,768]{1,0:T(8,128)(2,1)}, bf16[256,768]{1,0:T(8,128)(2,1)}, u32[]{:S(2)}, u32[]{:S(2)}) collective-permute-start(bf16[256,768]{1,0:T(8,128)(2,1)} %get-tuple-element.28), channel_id=1, source_target_pairs={{0,1},{1,2},{2,3},{3,0},{4,5},{5,6},{6,7},{7,4},{8,9},{9,10},{10,1... | collective-permute-start | bytes 1179656 | tf_op jit(solution)/shard_map/ppermute | solution.py:27
  63.3 2.4 %assemble.1.rest = bf16[768,768]{1,0:T(8,128)(2,1)} custom-call(s32[69]{0:T(128)} %concatenate.3.refs_0_.ids, bf16[768,256]{1,0:T(8,128)(2,1)} %copy-done.8, bf16[384,256]{1,0:T(8,128)(2,1)} %collective-permute-done.5.far, bf16[768,256]{1,0:T(8,128)(2,1)} %copy-done.9, bf16[384,256]{1,0:T(8,128)(2,1)} %collective-permute-done.7.far_swapped), custom_call_target="tpu_custom_call" | custom-call | tf_op jit(solution)/shard_map/assemble/pallas_call | solution.py:251
  65.7 1.9 %collective-permute-start.16 = (bf16[768,768]{1,0:T(8,128)(2,1)}, bf16[768,768]{1,0:T(8,128)(2,1)S(1)}, u32[]{:S(2)}, u32[]{:S(2)}) collective-permute-start(bf16[768,768]{1,0:T(8,128)(2,1)} %assemble.1.rest), channel_id=1, source_target_pairs={{0,32},{4,228},{8,40},{12,236},{16,48},{20,244},{24,56},{28,252},{... | collective-permute-start | bytes 3538952 | tf_op jit(solution)/shard_map/ppermute | solution.py:381
  67.7 6.8 %all-to-all-start.1 = ((bf16[8,2,128,384]{3,2,1,0:T(8,128)(2,1)}), bf16[8,2,128,384]{3,2,1,0:T(8,128)(2,1)S(1)}, u32[]{:S(2)}, u32[]{:S(2)}) async-start(bf16[8,2,128,384]{3,2,1,0:T(8,128)(2,1)} %get-tuple-element.21), calls=%async_computation.1 | async-start | bytes 3145728 | tf_op jit(solution)/shard_map/all_to_all | solution.py:322
  74.5 5.0 %collective-permute-done.11 = bf16[256,768]{1,0:T(8,128)(2,1)} collective-permute-done((bf16[256,768]{1,0:T(8,128)(2,1)}, bf16[256,768]{1,0:T(8,128)(2,1)}, u32[]{:S(2)}, u32[]{:S(2)}) %collective-permute-start.11) | collective-permute-done | bytes 393248 | tf_op jit(solution)/shard_map/ppermute | solution.py:27
  79.5 1.4 %add_convert_fusion = bf16[256,768]{1,0:T(8,128)(2,1)S(1)} fusion(bf16[256,768]{1,0:T(8,128)(2,1)} %collective-permute-done.11, bf16[256,768]{1,0:T(8,128)(2,1)} %collective-permute-done.10, f32[256,768]{1,0:T(8,128)S(1)} %copy-done.7, bf16[256,768]{1,0:T(8,128)(2,1)} %collective-permute-done.9), kind=kLoop, calls=%fused_computation.1 | loop fusion | flops 1376256 | bytes 2359296 | tf_op jit(solution)/shard_map/convert_element_type | solution.py:382
  81.0 2.0 %collective-permute-start.12 = (bf16[256,384]{1,0:T(8,128)(2,1)S(1)}, bf16[256,384]{1,0:T(8,128)(2,1)S(1)}, u32[]{:S(2)}, u32[]{:S(2)}) collective-permute-start(bf16[256,384]{1,0:T(8,128)(2,1)S(1)} %get-tuple-element.48), channel_id=1, source_target_pairs={{0,32},{4,228},{8,40},{12,236},{16,48},{20,244},{24,56},{28,252},{... | collective-permute-start | bytes 589832 | tf_op jit(solution)/shard_map/ppermute | solution.py:384
  84.6 1.8 %collective-permute-done.8.paired_held = bf16[768,256]{1,0:T(8,128)(2,1)} collective-permute-done((bf16[768,256]{1,0:T(8,128)(2,1)}, bf16[768,256]{1,0:T(8,128)(2,1)}, u32[]{:S(2)}, u32[]{:S(2)}) %collective-permute-start.8) | collective-permute-done | bytes 393248 | tf_op jit(solution)/shard_map/ppermute | solution.py:371
  86.6 1.8 %collective-permute-done.12.came = bf16[256,384]{1,0:T(8,128)(2,1)S(1)} collective-permute-done((bf16[256,384]{1,0:T(8,128)(2,1)S(1)}, bf16[256,384]{1,0:T(8,128)(2,1)S(1)}, u32[]{:S(2)}, u32[]{:S(2)}) %collective-permute-start.12) | collective-permute-done | bytes 196640 | tf_op jit(solution)/shard_map/ppermute | solution.py:384
  90.9 3.4 %collective-permute-start.19 = (bf16[256,384]{1,0:T(8,128)(2,1)S(1)}, bf16[256,384]{1,0:T(8,128)(2,1)}, u32[]{:S(2)}, u32[]{:S(2)}) collective-permute-start(bf16[256,384]{1,0:T(8,128)(2,1)S(1)} %collective-permute-done.12.came), channel_id=1, source_target_pairs={{0,3},{1,0},{2,1},{3,2},{4,7},{5,4},{6,5},{7,6},{8,11},{9,8},{10,9... | collective-permute-start | bytes 589832 | tf_op jit(solution)/shard_map/ppermute | solution.py:27
  94.4 4.8 %collective-permute-done.15.refs_3_ = bf16[256,384]{1,0:T(8,128)(2,1)} collective-permute-done((bf16[256,384]{1,0:T(8,128)(2,1)S(1)}, bf16[256,384]{1,0:T(8,128)(2,1)}, u32[]{:S(2)}, u32[]{:S(2)}) %collective-permute-start.15) | collective-permute-done | bytes 196640 | tf_op jit(solution)/shard_map/ppermute | solution.py:27
  99.2 4.0 %first_product.1.refs_1_ = f32[768,384]{1,0:T(8,128)} custom-call(bf16[768,256]{1,0:T(8,128)(2,1)} %get-tuple-element.24.held, bf16[768,768]{1,0:T(8,128)(2,1)} %assemble.1.rest, bf16[768,256]{1,0:T(8,128)(2,1)} %collective-permute-done.8.paired_held, bf16[256,384]{1,0:T(8,128)(2,1)} %copy-done.11, bf16[256,384]{1,0:T(8,128)(2,1)} %copy-done.6, ...), custom_call_target="tpu_custom_call" | custom-call | tf_op jit(solution)/shard_map/first_product/pallas_call | solution.py:271
  103.2 1.9 %collective-permute-done.19.refs_5_ = bf16[256,384]{1,0:T(8,128)(2,1)} collective-permute-done((bf16[256,384]{1,0:T(8,128)(2,1)S(1)}, bf16[256,384]{1,0:T(8,128)(2,1)}, u32[]{:S(2)}, u32[]{:S(2)}) %collective-permute-start.19) | collective-permute-done | bytes 196640 | tf_op jit(solution)/shard_map/ppermute | solution.py:27
  105.1 3.4 %second_product.1 = (f32[96,384]{1,0:T(8,128)}, bf16[96,384]{1,0:T(8,128)(2,1)}, bf16[96,384]{1,0:T(8,128)(2,1)}, bf16[96,384]{1,0:T(8,128)(2,1)}, bf16[96,384]{...) custom-call(s32[69]{0:T(128)} %concatenate.3.refs_0_.ids, ...), custom_call_target="tpu_custom_call" | custom-call | tf_op jit(solution)/shard_map/second_product/pallas_call | solution.py:300
  109.4 6.5 %collective-permute-start.21 = (bf16[96,384]{1,0:T(8,128)(2,1)}, bf16[96,384]{1,0:T(8,128)(2,1)S(1)}, u32[]{:S(2)}, u32[]{:S(2)}) collective-permute-start(bf16[96,384]{1,0:T(8,128)(2,1)} %get-tuple-element.32), channel_id=1, source_target_pairs={{0,96},{32,128},{64,160},{96,192},{128,224},{160,0},{192,32},{224,... | collective-permute-start | bytes 221192 | tf_op jit(solution)/shard_map/ppermute | solution.py:27
  115.9 2.0 %collective-permute-start.23 = (bf16[96,384]{1,0:T(8,128)(2,1)}, bf16[96,384]{1,0:T(8,128)(2,1)S(1)}, u32[]{:S(2)}, u32[]{:S(2)}) collective-permute-start(bf16[96,384]{1,0:T(8,128)(2,1)} %get-tuple-element.34), channel_id=1, source_target_pairs={{0,224},{32,0},{64,32},{96,64},{128,96},{160,128},{192,160},{224,1... | collective-permute-start | bytes 221192 | tf_op jit(solution)/shard_map/ppermute | solution.py:27
  118.4 4.4 %collective-permute-start.25 = (bf16[96,384]{1,0:T(8,128)(2,1)}, bf16[96,384]{1,0:T(8,128)(2,1)S(1)}, u32[]{:S(2)}, u32[]{:S(2)}) collective-permute-start(bf16[96,384]{1,0:T(8,128)(2,1)} %get-tuple-element.37), channel_id=1, source_target_pairs={{0,128},{32,160},{64,192},{96,224},{128,0},{160,32},{192,64},{224,... | collective-permute-start | bytes 221192 | tf_op jit(solution)/shard_map/ppermute | solution.py:27
  122.8 3.7 %collective-permute-start.26 = (bf16[96,384]{1,0:T(8,128)(2,1)}, bf16[96,384]{1,0:T(8,128)(2,1)S(1)}, u32[]{:S(2)}, u32[]{:S(2)}) collective-permute-start(bf16[96,384]{1,0:T(8,128)(2,1)} %get-tuple-element.38), channel_id=1, source_target_pairs={{0,192},{32,224},{64,0},{96,32},{128,64},{160,96},{192,128},{224,1... | collective-permute-start | bytes 221192 | tf_op jit(solution)/shard_map/ppermute | solution.py:27
  126.5 1.8 %collective-permute-done.25 = bf16[96,384]{1,0:T(8,128)(2,1)S(1)} collective-permute-done((bf16[96,384]{1,0:T(8,128)(2,1)}, bf16[96,384]{1,0:T(8,128)(2,1)S(1)}, u32[]{:S(2)}, u32[]{:S(2)}) %collective-permute-start.25) | collective-permute-done | bytes 73760 | tf_op jit(solution)/shard_map/ppermute | solution.py:27
  128.3 2.6 %collective-permute-done.26 = bf16[96,384]{1,0:T(8,128)(2,1)S(1)} collective-permute-done((bf16[96,384]{1,0:T(8,128)(2,1)}, bf16[96,384]{1,0:T(8,128)(2,1)S(1)}, u32[]{:S(2)}, u32[]{:S(2)}) %collective-permute-start.26) | collective-permute-done | bytes 73760 | tf_op jit(solution)/shard_map/ppermute | solution.py:27
  134.1 2.7 %unpack.1 = (bf16[128,3072]{1,0:T(8,128)(2,1)}, bf16[128,3072]{1,0:T(8,128)(2,1)}) custom-call(bf16[8,2,128,384]{3,2,1,0:T(8,128)(2,1)} %copy-done), custom_call_target="tpu_custom_call" | custom-call | tf_op jit(solution)/shard_map/unpack/pallas_call | solution.py:58
  (79 shorter events, 17.4 us)
Async XLA Ops:
  3.3 42.6 %all-to-all-start = ((bf16[8,2,128,384]{3,2,1,0:T(8,128)(2,1)}), bf16[8,2,128,384]{3,2,1,0:T(8,128)(2,1)S(1)}, u32[]{:S(2)}, u32[]{:S(2)}) async-start(bf16[8,2,128,384]{3,2,1,0:T(8,128)(2,1)} %pack.1), calls=%async_computation | async-start | bytes 3145728 | tf_op jit(solution)/shard_map/all_to_all | solution.py:322
  13.7 9.6 %collective-permute-start.4 = (bf16[768,256]{1,0:T(8,128)(2,1)}, bf16[768,256]{1,0:T(8,128)(2,1)S(1)}, u32[]{:S(2)}, u32[]{:S(2)}) collective-permute-start(bf16[768,256]{1,0:T(8,128)(2,1)} %get-tuple-element.25), channel_id=1, source_target_pairs={{0,1},{1,2},{2,3},{3,0},{4,7},{5,4},{6,5},{7,6},{8,9},{9,10},{10,1... | collective-permute-start | bytes 1179656 | tf_op jit(solution)/shard_map/ppermute | solution.py:369
  19.4 26.5 %copy-start.10 = (bf16[256,768]{1,0:T(8,128)(2,1)}, bf16[256,768]{1,0:T(8,128)(2,1)S(1)}, u32[]{:S(2)}) copy-start(bf16[256,768]{1,0:T(8,128)(2,1)S(1)} %convolution_convert_fusion.refs_2_) | copy-start | bytes 1179652
  19.5 12.1 %collective-permute-start = (bf16[256,768]{1,0:T(8,128)(2,1)S(1)}, bf16[256,768]{1,0:T(8,128)(2,1)S(1)}, u32[]{:S(2)}, u32[]{:S(2)}) collective-permute-start(bf16[256,768]{1,0:T(8,128)(2,1)S(1)} %convolution_convert_fusion.refs_2_), channel_id=1, source_target_pairs={{0,1},{1,2},{2,3},{3,0},{4,5},{5,6},{6,7},{7,4},{8,9},{9,10},{10,1... | collective-permute-start | bytes 1179656 | tf_op jit(solution)/shard_map/ppermute | solution.py:27
  20.2 17.4 %collective-permute-start.1 = (bf16[256,768]{1,0:T(8,128)(2,1)S(1)}, bf16[256,768]{1,0:T(8,128)(2,1)S(1)}, u32[]{:S(2)}, u32[]{:S(2)}) collective-permute-start(bf16[256,768]{1,0:T(8,128)(2,1)S(1)} %convolution_convert_fusion.refs_2_), channel_id=1, source_target_pairs={{0,3},{1,0},{2,1},{3,2},{4,7},{5,4},{6,5},{7,6},{8,11},{9,8},{10,9... | collective-permute-start | bytes 1179656 | tf_op jit(solution)/shard_map/ppermute | solution.py:27
  21.6 16.1 %collective-permute-start.5 = (bf16[384,256]{1,0:T(8,128)(2,1)S(1)}, bf16[384,256]{1,0:T(8,128)(2,1)}, u32[]{:S(2)}, u32[]{:S(2)}) collective-permute-start(bf16[384,256]{1,0:T(8,128)(2,1)S(1)} %copy-done.16), channel_id=1, source_target_pairs={{0,2},{1,3},{2,0},{3,1},{4,6},{5,7},{6,4},{7,5},{8,10},{9,11},{10,... | collective-permute-start | bytes 589832 | tf_op jit(solution)/shard_map/ppermute | solution.py:27
  23.3 39.2 %copy-start.8 = (bf16[768,256]{1,0:T(8,128)(2,1)}, bf16[768,256]{1,0:T(8,128)(2,1)S(1)}, u32[]{:S(2)}) copy-start(bf16[768,256]{1,0:T(8,128)(2,1)S(1)} %collective-permute-done.4.near) | copy-start | bytes 1179652
  23.3 39.2 %collective-permute-start.6 = (bf16[768,256]{1,0:T(8,128)(2,1)S(1)}, bf16[768,256]{1,0:T(8,128)(2,1)S(1)}, u32[]{:S(2)}, u32[]{:S(2)}) collective-permute-start(bf16[768,256]{1,0:T(8,128)(2,1)S(1)} %collective-permute-done.4.near), channel_id=1, source_target_pairs={{0,4},{4,0},{8,12},{12,8},{16,20},{20,16},{24,28},{28,24},{1,5},{5... | collective-permute-start | bytes 1179656 | tf_op jit(solution)/shard_map/ppermute | solution.py:378
  31.5 10.3 %collective-permute-start.2 = (bf16[128,768]{1,0:T(8,128)(2,1)S(1)}, bf16[128,768]{1,0:T(8,128)(2,1)S(1)}, u32[]{:S(2)}, u32[]{:S(2)}) collective-permute-start(bf16[128,768]{1,0:T(8,128)(2,1)S(1)} %slice.16), channel_id=1, source_target_pairs={{0,1},{1,2},{2,3},{3,0},{4,5},{5,6},{6,7},{7,4},{8,9},{9,10},{10,1... | collective-permute-start | bytes 589832 | tf_op jit(solution)/shard_map/ppermute | solution.py:27
  37.6 8.3 %collective-permute-start.3 = (bf16[128,768]{1,0:T(8,128)(2,1)S(1)}, bf16[128,768]{1,0:T(8,128)(2,1)}, u32[]{:S(2)}, u32[]{:S(2)}) collective-permute-start(bf16[128,768]{1,0:T(8,128)(2,1)S(1)} %slice.17), channel_id=1, source_target_pairs={{0,3},{1,0},{2,1},{3,2},{4,7},{5,4},{6,5},{7,6},{8,11},{9,8},{10,9... | collective-permute-start | bytes 589832 | tf_op jit(solution)/shard_map/ppermute | solution.py:27
  37.7 24.8 %collective-permute-start.7 = (bf16[384,256]{1,0:T(8,128)(2,1)}, bf16[384,256]{1,0:T(8,128)(2,1)}, u32[]{:S(2)}, u32[]{:S(2)}) collective-permute-start(bf16[384,256]{1,0:T(8,128)(2,1)} %collective-permute-done.5.far), channel_id=1, source_target_pairs={{0,4},{4,0},{8,12},{12,8},{16,20},{20,16},{24,28},{28,24},{1,5},{5... | collective-permute-start | bytes 589832 | tf_op jit(solution)/shard_map/ppermute | solution.py:379
  59.1 15.4 %collective-permute-start.10 = (bf16[256,768]{1,0:T(8,128)(2,1)}, bf16[256,768]{1,0:T(8,128)(2,1)}, u32[]{:S(2)}, u32[]{:S(2)}) collective-permute-start(bf16[256,768]{1,0:T(8,128)(2,1)} %get-tuple-element.29), channel_id=1, source_target_pairs={{0,2},{1,3},{2,0},{3,1},{4,6},{5,7},{6,4},{7,5},{8,10},{9,11},{10,... | collective-permute-start | bytes 1179656 | tf_op jit(solution)/shard_map/ppermute | solution.py:27
  59.2 20.3 %collective-permute-start.11 = (bf16[256,768]{1,0:T(8,128)(2,1)}, bf16[256,768]{1,0:T(8,128)(2,1)}, u32[]{:S(2)}, u32[]{:S(2)}) collective-permute-start(bf16[256,768]{1,0:T(8,128)(2,1)} %get-tuple-element.30), channel_id=1, source_target_pairs={{0,3},{1,0},{2,1},{3,2},{4,7},{5,4},{6,5},{7,6},{8,11},{9,8},{10,9... | collective-permute-start | bytes 1179656 | tf_op jit(solution)/shard_map/ppermute | solution.py:27
  60.4 19.1 %collective-permute-start.9 = (bf16[256,768]{1,0:T(8,128)(2,1)}, bf16[256,768]{1,0:T(8,128)(2,1)}, u32[]{:S(2)}, u32[]{:S(2)}) collective-permute-start(bf16[256,768]{1,0:T(8,128)(2,1)} %get-tuple-element.28), channel_id=1, source_target_pairs={{0,1},{1,2},{2,3},{3,0},{4,5},{5,6},{6,7},{7,4},{8,9},{9,10},{10,1... | collective-permute-start | bytes 1179656 | tf_op jit(solution)/shard_map/ppermute | solution.py:27
  65.7 37.5 %collective-permute-start.16 = (bf16[768,768]{1,0:T(8,128)(2,1)}, bf16[768,768]{1,0:T(8,128)(2,1)S(1)}, u32[]{:S(2)}, u32[]{:S(2)}) collective-permute-start(bf16[768,768]{1,0:T(8,128)(2,1)} %assemble.1.rest), channel_id=1, source_target_pairs={{0,32},{4,228},{8,40},{12,236},{16,48},{20,244},{24,56},{28,252},{... | collective-permute-start | bytes 3538952 | tf_op jit(solution)/shard_map/ppermute | solution.py:381
  67.6 18.8 %collective-permute-start.8 = (bf16[768,256]{1,0:T(8,128)(2,1)}, bf16[768,256]{1,0:T(8,128)(2,1)}, u32[]{:S(2)}, u32[]{:S(2)}) collective-permute-start(bf16[768,256]{1,0:T(8,128)(2,1)} %get-tuple-element.24.held), channel_id=1, source_target_pairs={{0,32},{4,228},{8,40},{12,236},{16,48},{20,244},{24,56},{28,252},{... | collective-permute-start | bytes 1179656 | tf_op jit(solution)/shard_map/ppermute | solution.py:371
  67.7 65.2 %all-to-all-start.1 = ((bf16[8,2,128,384]{3,2,1,0:T(8,128)(2,1)}), bf16[8,2,128,384]{3,2,1,0:T(8,128)(2,1)S(1)}, u32[]{:S(2)}, u32[]{:S(2)}) async-start(bf16[8,2,128,384]{3,2,1,0:T(8,128)(2,1)} %get-tuple-element.21), calls=%async_computation.1 | async-start | bytes 3145728 | tf_op jit(solution)/shard_map/all_to_all | solution.py:322
  81.0 18.2 %copy-start.6 = (bf16[256,384]{1,0:T(8,128)(2,1)}, bf16[256,384]{1,0:T(8,128)(2,1)S(1)}, u32[]{:S(2)}) copy-start(bf16[256,384]{1,0:T(8,128)(2,1)S(1)} %get-tuple-element.47.refs_0_) | copy-start | bytes 589828
  81.0 7.4 %collective-permute-start.12 = (bf16[256,384]{1,0:T(8,128)(2,1)S(1)}, bf16[256,384]{1,0:T(8,128)(2,1)S(1)}, u32[]{:S(2)}, u32[]{:S(2)}) collective-permute-start(bf16[256,384]{1,0:T(8,128)(2,1)S(1)} %get-tuple-element.48), channel_id=1, source_target_pairs={{0,32},{4,228},{8,40},{12,236},{16,48},{20,244},{24,56},{28,252},{... | collective-permute-start | bytes 589832 | tf_op jit(solution)/shard_map/ppermute | solution.py:384
  83.0 6.7 %collective-permute-start.13 = (bf16[256,384]{1,0:T(8,128)(2,1)S(1)}, bf16[256,384]{1,0:T(8,128)(2,1)S(1)}, u32[]{:S(2)}, u32[]{:S(2)}) collective-permute-start(bf16[256,384]{1,0:T(8,128)(2,1)S(1)} %get-tuple-element.47.refs_0_), channel_id=1, source_target_pairs={{0,1},{1,2},{2,3},{3,0},{4,5},{5,6},{6,7},{7,4},{8,9},{9,10},{10,1... | collective-permute-start | bytes 589832 | tf_op jit(solution)/shard_map/ppermute | solution.py:27
  83.8 7.2 %collective-permute-start.14 = (bf16[256,384]{1,0:T(8,128)(2,1)S(1)}, bf16[256,384]{1,0:T(8,128)(2,1)S(1)}, u32[]{:S(2)}, u32[]{:S(2)}) collective-permute-start(bf16[256,384]{1,0:T(8,128)(2,1)S(1)} %get-tuple-element.47.refs_0_), channel_id=1, source_target_pairs={{0,2},{1,3},{2,0},{3,1},{4,6},{5,7},{6,4},{7,5},{8,10},{9,11},{10,... | collective-permute-start | bytes 589832 | tf_op jit(solution)/shard_map/ppermute | solution.py:27
  86.4 12.8 %collective-permute-start.15 = (bf16[256,384]{1,0:T(8,128)(2,1)S(1)}, bf16[256,384]{1,0:T(8,128)(2,1)}, u32[]{:S(2)}, u32[]{:S(2)}) collective-permute-start(bf16[256,384]{1,0:T(8,128)(2,1)S(1)} %get-tuple-element.47.refs_0_), channel_id=1, source_target_pairs={{0,3},{1,0},{2,1},{3,2},{4,7},{5,4},{6,5},{7,6},{8,11},{9,8},{10,9... | collective-permute-start | bytes 589832 | tf_op jit(solution)/shard_map/ppermute | solution.py:27
  88.4 14.8 %collective-permute-start.17 = (bf16[256,384]{1,0:T(8,128)(2,1)S(1)}, bf16[256,384]{1,0:T(8,128)(2,1)}, u32[]{:S(2)}, u32[]{:S(2)}) collective-permute-start(bf16[256,384]{1,0:T(8,128)(2,1)S(1)} %collective-permute-done.12.came), channel_id=1, source_target_pairs={{0,1},{1,2},{2,3},{3,0},{4,5},{5,6},{6,7},{7,4},{8,9},{9,10},{10,1... | collective-permute-start | bytes 589832 | tf_op jit(solution)/shard_map/ppermute | solution.py:27
  89.6 13.6 %collective-permute-start.18 = (bf16[256,384]{1,0:T(8,128)(2,1)S(1)}, bf16[256,384]{1,0:T(8,128)(2,1)}, u32[]{:S(2)}, u32[]{:S(2)}) collective-permute-start(bf16[256,384]{1,0:T(8,128)(2,1)S(1)} %collective-permute-done.12.came), channel_id=1, source_target_pairs={{0,2},{1,3},{2,0},{3,1},{4,6},{5,7},{6,4},{7,5},{8,10},{9,11},{10,... | collective-permute-start | bytes 589832 | tf_op jit(solution)/shard_map/ppermute | solution.py:27
  90.9 14.2 %collective-permute-start.19 = (bf16[256,384]{1,0:T(8,128)(2,1)S(1)}, bf16[256,384]{1,0:T(8,128)(2,1)}, u32[]{:S(2)}, u32[]{:S(2)}) collective-permute-start(bf16[256,384]{1,0:T(8,128)(2,1)S(1)} %collective-permute-done.12.came), channel_id=1, source_target_pairs={{0,3},{1,0},{2,1},{3,2},{4,7},{5,4},{6,5},{7,6},{8,11},{9,8},{10,9... | collective-permute-start | bytes 589832 | tf_op jit(solution)/shard_map/ppermute | solution.py:27
  108.5 9.9 %collective-permute-start.20 = (bf16[96,384]{1,0:T(8,128)(2,1)}, bf16[96,384]{1,0:T(8,128)(2,1)S(1)}, u32[]{:S(2)}, u32[]{:S(2)}) collective-permute-start(bf16[96,384]{1,0:T(8,128)(2,1)} %get-tuple-element.31), channel_id=1, source_target_pairs={{0,32},{32,64},{64,96},{96,128},{128,160},{160,192},{192,224},{224... | collective-permute-start | bytes 221192 | tf_op jit(solution)/shard_map/ppermute | solution.py:27
  109.4 13.5 %collective-permute-start.21 = (bf16[96,384]{1,0:T(8,128)(2,1)}, bf16[96,384]{1,0:T(8,128)(2,1)S(1)}, u32[]{:S(2)}, u32[]{:S(2)}) collective-permute-start(bf16[96,384]{1,0:T(8,128)(2,1)} %get-tuple-element.32), channel_id=1, source_target_pairs={{0,96},{32,128},{64,160},{96,192},{128,224},{160,0},{192,32},{224,... | collective-permute-start | bytes 221192 | tf_op jit(solution)/shard_map/ppermute | solution.py:27
  115.9 10.6 %collective-permute-start.22 = (bf16[96,384]{1,0:T(8,128)(2,1)}, bf16[96,384]{1,0:T(8,128)(2,1)S(1)}, u32[]{:S(2)}, u32[]{:S(2)}) collective-permute-start(bf16[96,384]{1,0:T(8,128)(2,1)} %get-tuple-element.33), channel_id=1, source_target_pairs={{0,160},{32,192},{64,224},{96,0},{128,32},{160,64},{192,96},{224,1... | collective-permute-start | bytes 221192 | tf_op jit(solution)/shard_map/ppermute | solution.py:27
  115.9 10.6 %collective-permute-start.23 = (bf16[96,384]{1,0:T(8,128)(2,1)}, bf16[96,384]{1,0:T(8,128)(2,1)S(1)}, u32[]{:S(2)}, u32[]{:S(2)}) collective-permute-start(bf16[96,384]{1,0:T(8,128)(2,1)} %get-tuple-element.34), channel_id=1, source_target_pairs={{0,224},{32,0},{64,32},{96,64},{128,96},{160,128},{192,160},{224,1... | collective-permute-start | bytes 221192 | tf_op jit(solution)/shard_map/ppermute | solution.py:27
  117.9 8.6 %collective-permute-start.24 = (bf16[96,384]{1,0:T(8,128)(2,1)}, bf16[96,384]{1,0:T(8,128)(2,1)S(1)}, u32[]{:S(2)}, u32[]{:S(2)}) collective-permute-start(bf16[96,384]{1,0:T(8,128)(2,1)} %get-tuple-element.36), channel_id=1, source_target_pairs={{0,64},{32,96},{64,128},{96,160},{128,192},{160,224},{192,0},{224,... | collective-permute-start | bytes 221192 | tf_op jit(solution)/shard_map/ppermute | solution.py:27
  118.4 9.9 %collective-permute-start.25 = (bf16[96,384]{1,0:T(8,128)(2,1)}, bf16[96,384]{1,0:T(8,128)(2,1)S(1)}, u32[]{:S(2)}, u32[]{:S(2)}) collective-permute-start(bf16[96,384]{1,0:T(8,128)(2,1)} %get-tuple-element.37), channel_id=1, source_target_pairs={{0,128},{32,160},{64,192},{96,224},{128,0},{160,32},{192,64},{224,... | collective-permute-start | bytes 221192 | tf_op jit(solution)/shard_map/ppermute | solution.py:27
  122.8 8.1 %collective-permute-start.26 = (bf16[96,384]{1,0:T(8,128)(2,1)}, bf16[96,384]{1,0:T(8,128)(2,1)S(1)}, u32[]{:S(2)}, u32[]{:S(2)}) collective-permute-start(bf16[96,384]{1,0:T(8,128)(2,1)} %get-tuple-element.38), channel_id=1, source_target_pairs={{0,192},{32,224},{64,0},{96,32},{128,64},{160,96},{192,128},{224,1... | collective-permute-start | bytes 221192 | tf_op jit(solution)/shard_map/ppermute | solution.py:27
  (14 other events, 80.6 us)

commit v3 on v2

--- a/solution.py
+++ b/solution.py
@@ -36,11 +36,15 @@
 
 def pack(query, grad, frames):
     rows, width = query.shape
+    steps = 2
+    part = pl.BlockSpec((rows, width // steps), lambda i: (0, i))
+    shape = (frames, 2, rows, width // frames)
     return pl.pallas_call(
         pack_kernel,
-        out_shape=jax.ShapeDtypeStruct((frames, 2, rows, width // frames), query.dtype),
-        in_specs=[VMEM, VMEM],
-        out_specs=VMEM,
+        grid=(steps,),
+        out_shape=jax.ShapeDtypeStruct(shape, query.dtype),
+        in_specs=[part, part],
+        out_specs=pl.BlockSpec((frames // steps, *shape[1:]), lambda i: (i, 0, 0, 0)),
         name="pack",
     )(query, grad)
 
@@ -204,7 +208,7 @@
     share, width = tables[0].shape
     heads = width // (2 * HD)
     total = share * audio_count
-    count = 2
+    count = 4
     rows = pl.BlockSpec((count, *arrived.shape[1:]), lambda i: (i, 0, 0, 0))
     part = pl.BlockSpec((share, width), lambda i: (0, 0))
 

time: 137 us -> 137 us (level)
  no operation moved by 1% of the time
where the time goes in v3:
time: 137 us; the launch traced here: 136 us
  starting transfers between devices  55.9 us (41%)
  waiting for transfers between devices  35.8 us (26%)
  Pallas kernels  30 us (22%)
  local copies, waits for them, and re-layouts  8.81 us (6%)
  other arithmetic  2.41 us (2%)
  between operations  2.14 us (2%)
  matrix products  1.39 us (1%)
    ppermute x21, starting transfers between devices, shifted(): lax.ppermute(array, axis, [(i, (i + by) % count) for i in range(count)])  38.9 us
    ppermute x21, waiting for transfers between devices, shifted(): lax.ppermute(array, axis, [(i, (i + by) % count) for i in range(count)])  32.1 us
    pallas_call x1, Pallas kernels, attend(): pl.pallas_call(kernel, grid=(arrived.shape[0] // count,), out_shape=[jax....  11.9 us
    all_to_all x2, starting transfers between devices, to_owners(): return lax.all_to_all(array, axis, split_axis=0, concat_axis=0, tiled=True)  11.8 us
    unnamed x37, local copies, waits for them, and re-layouts  8.06 us
    pallas_call x1, Pallas kernels, first_product(): pl.pallas_call(first_product_kernel, out_shape=jax.ShapeDtypeStruct(shape...  3.98 us
    pallas_call x1, Pallas kernels, second_product(): pl.pallas_call(kernel, out_shape=[jax.ShapeDtypeStruct(shape, F32)] + [ja...  3.41 us
    pallas_call x1, Pallas kernels, turn(): pl.pallas_call(kernel, out_shape=[jax.ShapeDtypeStruct((share, count), la...  3.32 us
  transfers between devices with their start and end apart: 29, of which 12 were waited for; matrix products, arithmetic and copies ran while one was open for 6% of the time, Pallas kernels for 18%

profile of v3, /device:TPU:26, one launch (start us, length us, event | category | flops | bytes accessed | tf_op | source)
XLA Modules:
  0.0 136.5 jit_solution(2776009053760708176)
XLA Ops:
  0.6 2.4 %pack.1 = bf16[8,2,128,384]{3,2,1,0:T(8,128)(2,1)} custom-call(bf16[128,3072]{1,0:T(8,128)(2,1)} %bitcast.20, bf16[128,3072]{1,0:T(8,128)(2,1)} %bitcast.21), custom_call_target="tpu_custom_call" | custom-call | tf_op jit(solution)/shard_map/pack/pallas_call | solution.py:42
  3.0 5.0 %all-to-all-start = ((bf16[8,2,128,384]{3,2,1,0:T(8,128)(2,1)}), bf16[8,2,128,384]{3,2,1,0:T(8,128)(2,1)S(1)}, u32[]{:S(2)}, u32[]{:S(2)}) async-start(bf16[8,2,128,384]{3,2,1,0:T(8,128)(2,1)} %pack.1), calls=%async_computation | async-start | bytes 3145728 | tf_op jit(solution)/shard_map/all_to_all | solution.py:326
  10.0 3.3 %turn.1 = (bf16[768,256]{1,0:T(8,128)(2,1)}, bf16[768,256]{1,0:T(8,128)(2,1)}, bf16[384,256]{1,0:T(8,128)(2,1)}) custom-call(s32[69]{0:T(128)} %concatenate.3.refs_0_.ids, bf16[256,3072]{1,0:T(8,128)(2,1)} %bitcast.19), custom_call_target="tpu_custom_call" | custom-call | tf_op jit(solution)/shard_map/turn/pallas_call | solution.py:99
  14.4 3.3 %copy.14 = bf16[384,8,2,384]{3,1,2,0:T(8,128)(2,1)S(1)} copy(bf16[384,8,2,384]{3,2,1,0:T(2,128)(2,1)} %bitcast.17) | data formatting | bytes 9437184
  17.7 1.4 %convolution_convert_fusion.refs_2_ = bf16[256,768]{1,0:T(8,128)(2,1)S(1)} fusion(bf16[3072,768]{1,0:T(8,128)(2,1)S(1)} %bitcast.18, bf16[1,256,3072]{2,1,0:T(8,128)(2,1)S(1)} %copy-done.2), kind=kOutput, calls=%fused_computation | convolution fusion | flops 1208156160 | bytes 6684672 | tf_op jit(solution)/shard_map/dot_general | solution.py:363
  21.3 1.7 %collective-permute-start.5 = (bf16[384,256]{1,0:T(8,128)(2,1)S(1)}, bf16[384,256]{1,0:T(8,128)(2,1)}, u32[]{:S(2)}, u32[]{:S(2)}) collective-permute-start(bf16[384,256]{1,0:T(8,128)(2,1)S(1)} %copy-done.16), channel_id=1, source_target_pairs={{0,2},{1,3},{2,0},{3,1},{4,6},{5,7},{6,4},{7,5},{8,10},{9,11},{10,... | collective-permute-start | bytes 589832 | tf_op jit(solution)/shard_map/ppermute | solution.py:27
  23.0 8.2 %collective-permute-done.refs_3_ = bf16[256,768]{1,0:T(8,128)(2,1)S(1)} collective-permute-done((bf16[256,768]{1,0:T(8,128)(2,1)S(1)}, bf16[256,768]{1,0:T(8,128)(2,1)S(1)}, u32[]{:S(2)}, u32[]{:S(2)}) %collective-permute-start) | collective-permute-done | bytes 393248 | tf_op jit(solution)/shard_map/ppermute | solution.py:27
  31.2 5.9 %collective-permute-start.2 = (bf16[128,768]{1,0:T(8,128)(2,1)S(1)}, bf16[128,768]{1,0:T(8,128)(2,1)S(1)}, u32[]{:S(2)}, u32[]{:S(2)}) collective-permute-start(bf16[128,768]{1,0:T(8,128)(2,1)S(1)} %slice.16), channel_id=1, source_target_pairs={{0,1},{1,2},{2,3},{3,0},{4,5},{5,6},{6,7},{7,4},{8,9},{9,10},{10,1... | collective-permute-start | bytes 589832 | tf_op jit(solution)/shard_map/ppermute | solution.py:27
  37.6 4.0 %collective-permute-done.2.refs_5_ = bf16[128,768]{1,0:T(8,128)(2,1)S(1)} collective-permute-done((bf16[128,768]{1,0:T(8,128)(2,1)S(1)}, bf16[128,768]{1,0:T(8,128)(2,1)S(1)}, u32[]{:S(2)}, u32[]{:S(2)}) %collective-permute-start.2) | collective-permute-done | bytes 196640 | tf_op jit(solution)/shard_map/ppermute | solution.py:27
  42.2 3.4 %collective-permute-done.3.refs_6_ = bf16[128,768]{1,0:T(8,128)(2,1)} collective-permute-done((bf16[128,768]{1,0:T(8,128)(2,1)S(1)}, bf16[128,768]{1,0:T(8,128)(2,1)}, u32[]{:S(2)}, u32[]{:S(2)}) %collective-permute-start.3) | collective-permute-done | bytes 196640 | tf_op jit(solution)/shard_map/ppermute | solution.py:27
  46.8 11.9 %attend.1 = (bf16[8,2,128,384]{3,2,1,0:T(8,128)(2,1)}, f32[256,768]{1,0:T(8,128)}, bf16[256,768]{1,0:T(8,128)(2,1)}, bf16[256,768]{1,0:T(8,128)(2,1)}, bf16[256,768]{1,0:T(8,128)(2,1)}) custom-call(s32[69]{0:T(128)} %concatenate.3.refs_0_.ids, bf16[8,2,128,384]{3,2,1,0:T(8,128)(2,1)} %copy-done.1, bf16[256,768]{1,0:T(8,128)(2,1)} %copy-done.10, ...), custom_call_target="tpu_custom_call" | custom-call | tf_op jit(solution)/shard_map/attend/pallas_call | solution.py:218
  60.1 2.1 %collective-permute-start.9 = (bf16[256,768]{1,0:T(8,128)(2,1)}, bf16[256,768]{1,0:T(8,128)(2,1)}, u32[]{:S(2)}, u32[]{:S(2)}) collective-permute-start(bf16[256,768]{1,0:T(8,128)(2,1)} %get-tuple-element.28), channel_id=1, source_target_pairs={{0,1},{1,2},{2,3},{3,0},{4,5},{5,6},{6,7},{7,4},{8,9},{9,10},{10,1... | collective-permute-start | bytes 1179656 | tf_op jit(solution)/shard_map/ppermute | solution.py:27
  63.0 2.4 %assemble.1.rest = bf16[768,768]{1,0:T(8,128)(2,1)} custom-call(s32[69]{0:T(128)} %concatenate.3.refs_0_.ids, bf16[768,256]{1,0:T(8,128)(2,1)} %copy-done.8, bf16[384,256]{1,0:T(8,128)(2,1)} %collective-permute-done.5.far, bf16[768,256]{1,0:T(8,128)(2,1)} %copy-done.9, bf16[384,256]{1,0:T(8,128)(2,1)} %collective-permute-done.7.far_swapped), custom_call_target="tpu_custom_call" | custom-call | tf_op jit(solution)/shard_map/assemble/pallas_call | solution.py:255
  65.4 1.9 %collective-permute-start.16 = (bf16[768,768]{1,0:T(8,128)(2,1)}, bf16[768,768]{1,0:T(8,128)(2,1)S(1)}, u32[]{:S(2)}, u32[]{:S(2)}) collective-permute-start(bf16[768,768]{1,0:T(8,128)(2,1)} %assemble.1.rest), channel_id=1, source_target_pairs={{0,32},{4,228},{8,40},{12,236},{16,48},{20,244},{24,56},{28,252},{... | collective-permute-start | bytes 3538952 | tf_op jit(solution)/shard_map/ppermute | solution.py:385
  67.4 6.8 %all-to-all-start.1 = ((bf16[8,2,128,384]{3,2,1,0:T(8,128)(2,1)}), bf16[8,2,128,384]{3,2,1,0:T(8,128)(2,1)S(1)}, u32[]{:S(2)}, u32[]{:S(2)}) async-start(bf16[8,2,128,384]{3,2,1,0:T(8,128)(2,1)} %get-tuple-element.21), calls=%async_computation.1 | async-start | bytes 3145728 | tf_op jit(solution)/shard_map/all_to_all | solution.py:326
  74.2 5.0 %collective-permute-done.11 = bf16[256,768]{1,0:T(8,128)(2,1)} collective-permute-done((bf16[256,768]{1,0:T(8,128)(2,1)}, bf16[256,768]{1,0:T(8,128)(2,1)}, u32[]{:S(2)}, u32[]{:S(2)}) %collective-permute-start.11) | collective-permute-done | bytes 393248 | tf_op jit(solution)/shard_map/ppermute | solution.py:27
  79.2 1.4 %add_convert_fusion = bf16[256,768]{1,0:T(8,128)(2,1)S(1)} fusion(bf16[256,768]{1,0:T(8,128)(2,1)} %collective-permute-done.11, bf16[256,768]{1,0:T(8,128)(2,1)} %collective-permute-done.10, f32[256,768]{1,0:T(8,128)S(1)} %copy-done.7, bf16[256,768]{1,0:T(8,128)(2,1)} %collective-permute-done.9), kind=kLoop, calls=%fused_computation.1 | loop fusion | flops 1376256 | bytes 2359296 | tf_op jit(solution)/shard_map/convert_element_type | solution.py:386
  80.7 2.0 %collective-permute-start.12 = (bf16[256,384]{1,0:T(8,128)(2,1)S(1)}, bf16[256,384]{1,0:T(8,128)(2,1)S(1)}, u32[]{:S(2)}, u32[]{:S(2)}) collective-permute-start(bf16[256,384]{1,0:T(8,128)(2,1)S(1)} %get-tuple-element.48), channel_id=1, source_target_pairs={{0,32},{4,228},{8,40},{12,236},{16,48},{20,244},{24,56},{28,252},{... | collective-permute-start | bytes 589832 | tf_op jit(solution)/shard_map/ppermute | solution.py:388
  84.3 1.8 %collective-permute-done.8.paired_held = bf16[768,256]{1,0:T(8,128)(2,1)} collective-permute-done((bf16[768,256]{1,0:T(8,128)(2,1)}, bf16[768,256]{1,0:T(8,128)(2,1)}, u32[]{:S(2)}, u32[]{:S(2)}) %collective-permute-start.8) | collective-permute-done | bytes 393248 | tf_op jit(solution)/shard_map/ppermute | solution.py:375
  86.3 1.8 %collective-permute-done.12.came = bf16[256,384]{1,0:T(8,128)(2,1)S(1)} collective-permute-done((bf16[256,384]{1,0:T(8,128)(2,1)S(1)}, bf16[256,384]{1,0:T(8,128)(2,1)S(1)}, u32[]{:S(2)}, u32[]{:S(2)}) %collective-permute-start.12) | collective-permute-done | bytes 196640 | tf_op jit(solution)/shard_map/ppermute | solution.py:388
  90.7 3.4 %collective-permute-start.19 = (bf16[256,384]{1,0:T(8,128)(2,1)S(1)}, bf16[256,384]{1,0:T(8,128)(2,1)}, u32[]{:S(2)}, u32[]{:S(2)}) collective-permute-start(bf16[256,384]{1,0:T(8,128)(2,1)S(1)} %collective-permute-done.12.came), channel_id=1, source_target_pairs={{0,3},{1,0},{2,1},{3,2},{4,7},{5,4},{6,5},{7,6},{8,11},{9,8},{10,9... | collective-permute-start | bytes 589832 | tf_op jit(solution)/shard_map/ppermute | solution.py:27
  94.1 4.8 %collective-permute-done.15.refs_3_ = bf16[256,384]{1,0:T(8,128)(2,1)} collective-permute-done((bf16[256,384]{1,0:T(8,128)(2,1)S(1)}, bf16[256,384]{1,0:T(8,128)(2,1)}, u32[]{:S(2)}, u32[]{:S(2)}) %collective-permute-start.15) | collective-permute-done | bytes 196640 | tf_op jit(solution)/shard_map/ppermute | solution.py:27
  98.9 4.0 %first_product.1.refs_1_ = f32[768,384]{1,0:T(8,128)} custom-call(bf16[768,256]{1,0:T(8,128)(2,1)} %get-tuple-element.24.held, bf16[768,768]{1,0:T(8,128)(2,1)} %assemble.1.rest, bf16[768,256]{1,0:T(8,128)(2,1)} %collective-permute-done.8.paired_held, bf16[256,384]{1,0:T(8,128)(2,1)} %copy-done.11, bf16[256,384]{1,0:T(8,128)(2,1)} %copy-done.6, ...), custom_call_target="tpu_custom_call" | custom-call | tf_op jit(solution)/shard_map/first_product/pallas_call | solution.py:275
  102.9 2.0 %collective-permute-done.19.refs_5_ = bf16[256,384]{1,0:T(8,128)(2,1)} collective-permute-done((bf16[256,384]{1,0:T(8,128)(2,1)S(1)}, bf16[256,384]{1,0:T(8,128)(2,1)}, u32[]{:S(2)}, u32[]{:S(2)}) %collective-permute-start.19) | collective-permute-done | bytes 196640 | tf_op jit(solution)/shard_map/ppermute | solution.py:27
  104.9 3.4 %second_product.1 = (f32[96,384]{1,0:T(8,128)}, bf16[96,384]{1,0:T(8,128)(2,1)}, bf16[96,384]{1,0:T(8,128)(2,1)}, bf16[96,384]{1,0:T(8,128)(2,1)}, bf16[96,384]{...) custom-call(s32[69]{0:T(128)} %concatenate.3.refs_0_.ids, ...), custom_call_target="tpu_custom_call" | custom-call | tf_op jit(solution)/shard_map/second_product/pallas_call | solution.py:304
  109.1 6.5 %collective-permute-start.21 = (bf16[96,384]{1,0:T(8,128)(2,1)}, bf16[96,384]{1,0:T(8,128)(2,1)S(1)}, u32[]{:S(2)}, u32[]{:S(2)}) collective-permute-start(bf16[96,384]{1,0:T(8,128)(2,1)} %get-tuple-element.32), channel_id=1, source_target_pairs={{0,96},{32,128},{64,160},{96,192},{128,224},{160,0},{192,32},{224,... | collective-permute-start | bytes 221192 | tf_op jit(solution)/shard_map/ppermute | solution.py:27
  115.6 2.0 %collective-permute-start.23 = (bf16[96,384]{1,0:T(8,128)(2,1)}, bf16[96,384]{1,0:T(8,128)(2,1)S(1)}, u32[]{:S(2)}, u32[]{:S(2)}) collective-permute-start(bf16[96,384]{1,0:T(8,128)(2,1)} %get-tuple-element.34), channel_id=1, source_target_pairs={{0,224},{32,0},{64,32},{96,64},{128,96},{160,128},{192,160},{224,1... | collective-permute-start | bytes 221192 | tf_op jit(solution)/shard_map/ppermute | solution.py:27
  118.2 4.4 %collective-permute-start.25 = (bf16[96,384]{1,0:T(8,128)(2,1)}, bf16[96,384]{1,0:T(8,128)(2,1)S(1)}, u32[]{:S(2)}, u32[]{:S(2)}) collective-permute-start(bf16[96,384]{1,0:T(8,128)(2,1)} %get-tuple-element.37), channel_id=1, source_target_pairs={{0,128},{32,160},{64,192},{96,224},{128,0},{160,32},{192,64},{224,... | collective-permute-start | bytes 221192 | tf_op jit(solution)/shard_map/ppermute | solution.py:27
  122.6 3.7 %collective-permute-start.26 = (bf16[96,384]{1,0:T(8,128)(2,1)}, bf16[96,384]{1,0:T(8,128)(2,1)S(1)}, u32[]{:S(2)}, u32[]{:S(2)}) collective-permute-start(bf16[96,384]{1,0:T(8,128)(2,1)} %get-tuple-element.38), channel_id=1, source_target_pairs={{0,192},{32,224},{64,0},{96,32},{128,64},{160,96},{192,128},{224,1... | collective-permute-start | bytes 221192 | tf_op jit(solution)/shard_map/ppermute | solution.py:27
  126.3 1.8 %collective-permute-done.25 = bf16[96,384]{1,0:T(8,128)(2,1)S(1)} collective-permute-done((bf16[96,384]{1,0:T(8,128)(2,1)}, bf16[96,384]{1,0:T(8,128)(2,1)S(1)}, u32[]{:S(2)}, u32[]{:S(2)}) %collective-permute-start.25) | collective-permute-done | bytes 73760 | tf_op jit(solution)/shard_map/ppermute | solution.py:27
  128.1 2.6 %collective-permute-done.26 = bf16[96,384]{1,0:T(8,128)(2,1)S(1)} collective-permute-done((bf16[96,384]{1,0:T(8,128)(2,1)}, bf16[96,384]{1,0:T(8,128)(2,1)S(1)}, u32[]{:S(2)}, u32[]{:S(2)}) %collective-permute-start.26) | collective-permute-done | bytes 73760 | tf_op jit(solution)/shard_map/ppermute | solution.py:27
  133.8 2.7 %unpack.1 = (bf16[128,3072]{1,0:T(8,128)(2,1)}, bf16[128,3072]{1,0:T(8,128)(2,1)}) custom-call(bf16[8,2,128,384]{3,2,1,0:T(8,128)(2,1)} %copy-done), custom_call_target="tpu_custom_call" | custom-call | tf_op jit(solution)/shard_map/unpack/pallas_call | solution.py:62
  (79 shorter events, 17.6 us)
Async XLA Ops:
  3.0 42.6 %all-to-all-start = ((bf16[8,2,128,384]{3,2,1,0:T(8,128)(2,1)}), bf16[8,2,128,384]{3,2,1,0:T(8,128)(2,1)S(1)}, u32[]{:S(2)}, u32[]{:S(2)}) async-start(bf16[8,2,128,384]{3,2,1,0:T(8,128)(2,1)} %pack.1), calls=%async_computation | async-start | bytes 3145728 | tf_op jit(solution)/shard_map/all_to_all | solution.py:326
  13.4 9.6 %collective-permute-start.4 = (bf16[768,256]{1,0:T(8,128)(2,1)}, bf16[768,256]{1,0:T(8,128)(2,1)S(1)}, u32[]{:S(2)}, u32[]{:S(2)}) collective-permute-start(bf16[768,256]{1,0:T(8,128)(2,1)} %get-tuple-element.25), channel_id=1, source_target_pairs={{0,1},{1,2},{2,3},{3,0},{4,7},{5,4},{6,5},{7,6},{8,9},{9,10},{10,1... | collective-permute-start | bytes 1179656 | tf_op jit(solution)/shard_map/ppermute | solution.py:373
  19.1 26.5 %copy-start.10 = (bf16[256,768]{1,0:T(8,128)(2,1)}, bf16[256,768]{1,0:T(8,128)(2,1)S(1)}, u32[]{:S(2)}) copy-start(bf16[256,768]{1,0:T(8,128)(2,1)S(1)} %convolution_convert_fusion.refs_2_) | copy-start | bytes 1179652
  19.1 12.1 %collective-permute-start = (bf16[256,768]{1,0:T(8,128)(2,1)S(1)}, bf16[256,768]{1,0:T(8,128)(2,1)S(1)}, u32[]{:S(2)}, u32[]{:S(2)}) collective-permute-start(bf16[256,768]{1,0:T(8,128)(2,1)S(1)} %convolution_convert_fusion.refs_2_), channel_id=1, source_target_pairs={{0,1},{1,2},{2,3},{3,0},{4,5},{5,6},{6,7},{7,4},{8,9},{9,10},{10,1... | collective-permute-start | bytes 1179656 | tf_op jit(solution)/shard_map/ppermute | solution.py:27
  19.9 17.4 %collective-permute-start.1 = (bf16[256,768]{1,0:T(8,128)(2,1)S(1)}, bf16[256,768]{1,0:T(8,128)(2,1)S(1)}, u32[]{:S(2)}, u32[]{:S(2)}) collective-permute-start(bf16[256,768]{1,0:T(8,128)(2,1)S(1)} %convolution_convert_fusion.refs_2_), channel_id=1, source_target_pairs={{0,3},{1,0},{2,1},{3,2},{4,7},{5,4},{6,5},{7,6},{8,11},{9,8},{10,9... | collective-permute-start | bytes 1179656 | tf_op jit(solution)/shard_map/ppermute | solution.py:27
  21.3 16.1 %collective-permute-start.5 = (bf16[384,256]{1,0:T(8,128)(2,1)S(1)}, bf16[384,256]{1,0:T(8,128)(2,1)}, u32[]{:S(2)}, u32[]{:S(2)}) collective-permute-start(bf16[384,256]{1,0:T(8,128)(2,1)S(1)} %copy-done.16), channel_id=1, source_target_pairs={{0,2},{1,3},{2,0},{3,1},{4,6},{5,7},{6,4},{7,5},{8,10},{9,11},{10,... | collective-permute-start | bytes 589832 | tf_op jit(solution)/shard_map/ppermute | solution.py:27
  23.0 39.3 %copy-start.8 = (bf16[768,256]{1,0:T(8,128)(2,1)}, bf16[768,256]{1,0:T(8,128)(2,1)S(1)}, u32[]{:S(2)}) copy-start(bf16[768,256]{1,0:T(8,128)(2,1)S(1)} %collective-permute-done.4.near) | copy-start | bytes 1179652
  23.0 39.3 %collective-permute-start.6 = (bf16[768,256]{1,0:T(8,128)(2,1)S(1)}, bf16[768,256]{1,0:T(8,128)(2,1)S(1)}, u32[]{:S(2)}, u32[]{:S(2)}) collective-permute-start(bf16[768,256]{1,0:T(8,128)(2,1)S(1)} %collective-permute-done.4.near), channel_id=1, source_target_pairs={{0,4},{4,0},{8,12},{12,8},{16,20},{20,16},{24,28},{28,24},{1,5},{5... | collective-permute-start | bytes 1179656 | tf_op jit(solution)/shard_map/ppermute | solution.py:382
  31.2 10.3 %collective-permute-start.2 = (bf16[128,768]{1,0:T(8,128)(2,1)S(1)}, bf16[128,768]{1,0:T(8,128)(2,1)S(1)}, u32[]{:S(2)}, u32[]{:S(2)}) collective-permute-start(bf16[128,768]{1,0:T(8,128)(2,1)S(1)} %slice.16), channel_id=1, source_target_pairs={{0,1},{1,2},{2,3},{3,0},{4,5},{5,6},{6,7},{7,4},{8,9},{9,10},{10,1... | collective-permute-start | bytes 589832 | tf_op jit(solution)/shard_map/ppermute | solution.py:27
  37.3 8.3 %collective-permute-start.3 = (bf16[128,768]{1,0:T(8,128)(2,1)S(1)}, bf16[128,768]{1,0:T(8,128)(2,1)}, u32[]{:S(2)}, u32[]{:S(2)}) collective-permute-start(bf16[128,768]{1,0:T(8,128)(2,1)S(1)} %slice.17), channel_id=1, source_target_pairs={{0,3},{1,0},{2,1},{3,2},{4,7},{5,4},{6,5},{7,6},{8,11},{9,8},{10,9... | collective-permute-start | bytes 589832 | tf_op jit(solution)/shard_map/ppermute | solution.py:27
  37.4 24.8 %collective-permute-start.7 = (bf16[384,256]{1,0:T(8,128)(2,1)}, bf16[384,256]{1,0:T(8,128)(2,1)}, u32[]{:S(2)}, u32[]{:S(2)}) collective-permute-start(bf16[384,256]{1,0:T(8,128)(2,1)} %collective-permute-done.5.far), channel_id=1, source_target_pairs={{0,4},{4,0},{8,12},{12,8},{16,20},{20,16},{24,28},{28,24},{1,5},{5... | collective-permute-start | bytes 589832 | tf_op jit(solution)/shard_map/ppermute | solution.py:383
  58.6 15.6 %collective-permute-start.10 = (bf16[256,768]{1,0:T(8,128)(2,1)}, bf16[256,768]{1,0:T(8,128)(2,1)}, u32[]{:S(2)}, u32[]{:S(2)}) collective-permute-start(bf16[256,768]{1,0:T(8,128)(2,1)} %get-tuple-element.29), channel_id=1, source_target_pairs={{0,2},{1,3},{2,0},{3,1},{4,6},{5,7},{6,4},{7,5},{8,10},{9,11},{10,... | collective-permute-start | bytes 1179656 | tf_op jit(solution)/shard_map/ppermute | solution.py:27
  58.9 20.3 %collective-permute-start.11 = (bf16[256,768]{1,0:T(8,128)(2,1)}, bf16[256,768]{1,0:T(8,128)(2,1)}, u32[]{:S(2)}, u32[]{:S(2)}) collective-permute-start(bf16[256,768]{1,0:T(8,128)(2,1)} %get-tuple-element.30), channel_id=1, source_target_pairs={{0,3},{1,0},{2,1},{3,2},{4,7},{5,4},{6,5},{7,6},{8,11},{9,8},{10,9... | collective-permute-start | bytes 1179656 | tf_op jit(solution)/shard_map/ppermute | solution.py:27
  60.1 19.1 %collective-permute-start.9 = (bf16[256,768]{1,0:T(8,128)(2,1)}, bf16[256,768]{1,0:T(8,128)(2,1)}, u32[]{:S(2)}, u32[]{:S(2)}) collective-permute-start(bf16[256,768]{1,0:T(8,128)(2,1)} %get-tuple-element.28), channel_id=1, source_target_pairs={{0,1},{1,2},{2,3},{3,0},{4,5},{5,6},{6,7},{7,4},{8,9},{9,10},{10,1... | collective-permute-start | bytes 1179656 | tf_op jit(solution)/shard_map/ppermute | solution.py:27
  65.4 37.5 %collective-permute-start.16 = (bf16[768,768]{1,0:T(8,128)(2,1)}, bf16[768,768]{1,0:T(8,128)(2,1)S(1)}, u32[]{:S(2)}, u32[]{:S(2)}) collective-permute-start(bf16[768,768]{1,0:T(8,128)(2,1)} %assemble.1.rest), channel_id=1, source_target_pairs={{0,32},{4,228},{8,40},{12,236},{16,48},{20,244},{24,56},{28,252},{... | collective-permute-start | bytes 3538952 | tf_op jit(solution)/shard_map/ppermute | solution.py:385
  67.3 18.8 %collective-permute-start.8 = (bf16[768,256]{1,0:T(8,128)(2,1)}, bf16[768,256]{1,0:T(8,128)(2,1)}, u32[]{:S(2)}, u32[]{:S(2)}) collective-permute-start(bf16[768,256]{1,0:T(8,128)(2,1)} %get-tuple-element.24.held), channel_id=1, source_target_pairs={{0,32},{4,228},{8,40},{12,236},{16,48},{20,244},{24,56},{28,252},{... | collective-permute-start | bytes 1179656 | tf_op jit(solution)/shard_map/ppermute | solution.py:375
  67.4 65.2 %all-to-all-start.1 = ((bf16[8,2,128,384]{3,2,1,0:T(8,128)(2,1)}), bf16[8,2,128,384]{3,2,1,0:T(8,128)(2,1)S(1)}, u32[]{:S(2)}, u32[]{:S(2)}) async-start(bf16[8,2,128,384]{3,2,1,0:T(8,128)(2,1)} %get-tuple-element.21), calls=%async_computation.1 | async-start | bytes 3145728 | tf_op jit(solution)/shard_map/all_to_all | solution.py:326
  80.7 18.2 %copy-start.6 = (bf16[256,384]{1,0:T(8,128)(2,1)}, bf16[256,384]{1,0:T(8,128)(2,1)S(1)}, u32[]{:S(2)}) copy-start(bf16[256,384]{1,0:T(8,128)(2,1)S(1)} %get-tuple-element.47.refs_0_) | copy-start | bytes 589828
  80.7 7.4 %collective-permute-start.12 = (bf16[256,384]{1,0:T(8,128)(2,1)S(1)}, bf16[256,384]{1,0:T(8,128)(2,1)S(1)}, u32[]{:S(2)}, u32[]{:S(2)}) collective-permute-start(bf16[256,384]{1,0:T(8,128)(2,1)S(1)} %get-tuple-element.48), channel_id=1, source_target_pairs={{0,32},{4,228},{8,40},{12,236},{16,48},{20,244},{24,56},{28,252},{... | collective-permute-start | bytes 589832 | tf_op jit(solution)/shard_map/ppermute | solution.py:388
  82.7 6.7 %collective-permute-start.13 = (bf16[256,384]{1,0:T(8,128)(2,1)S(1)}, bf16[256,384]{1,0:T(8,128)(2,1)S(1)}, u32[]{:S(2)}, u32[]{:S(2)}) collective-permute-start(bf16[256,384]{1,0:T(8,128)(2,1)S(1)} %get-tuple-element.47.refs_0_), channel_id=1, source_target_pairs={{0,1},{1,2},{2,3},{3,0},{4,5},{5,6},{6,7},{7,4},{8,9},{9,10},{10,1... | collective-permute-start | bytes 589832 | tf_op jit(solution)/shard_map/ppermute | solution.py:27
  83.5 7.2 %collective-permute-start.14 = (bf16[256,384]{1,0:T(8,128)(2,1)S(1)}, bf16[256,384]{1,0:T(8,128)(2,1)S(1)}, u32[]{:S(2)}, u32[]{:S(2)}) collective-permute-start(bf16[256,384]{1,0:T(8,128)(2,1)S(1)} %get-tuple-element.47.refs_0_), channel_id=1, source_target_pairs={{0,2},{1,3},{2,0},{3,1},{4,6},{5,7},{6,4},{7,5},{8,10},{9,11},{10,... | collective-permute-start | bytes 589832 | tf_op jit(solution)/shard_map/ppermute | solution.py:27
  86.1 12.8 %collective-permute-start.15 = (bf16[256,384]{1,0:T(8,128)(2,1)S(1)}, bf16[256,384]{1,0:T(8,128)(2,1)}, u32[]{:S(2)}, u32[]{:S(2)}) collective-permute-start(bf16[256,384]{1,0:T(8,128)(2,1)S(1)} %get-tuple-element.47.refs_0_), channel_id=1, source_target_pairs={{0,3},{1,0},{2,1},{3,2},{4,7},{5,4},{6,5},{7,6},{8,11},{9,8},{10,9... | collective-permute-start | bytes 589832 | tf_op jit(solution)/shard_map/ppermute | solution.py:27
  88.1 14.8 %collective-permute-start.17 = (bf16[256,384]{1,0:T(8,128)(2,1)S(1)}, bf16[256,384]{1,0:T(8,128)(2,1)}, u32[]{:S(2)}, u32[]{:S(2)}) collective-permute-start(bf16[256,384]{1,0:T(8,128)(2,1)S(1)} %collective-permute-done.12.came), channel_id=1, source_target_pairs={{0,1},{1,2},{2,3},{3,0},{4,5},{5,6},{6,7},{7,4},{8,9},{9,10},{10,1... | collective-permute-start | bytes 589832 | tf_op jit(solution)/shard_map/ppermute | solution.py:27
  89.4 13.5 %collective-permute-start.18 = (bf16[256,384]{1,0:T(8,128)(2,1)S(1)}, bf16[256,384]{1,0:T(8,128)(2,1)}, u32[]{:S(2)}, u32[]{:S(2)}) collective-permute-start(bf16[256,384]{1,0:T(8,128)(2,1)S(1)} %collective-permute-done.12.came), channel_id=1, source_target_pairs={{0,2},{1,3},{2,0},{3,1},{4,6},{5,7},{6,4},{7,5},{8,10},{9,11},{10,... | collective-permute-start | bytes 589832 | tf_op jit(solution)/shard_map/ppermute | solution.py:27
  90.7 14.2 %collective-permute-start.19 = (bf16[256,384]{1,0:T(8,128)(2,1)S(1)}, bf16[256,384]{1,0:T(8,128)(2,1)}, u32[]{:S(2)}, u32[]{:S(2)}) collective-permute-start(bf16[256,384]{1,0:T(8,128)(2,1)S(1)} %collective-permute-done.12.came), channel_id=1, source_target_pairs={{0,3},{1,0},{2,1},{3,2},{4,7},{5,4},{6,5},{7,6},{8,11},{9,8},{10,9... | collective-permute-start | bytes 589832 | tf_op jit(solution)/shard_map/ppermute | solution.py:27
  108.3 9.9 %collective-permute-start.20 = (bf16[96,384]{1,0:T(8,128)(2,1)}, bf16[96,384]{1,0:T(8,128)(2,1)S(1)}, u32[]{:S(2)}, u32[]{:S(2)}) collective-permute-start(bf16[96,384]{1,0:T(8,128)(2,1)} %get-tuple-element.31), channel_id=1, source_target_pairs={{0,32},{32,64},{64,96},{96,128},{128,160},{160,192},{192,224},{224... | collective-permute-start | bytes 221192 | tf_op jit(solution)/shard_map/ppermute | solution.py:27
  109.1 13.5 %collective-permute-start.21 = (bf16[96,384]{1,0:T(8,128)(2,1)}, bf16[96,384]{1,0:T(8,128)(2,1)S(1)}, u32[]{:S(2)}, u32[]{:S(2)}) collective-permute-start(bf16[96,384]{1,0:T(8,128)(2,1)} %get-tuple-element.32), channel_id=1, source_target_pairs={{0,96},{32,128},{64,160},{96,192},{128,224},{160,0},{192,32},{224,... | collective-permute-start | bytes 221192 | tf_op jit(solution)/shard_map/ppermute | solution.py:27
  115.6 10.6 %collective-permute-start.22 = (bf16[96,384]{1,0:T(8,128)(2,1)}, bf16[96,384]{1,0:T(8,128)(2,1)S(1)}, u32[]{:S(2)}, u32[]{:S(2)}) collective-permute-start(bf16[96,384]{1,0:T(8,128)(2,1)} %get-tuple-element.33), channel_id=1, source_target_pairs={{0,160},{32,192},{64,224},{96,0},{128,32},{160,64},{192,96},{224,1... | collective-permute-start | bytes 221192 | tf_op jit(solution)/shard_map/ppermute | solution.py:27
  115.6 10.6 %collective-permute-start.23 = (bf16[96,384]{1,0:T(8,128)(2,1)}, bf16[96,384]{1,0:T(8,128)(2,1)S(1)}, u32[]{:S(2)}, u32[]{:S(2)}) collective-permute-start(bf16[96,384]{1,0:T(8,128)(2,1)} %get-tuple-element.34), channel_id=1, source_target_pairs={{0,224},{32,0},{64,32},{96,64},{128,96},{160,128},{192,160},{224,1... | collective-permute-start | bytes 221192 | tf_op jit(solution)/shard_map/ppermute | solution.py:27
  117.6 8.6 %collective-permute-start.24 = (bf16[96,384]{1,0:T(8,128)(2,1)}, bf16[96,384]{1,0:T(8,128)(2,1)S(1)}, u32[]{:S(2)}, u32[]{:S(2)}) collective-permute-start(bf16[96,384]{1,0:T(8,128)(2,1)} %get-tuple-element.36), channel_id=1, source_target_pairs={{0,64},{32,96},{64,128},{96,160},{128,192},{160,224},{192,0},{224,... | collective-permute-start | bytes 221192 | tf_op jit(solution)/shard_map/ppermute | solution.py:27
  118.2 9.9 %collective-permute-start.25 = (bf16[96,384]{1,0:T(8,128)(2,1)}, bf16[96,384]{1,0:T(8,128)(2,1)S(1)}, u32[]{:S(2)}, u32[]{:S(2)}) collective-permute-start(bf16[96,384]{1,0:T(8,128)(2,1)} %get-tuple-element.37), channel_id=1, source_target_pairs={{0,128},{32,160},{64,192},{96,224},{128,0},{160,32},{192,64},{224,... | collective-permute-start | bytes 221192 | tf_op jit(solution)/shard_map/ppermute | solution.py:27
  122.6 8.1 %collective-permute-start.26 = (bf16[96,384]{1,0:T(8,128)(2,1)}, bf16[96,384]{1,0:T(8,128)(2,1)S(1)}, u32[]{:S(2)}, u32[]{:S(2)}) collective-permute-start(bf16[96,384]{1,0:T(8,128)(2,1)} %get-tuple-element.38), channel_id=1, source_target_pairs={{0,192},{32,224},{64,0},{96,32},{128,64},{160,96},{192,128},{224,1... | collective-permute-start | bytes 221192 | tf_op jit(solution)/shard_map/ppermute | solution.py:27
  (14 other events, 80.5 us)

commit v4 on v3

--- a/solution.py
+++ b/solution.py
@@ -151,7 +151,7 @@
         key_index = jnp.where(key_row < KB, first + key_row, second + key_row - KB)
         allowed = key_index < ids[4]
         live = query_lane + index * QB < ids[3]
-        parts = []
+        items = []
         for h in range(heads):
             cols = slice(h * HD, (h + 1) * HD)
             vcols = slice((heads + h) * HD, (heads + h + 1) * HD)
@@ -163,16 +163,24 @@
             value = jnp.concatenate(
                 [table[pl.ds(first, KB), vcols], table[pl.ds(second, KB), vcols]], axis=0
             )
-            scores = dot(key, query, 1, 1)
-            prob_grad = dot(value, grad, 1, 1)
-            scores = jnp.where(allowed, scores, -1e30)
-            scores = scores - jnp.max(scores, axis=0, keepdims=True)
-            weights = jnp.exp2(scores * (SCALING * LOG2_E))
+            items.append((query, grad, key, value))
+        scores = [dot(key, query, 1, 1) for query, _, key, _ in items]
+        prob_grads = [dot(value, grad, 1, 1) for _, grad, _, value in items]
+        return first, second, allowed, live, items, scores, prob_grads
+
+    def rest_of(first, second, allowed, live, items, scores, prob_grads):
+        lows = []
+        for score, prob_grad in zip(scores, prob_grads):
+            score = jnp.where(allowed, score, -1e30)
+            score = score - jnp.max(score, axis=0, keepdims=True)
+            weights = jnp.exp2(score * (SCALING * LOG2_E))
             inverse = 1.0 / jnp.sum(weights, axis=0, keepdims=True)
             probability = weights * jnp.where(live, inverse, 0.0)
-            prob_low = probability.astype(BF16)
             row_dot = jnp.sum(probability * prob_grad, axis=0, keepdims=True)
             score_grad = (probability * (prob_grad - row_dot)).astype(BF16)
+            lows.append((probability.astype(BF16), score_grad))
+        parts = []
+        for (query, grad, key, value), (prob_low, score_grad) in zip(items, lows):
             output = dot(prob_low, value, 0, 0).astype(BF16)
             query_part = (dot(score_grad, key, 0, 0) * SCALING).astype(BF16)
             key_part = dot(score_grad, query, 1, 0) * SCALING
@@ -189,9 +197,10 @@
                 into[pl.ds(first, KB), :] += part[:KB]
                 into[pl.ds(second, KB), :] += part[KB:]
 
-    made = [(k, *one(k)) for k in range(count)]
-    for entry in made:
-        finish(*entry)
+    ready = one(0)
+    for k in range(count):
+        now, ready = ready, one(k + 1) if k + 1 < count else None
+        finish(k, *rest_of(*now))
 
     @pl.when(step == pl.num_programs(0) - 1)
     def _():
@@ -383,8 +392,8 @@
     far_swapped = lax.ppermute(far, "frame", beside)
     rest = assemble(ids, near, far, near_swapped, far_swapped)
     paired_rest = lax.ppermute(rest, ("dp", "frame"), paired)
-    total = total_of(added).astype(BF16)
-    mine, theirs = total[:, :local_width], total[:, local_width:]
+    theirs = total_of([part[:, local_width:] for part in added]).astype(BF16)
+    mine = total_of([part[:, :local_width] for part in added]).astype(BF16)
     came = lax.ppermute(theirs, ("dp", "frame"), paired)
     shares, paired_shares = [mine], [came]
     for k in hops:

time: 137 us -> 134 us (0.978)
  the two profiles are of different devices: /device:TPU:26 before, /device:TPU:1 now
where the time goes in v4:
time: 134 us; the launch traced here: 132 us
  starting transfers between devices  57.8 us (43%)
  waiting for transfers between devices  31.8 us (24%)
  Pallas kernels  25 us (19%)
  local copies, waits for them, and re-layouts  11 us (8%)
  other arithmetic  2.56 us (2%)
  between operations  2.14 us (2%)
  matrix products  1.39 us (1%)
    ppermute x21, waiting for transfers between devices, shifted(): lax.ppermute(array, axis, [(i, (i + by) % count) for i in range(count)])  31.7 us
    ppermute x21, starting transfers between devices, shifted(): lax.ppermute(array, axis, [(i, (i + by) % count) for i in range(count)])  28.4 us
    all_to_all x2, starting transfers between devices, to_owners(): return lax.all_to_all(array, axis, split_axis=0, concat_axis=0, tiled=True)  11.8 us
    unnamed x39, local copies, waits for them, and re-layouts  8.8 us
    pallas_call x1, Pallas kernels, attend(): pl.pallas_call(kernel, grid=(arrived.shape[0] // count,), out_shape=[jax....  6.91 us
    ppermute x1, starting transfers between devices, per_device(): paired_rest = lax.ppermute(rest, ('dp', 'frame'), paired)  5.58 us
    ppermute x1, starting transfers between devices, per_device(): paired_held = lax.ppermute(held, ('dp', 'frame'), paired)  4.09 us
    pallas_call x1, Pallas kernels, first_product(): pl.pallas_call(first_product_kernel, out_shape=jax.ShapeDtypeStruct(shape...  3.98 us
  transfers between devices with their start and end apart: 29, of which 9 were waited for; matrix products, arithmetic and copies ran while one was open for 8% of the time, Pallas kernels for 15%

profile of v4, /device:TPU:1, one launch (start us, length us, event | category | flops | bytes accessed | tf_op | source)
XLA Modules:
  0.0 131.6 jit_solution(5666698749480316358)
XLA Ops:
  0.6 2.4 %pack.1 = bf16[8,2,128,384]{3,2,1,0:T(8,128)(2,1)} custom-call(bf16[128,3072]{1,0:T(8,128)(2,1)} %bitcast.20, bf16[128,3072]{1,0:T(8,128)(2,1)} %bitcast.21), custom_call_target="tpu_custom_call" | custom-call | tf_op jit(solution)/shard_map/pack/pallas_call | solution.py:42
  3.0 6.8 %all-to-all-start = ((bf16[8,2,128,384]{3,2,1,0:T(8,128)(2,1)}), bf16[8,2,128,384]{3,2,1,0:T(8,128)(2,1)S(1)}, u32[]{:S(2)}, u32[]{:S(2)}) async-start(bf16[8,2,128,384]{3,2,1,0:T(8,128)(2,1)} %pack.1), calls=%async_computation | async-start | bytes 3145728 | tf_op jit(solution)/shard_map/all_to_all | solution.py:335
  11.9 3.3 %turn.1 = (bf16[768,256]{1,0:T(8,128)(2,1)}, bf16[768,256]{1,0:T(8,128)(2,1)}, bf16[384,256]{1,0:T(8,128)(2,1)}) custom-call(s32[69]{0:T(128)} %concatenate.3.refs_0_.ids, bf16[256,3072]{1,0:T(8,128)(2,1)} %bitcast.19), custom_call_target="tpu_custom_call" | custom-call | tf_op jit(solution)/shard_map/turn/pallas_call | solution.py:99
  15.2 1.9 %collective-permute-start.4 = (bf16[768,256]{1,0:T(8,128)(2,1)}, bf16[768,256]{1,0:T(8,128)(2,1)S(1)}, u32[]{:S(2)}, u32[]{:S(2)}) collective-permute-start(bf16[768,256]{1,0:T(8,128)(2,1)} %get-tuple-element.25), channel_id=1, source_target_pairs={{0,1},{1,2},{2,3},{3,0},{4,7},{5,4},{6,5},{7,6},{8,9},{9,10},{10,1... | collective-permute-start | bytes 1179656 | tf_op jit(solution)/shard_map/ppermute | solution.py:382
  17.0 3.3 %copy.14 = bf16[384,8,2,384]{3,1,2,0:T(8,128)(2,1)S(1)} copy(bf16[384,8,2,384]{3,2,1,0:T(2,128)(2,1)} %bitcast.17) | data formatting | bytes 9437184
  20.3 1.4 %convolution_convert_fusion.refs_2_ = bf16[256,768]{1,0:T(8,128)(2,1)S(1)} fusion(bf16[3072,768]{1,0:T(8,128)(2,1)S(1)} %bitcast.18, bf16[1,256,3072]{2,1,0:T(8,128)(2,1)S(1)} %copy-done.2), kind=kOutput, calls=%fused_computation | convolution fusion | flops 1208156160 | bytes 6684672 | tf_op jit(solution)/shard_map/dot_general | solution.py:372
  21.8 2.7 %collective-permute-start.1 = (bf16[256,768]{1,0:T(8,128)(2,1)S(1)}, bf16[256,768]{1,0:T(8,128)(2,1)S(1)}, u32[]{:S(2)}, u32[]{:S(2)}) collective-permute-start(bf16[256,768]{1,0:T(8,128)(2,1)S(1)} %convolution_convert_fusion.refs_2_), channel_id=1, source_target_pairs={{0,3},{1,0},{2,1},{3,2},{4,7},{5,4},{6,5},{7,6},{8,11},{9,8},{10,9... | collective-permute-start | bytes 1179656 | tf_op jit(solution)/shard_map/ppermute | solution.py:27
  25.6 10.6 %collective-permute-done.5.far = bf16[384,256]{1,0:T(8,128)(2,1)S(1)} collective-permute-done((bf16[384,256]{1,0:T(8,128)(2,1)S(1)}, bf16[384,256]{1,0:T(8,128)(2,1)S(1)}, u32[]{:S(2)}, u32[]{:S(2)}) %collective-permute-start.5) | collective-permute-done | bytes 196640 | tf_op jit(solution)/shard_map/ppermute | solution.py:27
  36.2 1.7 %collective-permute-start.7 = (bf16[384,256]{1,0:T(8,128)(2,1)S(1)}, bf16[384,256]{1,0:T(8,128)(2,1)S(1)}, u32[]{:S(2)}, u32[]{:S(2)}) collective-permute-start(bf16[384,256]{1,0:T(8,128)(2,1)S(1)} %collective-permute-done.5.far), channel_id=1, source_target_pairs={{0,4},{4,0},{8,12},{12,8},{16,20},{20,16},{24,28},{28,24},{1,5},{5... | collective-permute-start | bytes 589832 | tf_op jit(solution)/shard_map/ppermute | solution.py:392
  38.6 1.5 %collective-permute-start.2 = (bf16[128,768]{1,0:T(8,128)(2,1)}, bf16[128,768]{1,0:T(8,128)(2,1)}, u32[]{:S(2)}, u32[]{:S(2)}) collective-permute-start(bf16[128,768]{1,0:T(8,128)(2,1)} %slice.40), channel_id=1, source_target_pairs={{0,1},{1,2},{2,3},{3,0},{4,5},{5,6},{6,7},{7,4},{8,9},{9,10},{10,1... | collective-permute-start | bytes 589832 | tf_op jit(solution)/shard_map/ppermute | solution.py:27
  43.5 2.4 %assemble.1.rest = bf16[768,768]{1,0:T(8,128)(2,1)} custom-call(s32[69]{0:T(128)} %concatenate.3.refs_0_.ids, bf16[768,256]{1,0:T(8,128)(2,1)} %copy-done.7, bf16[384,256]{1,0:T(8,128)(2,1)} %copy-done.14, bf16[768,256]{1,0:T(8,128)(2,1)} %copy-done.8, bf16[384,256]{1,0:T(8,128)(2,1)} %copy-done.15), custom_call_target="tpu_custom_call" | custom-call | tf_op jit(solution)/shard_map/assemble/pallas_call | solution.py:264
  45.8 5.6 %collective-permute-start.16 = (bf16[768,768]{1,0:T(8,128)(2,1)}, bf16[768,768]{1,0:T(8,128)(2,1)S(1)}, u32[]{:S(2)}, u32[]{:S(2)}) collective-permute-start(bf16[768,768]{1,0:T(8,128)(2,1)} %assemble.1.rest), channel_id=1, source_target_pairs={{0,32},{4,228},{8,40},{12,236},{16,48},{20,244},{24,56},{28,252},{... | collective-permute-start | bytes 3538952 | tf_op jit(solution)/shard_map/ppermute | solution.py:394
  52.6 6.9 %attend.1 = (bf16[8,2,128,384]{3,2,1,0:T(8,128)(2,1)}, f32[256,768]{1,0:T(8,128)}, bf16[256,768]{1,0:T(8,128)(2,1)}, bf16[256,768]{1,0:T(8,128)(2,1)}, bf16[256,768]{1,0:T(8,128)(2,1)}) custom-call(s32[69]{0:T(128)} %concatenate.3.refs_0_.ids, bf16[8,2,128,384]{3,2,1,0:T(8,128)(2,1)} %copy-done.1, bf16[256,768]{1,0:T(8,128)(2,1)} %copy-done.9, ...), custom_call_target="tpu_custom_call" | custom-call | tf_op jit(solution)/shard_map/attend/pallas_call | solution.py:227
  61.9 4.9 %all-to-all-start.1 = ((bf16[8,2,128,384]{3,2,1,0:T(8,128)(2,1)}), bf16[8,2,128,384]{3,2,1,0:T(8,128)(2,1)S(1)}, u32[]{:S(2)}, u32[]{:S(2)}) async-start(bf16[8,2,128,384]{3,2,1,0:T(8,128)(2,1)} %get-tuple-element.21), calls=%async_computation.1 | async-start | bytes 3145728 | tf_op jit(solution)/shard_map/all_to_all | solution.py:335
  66.8 4.1 %collective-permute-start.8 = (bf16[768,256]{1,0:T(8,128)(2,1)}, bf16[768,256]{1,0:T(8,128)(2,1)S(1)}, u32[]{:S(2)}, u32[]{:S(2)}) collective-permute-start(bf16[768,256]{1,0:T(8,128)(2,1)} %get-tuple-element.24.held), channel_id=1, source_target_pairs={{0,32},{4,228},{8,40},{12,236},{16,48},{20,244},{24,56},{28,252},{... | collective-permute-start | bytes 1179656 | tf_op jit(solution)/shard_map/ppermute | solution.py:384
  70.9 1.5 %collective-permute-done.10 = bf16[256,768]{1,0:T(8,128)(2,1)S(1)} collective-permute-done((bf16[256,768]{1,0:T(8,128)(2,1)}, bf16[256,768]{1,0:T(8,128)(2,1)S(1)}, u32[]{:S(2)}, u32[]{:S(2)}) %collective-permute-start.10) | collective-permute-done | bytes 393248 | tf_op jit(solution)/shard_map/ppermute | solution.py:27
  72.5 5.9 %collective-permute-done.11 = bf16[256,768]{1,0:T(8,128)(2,1)} collective-permute-done((bf16[256,768]{1,0:T(8,128)(2,1)}, bf16[256,768]{1,0:T(8,128)(2,1)}, u32[]{:S(2)}, u32[]{:S(2)}) %collective-permute-start.11) | collective-permute-done | bytes 393248 | tf_op jit(solution)/shard_map/ppermute | solution.py:27
  78.4 1.6 %add_convert_fusion = (bf16[256,384]{1,0:T(8,128)(2,1)S(1)}, bf16[256,384]{1,0:T(8,128)(2,1)S(1)}) fusion(f32[256,768]{1,0:T(8,128)} %get-tuple-element.27, bf16[256,768]{1,0:T(8,128)(2,1)} %collective-permute-done.11, bf16[256,768]{1,0:T(8,128)(2,1)S(1)} %collective-permute-done.10, bf16[256,768]{1,0:T(8,128)(2,1)} %collective-permute-done.9), kind=kLoop, calls=%fused_computation.1 | loop fusion | flops 1376256 | bytes 2359296 | tf_op jit(solution)/shard_map/convert_element_type | solution.py:396
  80.0 3.4 %collective-permute-start.12 = (bf16[256,384]{1,0:T(8,128)(2,1)S(1)}, bf16[256,384]{1,0:T(8,128)(2,1)S(1)}, u32[]{:S(2)}, u32[]{:S(2)}) collective-permute-start(bf16[256,384]{1,0:T(8,128)(2,1)S(1)} %get-tuple-element.46), channel_id=1, source_target_pairs={{0,32},{4,228},{8,40},{12,236},{16,48},{20,244},{24,56},{28,252},{... | collective-permute-start | bytes 589832 | tf_op jit(solution)/shard_map/ppermute | solution.py:397
  84.5 3.1 %collective-permute-start.14 = (bf16[256,384]{1,0:T(8,128)(2,1)S(1)}, bf16[256,384]{1,0:T(8,128)(2,1)S(1)}, u32[]{:S(2)}, u32[]{:S(2)}) collective-permute-start(bf16[256,384]{1,0:T(8,128)(2,1)S(1)} %get-tuple-element.45.refs_0_), channel_id=1, source_target_pairs={{0,2},{1,3},{2,0},{3,1},{4,6},{5,7},{6,4},{7,5},{8,10},{9,11},{10,... | collective-permute-start | bytes 589832 | tf_op jit(solution)/shard_map/ppermute | solution.py:27
  89.0 3.5 %collective-permute-done.13.refs_1_ = bf16[256,384]{1,0:T(8,128)(2,1)S(1)} collective-permute-done((bf16[256,384]{1,0:T(8,128)(2,1)S(1)}, bf16[256,384]{1,0:T(8,128)(2,1)S(1)}, u32[]{:S(2)}, u32[]{:S(2)}) %collective-permute-start.13) | collective-permute-done | bytes 196640 | tf_op jit(solution)/shard_map/ppermute | solution.py:27
  92.6 2.0 %collective-permute-start.18 = (bf16[256,384]{1,0:T(8,128)(2,1)S(1)}, bf16[256,384]{1,0:T(8,128)(2,1)}, u32[]{:S(2)}, u32[]{:S(2)}) collective-permute-start(bf16[256,384]{1,0:T(8,128)(2,1)S(1)} %collective-permute-done.12.came), channel_id=1, source_target_pairs={{0,2},{1,3},{2,0},{3,1},{4,6},{5,7},{6,4},{7,5},{8,10},{9,11},{10,... | collective-permute-start | bytes 589832 | tf_op jit(solution)/shard_map/ppermute | solution.py:27
  94.6 2.8 %collective-permute-done.14.refs_2_ = bf16[256,384]{1,0:T(8,128)(2,1)S(1)} collective-permute-done((bf16[256,384]{1,0:T(8,128)(2,1)S(1)}, bf16[256,384]{1,0:T(8,128)(2,1)S(1)}, u32[]{:S(2)}, u32[]{:S(2)}) %collective-permute-start.14) | collective-permute-done | bytes 196640 | tf_op jit(solution)/shard_map/ppermute | solution.py:27
  98.0 4.0 %first_product.1.refs_1_ = f32[768,384]{1,0:T(8,128)} custom-call(bf16[768,256]{1,0:T(8,128)(2,1)} %get-tuple-element.24.held, bf16[768,768]{1,0:T(8,128)(2,1)} %assemble.1.rest, bf16[768,256]{1,0:T(8,128)(2,1)} %copy-done.10, bf16[256,384]{1,0:T(8,128)(2,1)} %copy-done.11, bf16[256,384]{1,0:T(8,128)(2,1)} %copy-done.6, bf16[256,384]{1,0:T(8,128)(2,1)} %copy-done.12, ...), custom_call_target="tpu_custom_call" | custom-call | tf_op jit(solution)/shard_map/first_product/pallas_call | solution.py:284
  103.0 3.4 %second_product.1 = (f32[96,384]{1,0:T(8,128)}, bf16[96,384]{1,0:T(8,128)(2,1)}, bf16[96,384]{1,0:T(8,128)(2,1)}, bf16[96,384]{1,0:T(8,128)(2,1)}, bf16[96,384]{...) custom-call(s32[69]{0:T(128)} %concatenate.3.refs_0_.ids, ...), custom_call_target="tpu_custom_call" | custom-call | tf_op jit(solution)/shard_map/second_product/pallas_call | solution.py:313
  106.5 3.7 %collective-permute-start.21 = (bf16[96,384]{1,0:T(8,128)(2,1)}, bf16[96,384]{1,0:T(8,128)(2,1)S(1)}, u32[]{:S(2)}, u32[]{:S(2)}) collective-permute-start(bf16[96,384]{1,0:T(8,128)(2,1)} %get-tuple-element.32), channel_id=1, source_target_pairs={{0,96},{32,128},{64,160},{96,192},{128,224},{160,0},{192,32},{224,... | collective-permute-start | bytes 221192 | tf_op jit(solution)/shard_map/ppermute | solution.py:27
  111.0 1.7 %collective-permute-start.23 = (bf16[96,384]{1,0:T(8,128)(2,1)}, bf16[96,384]{1,0:T(8,128)(2,1)S(1)}, u32[]{:S(2)}, u32[]{:S(2)}) collective-permute-start(bf16[96,384]{1,0:T(8,128)(2,1)} %get-tuple-element.34), channel_id=1, source_target_pairs={{0,224},{32,0},{64,32},{96,64},{128,96},{160,128},{192,160},{224,1... | collective-permute-start | bytes 221192 | tf_op jit(solution)/shard_map/ppermute | solution.py:27
  112.7 2.1 %collective-permute-start.24 = (bf16[96,384]{1,0:T(8,128)(2,1)}, bf16[96,384]{1,0:T(8,128)(2,1)S(1)}, u32[]{:S(2)}, u32[]{:S(2)}) collective-permute-start(bf16[96,384]{1,0:T(8,128)(2,1)} %get-tuple-element.36), channel_id=1, source_target_pairs={{0,64},{32,96},{64,128},{96,160},{128,192},{160,224},{192,0},{224,... | collective-permute-start | bytes 221192 | tf_op jit(solution)/shard_map/ppermute | solution.py:27
  114.8 2.4 %collective-permute-start.25 = (bf16[96,384]{1,0:T(8,128)(2,1)}, bf16[96,384]{1,0:T(8,128)(2,1)S(1)}, u32[]{:S(2)}, u32[]{:S(2)}) collective-permute-start(bf16[96,384]{1,0:T(8,128)(2,1)} %get-tuple-element.37), channel_id=1, source_target_pairs={{0,128},{32,160},{64,192},{96,224},{128,0},{160,32},{192,64},{224,... | collective-permute-start | bytes 221192 | tf_op jit(solution)/shard_map/ppermute | solution.py:27
  117.2 2.2 %collective-permute-start.26 = (bf16[96,384]{1,0:T(8,128)(2,1)}, bf16[96,384]{1,0:T(8,128)(2,1)S(1)}, u32[]{:S(2)}, u32[]{:S(2)}) collective-permute-start(bf16[96,384]{1,0:T(8,128)(2,1)} %get-tuple-element.38), channel_id=1, source_target_pairs={{0,192},{32,224},{64,0},{96,32},{128,64},{160,96},{192,128},{224,1... | collective-permute-start | bytes 221192 | tf_op jit(solution)/shard_map/ppermute | solution.py:27
  119.4 5.4 %collective-permute-done.25 = bf16[96,384]{1,0:T(8,128)(2,1)S(1)} collective-permute-done((bf16[96,384]{1,0:T(8,128)(2,1)}, bf16[96,384]{1,0:T(8,128)(2,1)S(1)}, u32[]{:S(2)}, u32[]{:S(2)}) %collective-permute-start.25) | collective-permute-done | bytes 73760 | tf_op jit(solution)/shard_map/ppermute | solution.py:27
  128.9 2.7 %unpack.1 = (bf16[128,3072]{1,0:T(8,128)(2,1)}, bf16[128,3072]{1,0:T(8,128)(2,1)}) custom-call(bf16[8,2,128,384]{3,2,1,0:T(8,128)(2,1)} %copy-done), custom_call_target="tpu_custom_call" | custom-call | tf_op jit(solution)/shard_map/unpack/pallas_call | solution.py:62
  (80 shorter events, 18.9 us)
Async XLA Ops:
  3.0 48.4 %all-to-all-start = ((bf16[8,2,128,384]{3,2,1,0:T(8,128)(2,1)}), bf16[8,2,128,384]{3,2,1,0:T(8,128)(2,1)S(1)}, u32[]{:S(2)}, u32[]{:S(2)}) async-start(bf16[8,2,128,384]{3,2,1,0:T(8,128)(2,1)} %pack.1), calls=%async_computation | async-start | bytes 3145728 | tf_op jit(solution)/shard_map/all_to_all | solution.py:335
  15.2 9.3 %collective-permute-start.4 = (bf16[768,256]{1,0:T(8,128)(2,1)}, bf16[768,256]{1,0:T(8,128)(2,1)S(1)}, u32[]{:S(2)}, u32[]{:S(2)}) collective-permute-start(bf16[768,256]{1,0:T(8,128)(2,1)} %get-tuple-element.25), channel_id=1, source_target_pairs={{0,1},{1,2},{2,3},{3,0},{4,7},{5,4},{6,5},{7,6},{8,9},{9,10},{10,1... | collective-permute-start | bytes 1179656 | tf_op jit(solution)/shard_map/ppermute | solution.py:382
  21.7 21.0 %copy-start.9 = (bf16[256,768]{1,0:T(8,128)(2,1)}, bf16[256,768]{1,0:T(8,128)(2,1)S(1)}, u32[]{:S(2)}) copy-start(bf16[256,768]{1,0:T(8,128)(2,1)S(1)} %convolution_convert_fusion.refs_2_) | copy-start | bytes 1179652
  21.7 16.1 %collective-permute-start = (bf16[256,768]{1,0:T(8,128)(2,1)S(1)}, bf16[256,768]{1,0:T(8,128)(2,1)S(1)}, u32[]{:S(2)}, u32[]{:S(2)}) collective-permute-start(bf16[256,768]{1,0:T(8,128)(2,1)S(1)} %convolution_convert_fusion.refs_2_), channel_id=1, source_target_pairs={{0,1},{1,2},{2,3},{3,0},{4,5},{5,6},{6,7},{7,4},{8,9},{9,10},{10,1... | collective-permute-start | bytes 1179656 | tf_op jit(solution)/shard_map/ppermute | solution.py:27
  21.8 18.3 %collective-permute-start.1 = (bf16[256,768]{1,0:T(8,128)(2,1)S(1)}, bf16[256,768]{1,0:T(8,128)(2,1)S(1)}, u32[]{:S(2)}, u32[]{:S(2)}) collective-permute-start(bf16[256,768]{1,0:T(8,128)(2,1)S(1)} %convolution_convert_fusion.refs_2_), channel_id=1, source_target_pairs={{0,3},{1,0},{2,1},{3,2},{4,7},{5,4},{6,5},{7,6},{8,11},{9,8},{10,9... | collective-permute-start | bytes 1179656 | tf_op jit(solution)/shard_map/ppermute | solution.py:27
  24.5 11.7 %collective-permute-start.5 = (bf16[384,256]{1,0:T(8,128)(2,1)S(1)}, bf16[384,256]{1,0:T(8,128)(2,1)S(1)}, u32[]{:S(2)}, u32[]{:S(2)}) collective-permute-start(bf16[384,256]{1,0:T(8,128)(2,1)S(1)} %copy-done.17), channel_id=1, source_target_pairs={{0,2},{1,3},{2,0},{3,1},{4,6},{5,7},{6,4},{7,5},{8,10},{9,11},{10,... | collective-permute-start | bytes 589832 | tf_op jit(solution)/shard_map/ppermute | solution.py:27
  24.5 18.2 %copy-start.7 = (bf16[768,256]{1,0:T(8,128)(2,1)}, bf16[768,256]{1,0:T(8,128)(2,1)S(1)}, u32[]{:S(2)}) copy-start(bf16[768,256]{1,0:T(8,128)(2,1)S(1)} %collective-permute-done.4.near) | copy-start | bytes 1179652
  24.5 18.2 %collective-permute-start.6 = (bf16[768,256]{1,0:T(8,128)(2,1)S(1)}, bf16[768,256]{1,0:T(8,128)(2,1)S(1)}, u32[]{:S(2)}, u32[]{:S(2)}) collective-permute-start(bf16[768,256]{1,0:T(8,128)(2,1)S(1)} %collective-permute-done.4.near), channel_id=1, source_target_pairs={{0,4},{4,0},{8,12},{12,8},{16,20},{20,16},{24,28},{28,24},{1,5},{5... | collective-permute-start | bytes 1179656 | tf_op jit(solution)/shard_map/ppermute | solution.py:391
  36.2 5.9 %collective-permute-start.7 = (bf16[384,256]{1,0:T(8,128)(2,1)S(1)}, bf16[384,256]{1,0:T(8,128)(2,1)S(1)}, u32[]{:S(2)}, u32[]{:S(2)}) collective-permute-start(bf16[384,256]{1,0:T(8,128)(2,1)S(1)} %collective-permute-done.5.far), channel_id=1, source_target_pairs={{0,4},{4,0},{8,12},{12,8},{16,20},{20,16},{24,28},{28,24},{1,5},{5... | collective-permute-start | bytes 589832 | tf_op jit(solution)/shard_map/ppermute | solution.py:392
  38.6 12.8 %collective-permute-start.2 = (bf16[128,768]{1,0:T(8,128)(2,1)}, bf16[128,768]{1,0:T(8,128)(2,1)}, u32[]{:S(2)}, u32[]{:S(2)}) collective-permute-start(bf16[128,768]{1,0:T(8,128)(2,1)} %slice.40), channel_id=1, source_target_pairs={{0,1},{1,2},{2,3},{3,0},{4,5},{5,6},{6,7},{7,4},{8,9},{9,10},{10,1... | collective-permute-start | bytes 589832 | tf_op jit(solution)/shard_map/ppermute | solution.py:27
  40.9 10.6 %collective-permute-start.3 = (bf16[128,768]{1,0:T(8,128)(2,1)}, bf16[128,768]{1,0:T(8,128)(2,1)}, u32[]{:S(2)}, u32[]{:S(2)}) collective-permute-start(bf16[128,768]{1,0:T(8,128)(2,1)} %slice.41), channel_id=1, source_target_pairs={{0,3},{1,0},{2,1},{3,2},{4,7},{5,4},{6,5},{7,6},{8,11},{9,8},{10,9... | collective-permute-start | bytes 589832 | tf_op jit(solution)/shard_map/ppermute | solution.py:27
  45.8 56.2 %collective-permute-start.16 = (bf16[768,768]{1,0:T(8,128)(2,1)}, bf16[768,768]{1,0:T(8,128)(2,1)S(1)}, u32[]{:S(2)}, u32[]{:S(2)}) collective-permute-start(bf16[768,768]{1,0:T(8,128)(2,1)} %assemble.1.rest), channel_id=1, source_target_pairs={{0,32},{4,228},{8,40},{12,236},{16,48},{20,244},{24,56},{28,252},{... | collective-permute-start | bytes 3538952 | tf_op jit(solution)/shard_map/ppermute | solution.py:394
  59.5 13.0 %collective-permute-start.10 = (bf16[256,768]{1,0:T(8,128)(2,1)}, bf16[256,768]{1,0:T(8,128)(2,1)S(1)}, u32[]{:S(2)}, u32[]{:S(2)}) collective-permute-start(bf16[256,768]{1,0:T(8,128)(2,1)} %get-tuple-element.29), channel_id=1, source_target_pairs={{0,2},{1,3},{2,0},{3,1},{4,6},{5,7},{6,4},{7,5},{8,10},{9,11},{10,... | collective-permute-start | bytes 1179656 | tf_op jit(solution)/shard_map/ppermute | solution.py:27
  60.4 18.0 %collective-permute-start.11 = (bf16[256,768]{1,0:T(8,128)(2,1)}, bf16[256,768]{1,0:T(8,128)(2,1)}, u32[]{:S(2)}, u32[]{:S(2)}) collective-permute-start(bf16[256,768]{1,0:T(8,128)(2,1)} %get-tuple-element.30), channel_id=1, source_target_pairs={{0,3},{1,0},{2,1},{3,2},{4,7},{5,4},{6,5},{7,6},{8,11},{9,8},{10,9... | collective-permute-start | bytes 1179656 | tf_op jit(solution)/shard_map/ppermute | solution.py:27
  61.8 16.7 %collective-permute-start.9 = (bf16[256,768]{1,0:T(8,128)(2,1)}, bf16[256,768]{1,0:T(8,128)(2,1)}, u32[]{:S(2)}, u32[]{:S(2)}) collective-permute-start(bf16[256,768]{1,0:T(8,128)(2,1)} %get-tuple-element.28), channel_id=1, source_target_pairs={{0,1},{1,2},{2,3},{3,0},{4,5},{5,6},{6,7},{7,4},{8,9},{9,10},{10,1... | collective-permute-start | bytes 1179656 | tf_op jit(solution)/shard_map/ppermute | solution.py:27
  61.9 65.9 %all-to-all-start.1 = ((bf16[8,2,128,384]{3,2,1,0:T(8,128)(2,1)}), bf16[8,2,128,384]{3,2,1,0:T(8,128)(2,1)S(1)}, u32[]{:S(2)}, u32[]{:S(2)}) async-start(bf16[8,2,128,384]{3,2,1,0:T(8,128)(2,1)} %get-tuple-element.21), calls=%async_computation.1 | async-start | bytes 3145728 | tf_op jit(solution)/shard_map/all_to_all | solution.py:335
  66.8 20.7 %collective-permute-start.8 = (bf16[768,256]{1,0:T(8,128)(2,1)}, bf16[768,256]{1,0:T(8,128)(2,1)S(1)}, u32[]{:S(2)}, u32[]{:S(2)}) collective-permute-start(bf16[768,256]{1,0:T(8,128)(2,1)} %get-tuple-element.24.held), channel_id=1, source_target_pairs={{0,32},{4,228},{8,40},{12,236},{16,48},{20,244},{24,56},{28,252},{... | collective-permute-start | bytes 1179656 | tf_op jit(solution)/shard_map/ppermute | solution.py:384
  80.0 17.4 %copy-start.6 = (bf16[256,384]{1,0:T(8,128)(2,1)}, bf16[256,384]{1,0:T(8,128)(2,1)S(1)}, u32[]{:S(2)}) copy-start(bf16[256,384]{1,0:T(8,128)(2,1)S(1)} %get-tuple-element.45.refs_0_) | copy-start | bytes 589828
  80.0 8.1 %collective-permute-start.12 = (bf16[256,384]{1,0:T(8,128)(2,1)S(1)}, bf16[256,384]{1,0:T(8,128)(2,1)S(1)}, u32[]{:S(2)}, u32[]{:S(2)}) collective-permute-start(bf16[256,384]{1,0:T(8,128)(2,1)S(1)} %get-tuple-element.46), channel_id=1, source_target_pairs={{0,32},{4,228},{8,40},{12,236},{16,48},{20,244},{24,56},{28,252},{... | collective-permute-start | bytes 589832 | tf_op jit(solution)/shard_map/ppermute | solution.py:397
  83.4 9.2 %collective-permute-start.13 = (bf16[256,384]{1,0:T(8,128)(2,1)S(1)}, bf16[256,384]{1,0:T(8,128)(2,1)S(1)}, u32[]{:S(2)}, u32[]{:S(2)}) collective-permute-start(bf16[256,384]{1,0:T(8,128)(2,1)S(1)} %get-tuple-element.45.refs_0_), channel_id=1, source_target_pairs={{0,1},{1,2},{2,3},{3,0},{4,5},{5,6},{6,7},{7,4},{8,9},{9,10},{10,1... | collective-permute-start | bytes 589832 | tf_op jit(solution)/shard_map/ppermute | solution.py:27
  84.5 12.9 %collective-permute-start.14 = (bf16[256,384]{1,0:T(8,128)(2,1)S(1)}, bf16[256,384]{1,0:T(8,128)(2,1)S(1)}, u32[]{:S(2)}, u32[]{:S(2)}) collective-permute-start(bf16[256,384]{1,0:T(8,128)(2,1)S(1)} %get-tuple-element.45.refs_0_), channel_id=1, source_target_pairs={{0,2},{1,3},{2,0},{3,1},{4,6},{5,7},{6,4},{7,5},{8,10},{9,11},{10,... | collective-permute-start | bytes 589832 | tf_op jit(solution)/shard_map/ppermute | solution.py:27
  87.6 9.8 %collective-permute-start.15 = (bf16[256,384]{1,0:T(8,128)(2,1)S(1)}, bf16[256,384]{1,0:T(8,128)(2,1)}, u32[]{:S(2)}, u32[]{:S(2)}) collective-permute-start(bf16[256,384]{1,0:T(8,128)(2,1)S(1)} %get-tuple-element.45.refs_0_), channel_id=1, source_target_pairs={{0,3},{1,0},{2,1},{3,2},{4,7},{5,4},{6,5},{7,6},{8,11},{9,8},{10,9... | collective-permute-start | bytes 589832 | tf_op jit(solution)/shard_map/ppermute | solution.py:27
  88.1 13.9 %collective-permute-start.17 = (bf16[256,384]{1,0:T(8,128)(2,1)S(1)}, bf16[256,384]{1,0:T(8,128)(2,1)}, u32[]{:S(2)}, u32[]{:S(2)}) collective-permute-start(bf16[256,384]{1,0:T(8,128)(2,1)S(1)} %collective-permute-done.12.came), channel_id=1, source_target_pairs={{0,1},{1,2},{2,3},{3,0},{4,5},{5,6},{6,7},{7,4},{8,9},{9,10},{10,1... | collective-permute-start | bytes 589832 | tf_op jit(solution)/shard_map/ppermute | solution.py:27
  92.6 10.2 %collective-permute-start.18 = (bf16[256,384]{1,0:T(8,128)(2,1)S(1)}, bf16[256,384]{1,0:T(8,128)(2,1)}, u32[]{:S(2)}, u32[]{:S(2)}) collective-permute-start(bf16[256,384]{1,0:T(8,128)(2,1)S(1)} %collective-permute-done.12.came), channel_id=1, source_target_pairs={{0,2},{1,3},{2,0},{3,1},{4,6},{5,7},{6,4},{7,5},{8,10},{9,11},{10,... | collective-permute-start | bytes 589832 | tf_op jit(solution)/shard_map/ppermute | solution.py:27
  97.4 5.5 %collective-permute-start.19 = (bf16[256,384]{1,0:T(8,128)(2,1)S(1)}, bf16[256,384]{1,0:T(8,128)(2,1)}, u32[]{:S(2)}, u32[]{:S(2)}) collective-permute-start(bf16[256,384]{1,0:T(8,128)(2,1)S(1)} %collective-permute-done.12.came), channel_id=1, source_target_pairs={{0,3},{1,0},{2,1},{3,2},{4,7},{5,4},{6,5},{7,6},{8,11},{9,8},{10,9... | collective-permute-start | bytes 589832 | tf_op jit(solution)/shard_map/ppermute | solution.py:27
  106.4 8.3 %collective-permute-start.20 = (bf16[96,384]{1,0:T(8,128)(2,1)}, bf16[96,384]{1,0:T(8,128)(2,1)S(1)}, u32[]{:S(2)}, u32[]{:S(2)}) collective-permute-start(bf16[96,384]{1,0:T(8,128)(2,1)} %get-tuple-element.31), channel_id=1, source_target_pairs={{0,32},{32,64},{64,96},{96,128},{128,160},{160,192},{192,224},{224... | collective-permute-start | bytes 221192 | tf_op jit(solution)/shard_map/ppermute | solution.py:27
  106.5 10.7 %collective-permute-start.21 = (bf16[96,384]{1,0:T(8,128)(2,1)}, bf16[96,384]{1,0:T(8,128)(2,1)S(1)}, u32[]{:S(2)}, u32[]{:S(2)}) collective-permute-start(bf16[96,384]{1,0:T(8,128)(2,1)} %get-tuple-element.32), channel_id=1, source_target_pairs={{0,96},{32,128},{64,160},{96,192},{128,224},{160,0},{192,32},{224,... | collective-permute-start | bytes 221192 | tf_op jit(solution)/shard_map/ppermute | solution.py:27
  110.1 9.2 %collective-permute-start.22 = (bf16[96,384]{1,0:T(8,128)(2,1)}, bf16[96,384]{1,0:T(8,128)(2,1)S(1)}, u32[]{:S(2)}, u32[]{:S(2)}) collective-permute-start(bf16[96,384]{1,0:T(8,128)(2,1)} %get-tuple-element.33), channel_id=1, source_target_pairs={{0,160},{32,192},{64,224},{96,0},{128,32},{160,64},{192,96},{224,1... | collective-permute-start | bytes 221192 | tf_op jit(solution)/shard_map/ppermute | solution.py:27
  111.0 8.4 %collective-permute-start.23 = (bf16[96,384]{1,0:T(8,128)(2,1)}, bf16[96,384]{1,0:T(8,128)(2,1)S(1)}, u32[]{:S(2)}, u32[]{:S(2)}) collective-permute-start(bf16[96,384]{1,0:T(8,128)(2,1)} %get-tuple-element.34), channel_id=1, source_target_pairs={{0,224},{32,0},{64,32},{96,64},{128,96},{160,128},{192,160},{224,1... | collective-permute-start | bytes 221192 | tf_op jit(solution)/shard_map/ppermute | solution.py:27
  112.7 6.7 %collective-permute-start.24 = (bf16[96,384]{1,0:T(8,128)(2,1)}, bf16[96,384]{1,0:T(8,128)(2,1)S(1)}, u32[]{:S(2)}, u32[]{:S(2)}) collective-permute-start(bf16[96,384]{1,0:T(8,128)(2,1)} %get-tuple-element.36), channel_id=1, source_target_pairs={{0,64},{32,96},{64,128},{96,160},{128,192},{160,224},{192,0},{224,... | collective-permute-start | bytes 221192 | tf_op jit(solution)/shard_map/ppermute | solution.py:27
  114.8 10.0 %collective-permute-start.25 = (bf16[96,384]{1,0:T(8,128)(2,1)}, bf16[96,384]{1,0:T(8,128)(2,1)S(1)}, u32[]{:S(2)}, u32[]{:S(2)}) collective-permute-start(bf16[96,384]{1,0:T(8,128)(2,1)} %get-tuple-element.37), channel_id=1, source_target_pairs={{0,128},{32,160},{64,192},{96,224},{128,0},{160,32},{192,64},{224,... | collective-permute-start | bytes 221192 | tf_op jit(solution)/shard_map/ppermute | solution.py:27
  117.2 8.6 %collective-permute-start.26 = (bf16[96,384]{1,0:T(8,128)(2,1)}, bf16[96,384]{1,0:T(8,128)(2,1)S(1)}, u32[]{:S(2)}, u32[]{:S(2)}) collective-permute-start(bf16[96,384]{1,0:T(8,128)(2,1)} %get-tuple-element.38), channel_id=1, source_target_pairs={{0,192},{32,224},{64,0},{96,32},{128,64},{160,96},{192,128},{224,1... | collective-permute-start | bytes 221192 | tf_op jit(solution)/shard_map/ppermute | solution.py:27
  (15 other events, 68.9 us)

commit v5 on v4

--- a/solution.py
+++ b/solution.py
@@ -383,6 +383,7 @@
     far = shifted(far, "audio", 2)
     paired_held = lax.ppermute(held, ("dp", "frame"), paired)
 
+    arrived = pltpu.with_memory_space_constraint(arrived, pltpu.VMEM)
     results, grads = attend(ids, arrived, tables, audio_count)
     added = [grads[0]]
     for k in hops:
@@ -400,6 +401,10 @@
         shares.append(shifted(mine, "audio", k))
     for k in hops:
         paired_shares.append(shifted(came, "audio", k))
+    near_by = lambda arrays: [
+        pltpu.with_memory_space_constraint(array, pltpu.VMEM) for array in arrays
+    ]
+    shares[1:], paired_shares[1:] = near_by(shares[1:]), near_by(paired_shares[1:])
     so_far = first_product(held, rest, paired_held, came, shares)
     pieces = second_product(
         ids, so_far, paired_rest, paired_shares[1:], clips, 1.0 / clips

time: 134 us -> 132 us (0.985)
  local copies, waits for them, and re-layouts: 11 us -> 9.19 us
    unnamed x39 -> x33, local copies, waits for them, and re-layouts: 8.8 us -> 6.96 us
where the time goes in v5:
time: 132 us; the launch traced here: 130 us
  starting transfers between devices  58.1 us (44%)
  waiting for transfers between devices  32.3 us (24%)
  Pallas kernels  24.3 us (18%)
  local copies, waits for them, and re-layouts  9.19 us (7%)
  other arithmetic  2.21 us (2%)
  between operations  2.11 us (2%)
  matrix products  1.39 us (1%)
    ppermute x21, waiting for transfers between devices, shifted(): lax.ppermute(array, axis, [(i, (i + by) % count) for i in range(count)])  32.3 us
    ppermute x21, starting transfers between devices, shifted(): lax.ppermute(array, axis, [(i, (i + by) % count) for i in range(count)])  28.6 us
    all_to_all x2, starting transfers between devices, to_owners(): return lax.all_to_all(array, axis, split_axis=0, concat_axis=0, tiled=True)  11.9 us
    unnamed x33, local copies, waits for them, and re-layouts  6.96 us
    pallas_call x1, Pallas kernels, attend(): pl.pallas_call(kernel, grid=(arrived.shape[0] // count,), out_shape=[jax....  6.43 us
    ppermute x1, starting transfers between devices, per_device(): paired_rest = lax.ppermute(rest, ('dp', 'frame'), paired)  5.58 us
    ppermute x1, starting transfers between devices, per_device(): paired_held = lax.ppermute(held, ('dp', 'frame'), paired)  4.09 us
    pallas_call x1, Pallas kernels, first_product(): pl.pallas_call(first_product_kernel, out_shape=jax.ShapeDtypeStruct(shape...  3.84 us
  transfers between devices with their start and end apart: 29, of which 9 were waited for; matrix products, arithmetic and copies ran while one was open for 8% of the time, Pallas kernels for 15%

profile of v5, /device:TPU:1, one launch (start us, length us, event | category | flops | bytes accessed | tf_op | source)
XLA Modules:
  0.0 129.6 jit_solution(12116355520346471355)
XLA Ops:
  0.6 2.4 %pack.1 = bf16[8,2,128,384]{3,2,1,0:T(8,128)(2,1)} custom-call(bf16[128,3072]{1,0:T(8,128)(2,1)} %bitcast.20, bf16[128,3072]{1,0:T(8,128)(2,1)} %bitcast.21), custom_call_target="tpu_custom_call" | custom-call | tf_op jit(solution)/shard_map/pack/pallas_call | solution.py:42
  3.0 6.8 %all-to-all-start = ((bf16[8,2,128,384]{3,2,1,0:T(8,128)(2,1)}), bf16[8,2,128,384]{3,2,1,0:T(8,128)(2,1)S(1)}, u32[]{:S(2)}, u32[]{:S(2)}) async-start(bf16[8,2,128,384]{3,2,1,0:T(8,128)(2,1)} %pack.1), calls=%async_computation | async-start | bytes 3145728 | tf_op jit(solution)/shard_map/all_to_all | solution.py:335
  12.0 3.3 %turn.1 = (bf16[768,256]{1,0:T(8,128)(2,1)}, bf16[768,256]{1,0:T(8,128)(2,1)}, bf16[384,256]{1,0:T(8,128)(2,1)}) custom-call(s32[69]{0:T(128)} %concatenate.3.refs_0_.ids, bf16[256,3072]{1,0:T(8,128)(2,1)} %bitcast.19), custom_call_target="tpu_custom_call" | custom-call | tf_op jit(solution)/shard_map/turn/pallas_call | solution.py:99
  15.3 1.9 %collective-permute-start.4 = (bf16[768,256]{1,0:T(8,128)(2,1)}, bf16[768,256]{1,0:T(8,128)(2,1)S(1)}, u32[]{:S(2)}, u32[]{:S(2)}) collective-permute-start(bf16[768,256]{1,0:T(8,128)(2,1)} %get-tuple-element.25), channel_id=1, source_target_pairs={{0,1},{1,2},{2,3},{3,0},{4,7},{5,4},{6,5},{7,6},{8,9},{9,10},{10,1... | collective-permute-start | bytes 1179656 | tf_op jit(solution)/shard_map/ppermute | solution.py:382
  17.1 3.3 %copy.14 = bf16[384,8,2,384]{3,1,2,0:T(8,128)(2,1)S(1)} copy(bf16[384,8,2,384]{3,2,1,0:T(2,128)(2,1)} %bitcast.17) | data formatting | bytes 9437184
  20.4 1.4 %convolution_convert_fusion.refs_2_ = bf16[256,768]{1,0:T(8,128)(2,1)S(1)} fusion(bf16[3072,768]{1,0:T(8,128)(2,1)S(1)} %bitcast.18, bf16[1,256,3072]{2,1,0:T(8,128)(2,1)S(1)} %copy-done.1), kind=kOutput, calls=%fused_computation | convolution fusion | flops 1208156160 | bytes 6684672 | tf_op jit(solution)/shard_map/dot_general | solution.py:372
  21.9 2.7 %collective-permute-start.1 = (bf16[256,768]{1,0:T(8,128)(2,1)S(1)}, bf16[256,768]{1,0:T(8,128)(2,1)S(1)}, u32[]{:S(2)}, u32[]{:S(2)}) collective-permute-start(bf16[256,768]{1,0:T(8,128)(2,1)S(1)} %convolution_convert_fusion.refs_2_), channel_id=1, source_target_pairs={{0,3},{1,0},{2,1},{3,2},{4,7},{5,4},{6,5},{7,6},{8,11},{9,8},{10,9... | collective-permute-start | bytes 1179656 | tf_op jit(solution)/shard_map/ppermute | solution.py:27
  25.7 10.6 %collective-permute-done.5.far = bf16[384,256]{1,0:T(8,128)(2,1)S(1)} collective-permute-done((bf16[384,256]{1,0:T(8,128)(2,1)S(1)}, bf16[384,256]{1,0:T(8,128)(2,1)S(1)}, u32[]{:S(2)}, u32[]{:S(2)}) %collective-permute-start.5) | collective-permute-done | bytes 196640 | tf_op jit(solution)/shard_map/ppermute | solution.py:27
  36.3 1.7 %collective-permute-start.7 = (bf16[384,256]{1,0:T(8,128)(2,1)S(1)}, bf16[384,256]{1,0:T(8,128)(2,1)S(1)}, u32[]{:S(2)}, u32[]{:S(2)}) collective-permute-start(bf16[384,256]{1,0:T(8,128)(2,1)S(1)} %collective-permute-done.5.far), channel_id=1, source_target_pairs={{0,4},{4,0},{8,12},{12,8},{16,20},{20,16},{24,28},{28,24},{1,5},{5... | collective-permute-start | bytes 589832 | tf_op jit(solution)/shard_map/ppermute | solution.py:393
  38.7 1.5 %collective-permute-start.2 = (bf16[128,768]{1,0:T(8,128)(2,1)}, bf16[128,768]{1,0:T(8,128)(2,1)}, u32[]{:S(2)}, u32[]{:S(2)}) collective-permute-start(bf16[128,768]{1,0:T(8,128)(2,1)} %slice.40), channel_id=1, source_target_pairs={{0,1},{1,2},{2,3},{3,0},{4,5},{5,6},{6,7},{7,4},{8,9},{9,10},{10,1... | collective-permute-start | bytes 589832 | tf_op jit(solution)/shard_map/ppermute | solution.py:27
  43.5 2.4 %assemble.1.rest = bf16[768,768]{1,0:T(8,128)(2,1)} custom-call(s32[69]{0:T(128)} %concatenate.3.refs_0_.ids, bf16[768,256]{1,0:T(8,128)(2,1)} %copy-done.6, bf16[384,256]{1,0:T(8,128)(2,1)} %copy-done.11, bf16[768,256]{1,0:T(8,128)(2,1)} %copy-done.7, bf16[384,256]{1,0:T(8,128)(2,1)} %copy-done.12), custom_call_target="tpu_custom_call" | custom-call | tf_op jit(solution)/shard_map/assemble/pallas_call | solution.py:264
  45.9 5.6 %collective-permute-start.16 = (bf16[768,768]{1,0:T(8,128)(2,1)}, bf16[768,768]{1,0:T(8,128)(2,1)}, u32[]{:S(2)}, u32[]{:S(2)}) collective-permute-start(bf16[768,768]{1,0:T(8,128)(2,1)} %assemble.1.rest), channel_id=1, source_target_pairs={{0,32},{4,228},{8,40},{12,236},{16,48},{20,244},{24,56},{28,252},{... | collective-permute-start | bytes 3538952 | tf_op jit(solution)/shard_map/ppermute | solution.py:395
  51.5 6.4 %attend.1 = (bf16[8,2,128,384]{3,2,1,0:T(8,128)(2,1)}, f32[256,768]{1,0:T(8,128)}, bf16[256,768]{1,0:T(8,128)(2,1)}, bf16[256,768]{1,0:T(8,128)(2,1)}, bf16[256,768]{1,0:T(8,128)(2,1)}) custom-call(s32[69]{0:T(128)} %concatenate.3.refs_0_.ids, bf16[8,2,128,384]{3,2,1,0:T(8,128)(2,1)S(1)} %all-to-all-done.refs_1_, bf16[256,768]{1,0:T(8,128)(2,1)} %copy-done.8, ...), custom_call_target="tpu_custom_call" | custom-call | tf_op jit(solution)/shard_map/attend/pallas_call | solution.py:227
  60.3 5.1 %all-to-all-start.1 = ((bf16[8,2,128,384]{3,2,1,0:T(8,128)(2,1)}), bf16[8,2,128,384]{3,2,1,0:T(8,128)(2,1)S(1)}, u32[]{:S(2)}, u32[]{:S(2)}) async-start(bf16[8,2,128,384]{3,2,1,0:T(8,128)(2,1)} %get-tuple-element.21), calls=%async_computation.1 | async-start | bytes 3145728 | tf_op jit(solution)/shard_map/all_to_all | solution.py:335
  65.4 4.1 %collective-permute-start.8 = (bf16[768,256]{1,0:T(8,128)(2,1)}, bf16[768,256]{1,0:T(8,128)(2,1)S(1)}, u32[]{:S(2)}, u32[]{:S(2)}) collective-permute-start(bf16[768,256]{1,0:T(8,128)(2,1)} %get-tuple-element.24.held), channel_id=1, source_target_pairs={{0,32},{4,228},{8,40},{12,236},{16,48},{20,244},{24,56},{28,252},{... | collective-permute-start | bytes 1179656 | tf_op jit(solution)/shard_map/ppermute | solution.py:384
  69.5 1.4 %collective-permute-done.10 = bf16[256,768]{1,0:T(8,128)(2,1)S(1)} collective-permute-done((bf16[256,768]{1,0:T(8,128)(2,1)}, bf16[256,768]{1,0:T(8,128)(2,1)S(1)}, u32[]{:S(2)}, u32[]{:S(2)}) %collective-permute-start.10) | collective-permute-done | bytes 393248 | tf_op jit(solution)/shard_map/ppermute | solution.py:27
  70.9 5.9 %collective-permute-done.11 = bf16[256,768]{1,0:T(8,128)(2,1)S(1)} collective-permute-done((bf16[256,768]{1,0:T(8,128)(2,1)}, bf16[256,768]{1,0:T(8,128)(2,1)S(1)}, u32[]{:S(2)}, u32[]{:S(2)}) %collective-permute-start.11) | collective-permute-done | bytes 393248 | tf_op jit(solution)/shard_map/ppermute | solution.py:27
  78.1 3.4 %collective-permute-start.12 = (bf16[256,384]{1,0:T(8,128)(2,1)S(1)}, bf16[256,384]{1,0:T(8,128)(2,1)S(1)}, u32[]{:S(2)}, u32[]{:S(2)}) collective-permute-start(bf16[256,384]{1,0:T(8,128)(2,1)S(1)} %get-tuple-element.46), channel_id=1, source_target_pairs={{0,32},{4,228},{8,40},{12,236},{16,48},{20,244},{24,56},{28,252},{... | collective-permute-start | bytes 589832 | tf_op jit(solution)/shard_map/ppermute | solution.py:398
  82.6 3.0 %collective-permute-start.14 = (bf16[256,384]{1,0:T(8,128)(2,1)S(1)}, bf16[256,384]{1,0:T(8,128)(2,1)S(1)}, u32[]{:S(2)}, u32[]{:S(2)}) collective-permute-start(bf16[256,384]{1,0:T(8,128)(2,1)S(1)} %get-tuple-element.45.refs_0_), channel_id=1, source_target_pairs={{0,2},{1,3},{2,0},{3,1},{4,6},{5,7},{6,4},{7,5},{8,10},{9,11},{10,... | collective-permute-start | bytes 589832 | tf_op jit(solution)/shard_map/ppermute | solution.py:27
  87.0 3.4 %collective-permute-done.13.refs_1_ = bf16[256,384]{1,0:T(8,128)(2,1)S(1)} collective-permute-done((bf16[256,384]{1,0:T(8,128)(2,1)S(1)}, bf16[256,384]{1,0:T(8,128)(2,1)S(1)}, u32[]{:S(2)}, u32[]{:S(2)}) %collective-permute-start.13) | collective-permute-done | bytes 196640 | tf_op jit(solution)/shard_map/ppermute | solution.py:27
  90.4 2.1 %collective-permute-start.18 = (bf16[256,384]{1,0:T(8,128)(2,1)S(1)}, bf16[256,384]{1,0:T(8,128)(2,1)S(1)}, u32[]{:S(2)}, u32[]{:S(2)}) collective-permute-start(bf16[256,384]{1,0:T(8,128)(2,1)S(1)} %collective-permute-done.12.came), channel_id=1, source_target_pairs={{0,2},{1,3},{2,0},{3,1},{4,6},{5,7},{6,4},{7,5},{8,10},{9,11},{10,... | collective-permute-start | bytes 589832 | tf_op jit(solution)/shard_map/ppermute | solution.py:27
  92.5 2.7 %collective-permute-done.14.refs_2_ = bf16[256,384]{1,0:T(8,128)(2,1)S(1)} collective-permute-done((bf16[256,384]{1,0:T(8,128)(2,1)S(1)}, bf16[256,384]{1,0:T(8,128)(2,1)S(1)}, u32[]{:S(2)}, u32[]{:S(2)}) %collective-permute-start.14) | collective-permute-done | bytes 196640 | tf_op jit(solution)/shard_map/ppermute | solution.py:27
  95.3 3.8 %first_product.1.refs_1_ = f32[768,384]{1,0:T(8,128)} custom-call(bf16[768,256]{1,0:T(8,128)(2,1)} %get-tuple-element.24.held, bf16[768,768]{1,0:T(8,128)(2,1)} %assemble.1.rest, bf16[768,256]{1,0:T(8,128)(2,1)} %copy-done.9, bf16[256,384]{1,0:T(8,128)(2,1)} %copy-done.10, bf16[256,384]{1,0:T(8,128)(2,1)} %copy-done.4, ...), custom_call_target="tpu_custom_call" | custom-call | tf_op jit(solution)/shard_map/first_product/pallas_call | solution.py:284
  99.1 1.6 %collective-permute-done.18.refs_4_ = bf16[256,384]{1,0:T(8,128)(2,1)S(1)} collective-permute-done((bf16[256,384]{1,0:T(8,128)(2,1)S(1)}, bf16[256,384]{1,0:T(8,128)(2,1)S(1)}, u32[]{:S(2)}, u32[]{:S(2)}) %collective-permute-start.18) | collective-permute-done | bytes 196640 | tf_op jit(solution)/shard_map/ppermute | solution.py:27
  100.9 3.3 %second_product.1 = (f32[96,384]{1,0:T(8,128)}, bf16[96,384]{1,0:T(8,128)(2,1)}, bf16[96,384]{1,0:T(8,128)(2,1)}, bf16[96,384]{1,0:T(8,128)(2,1)}, bf16[96,384]{...) custom-call(s32[69]{0:T(128)} %concatenate.3.refs_0_.ids, ...), custom_call_target="tpu_custom_call" | custom-call | tf_op jit(solution)/shard_map/second_product/pallas_call | solution.py:313
  104.2 3.9 %collective-permute-start.21 = (bf16[96,384]{1,0:T(8,128)(2,1)}, bf16[96,384]{1,0:T(8,128)(2,1)S(1)}, u32[]{:S(2)}, u32[]{:S(2)}) collective-permute-start(bf16[96,384]{1,0:T(8,128)(2,1)} %get-tuple-element.32), channel_id=1, source_target_pairs={{0,96},{32,128},{64,160},{96,192},{128,224},{160,0},{192,32},{224,... | collective-permute-start | bytes 221192 | tf_op jit(solution)/shard_map/ppermute | solution.py:27
  108.7 1.9 %collective-permute-start.23 = (bf16[96,384]{1,0:T(8,128)(2,1)}, bf16[96,384]{1,0:T(8,128)(2,1)S(1)}, u32[]{:S(2)}, u32[]{:S(2)}) collective-permute-start(bf16[96,384]{1,0:T(8,128)(2,1)} %get-tuple-element.34), channel_id=1, source_target_pairs={{0,224},{32,0},{64,32},{96,64},{128,96},{160,128},{192,160},{224,1... | collective-permute-start | bytes 221192 | tf_op jit(solution)/shard_map/ppermute | solution.py:27
  110.6 2.1 %collective-permute-start.24 = (bf16[96,384]{1,0:T(8,128)(2,1)}, bf16[96,384]{1,0:T(8,128)(2,1)S(1)}, u32[]{:S(2)}, u32[]{:S(2)}) collective-permute-start(bf16[96,384]{1,0:T(8,128)(2,1)} %get-tuple-element.36), channel_id=1, source_target_pairs={{0,64},{32,96},{64,128},{96,160},{128,192},{160,224},{192,0},{224,... | collective-permute-start | bytes 221192 | tf_op jit(solution)/shard_map/ppermute | solution.py:27
  112.7 2.2 %collective-permute-start.25 = (bf16[96,384]{1,0:T(8,128)(2,1)}, bf16[96,384]{1,0:T(8,128)(2,1)S(1)}, u32[]{:S(2)}, u32[]{:S(2)}) collective-permute-start(bf16[96,384]{1,0:T(8,128)(2,1)} %get-tuple-element.37), channel_id=1, source_target_pairs={{0,128},{32,160},{64,192},{96,224},{128,0},{160,32},{192,64},{224,... | collective-permute-start | bytes 221192 | tf_op jit(solution)/shard_map/ppermute | solution.py:27
  114.9 2.4 %collective-permute-start.26 = (bf16[96,384]{1,0:T(8,128)(2,1)}, bf16[96,384]{1,0:T(8,128)(2,1)S(1)}, u32[]{:S(2)}, u32[]{:S(2)}) collective-permute-start(bf16[96,384]{1,0:T(8,128)(2,1)} %get-tuple-element.38), channel_id=1, source_target_pairs={{0,192},{32,224},{64,0},{96,32},{128,64},{160,96},{192,128},{224,1... | collective-permute-start | bytes 221192 | tf_op jit(solution)/shard_map/ppermute | solution.py:27
  117.3 5.6 %collective-permute-done.25 = bf16[96,384]{1,0:T(8,128)(2,1)S(1)} collective-permute-done((bf16[96,384]{1,0:T(8,128)(2,1)}, bf16[96,384]{1,0:T(8,128)(2,1)S(1)}, u32[]{:S(2)}, u32[]{:S(2)}) %collective-permute-start.25) | collective-permute-done | bytes 73760 | tf_op jit(solution)/shard_map/ppermute | solution.py:27
  126.9 2.7 %unpack.1 = (bf16[128,3072]{1,0:T(8,128)(2,1)}, bf16[128,3072]{1,0:T(8,128)(2,1)}) custom-call(bf16[8,2,128,384]{3,2,1,0:T(8,128)(2,1)} %copy-done), custom_call_target="tpu_custom_call" | custom-call | tf_op jit(solution)/shard_map/unpack/pallas_call | solution.py:62
  (74 shorter events, 17.2 us)
Async XLA Ops:
  3.0 48.5 %all-to-all-start = ((bf16[8,2,128,384]{3,2,1,0:T(8,128)(2,1)}), bf16[8,2,128,384]{3,2,1,0:T(8,128)(2,1)S(1)}, u32[]{:S(2)}, u32[]{:S(2)}) async-start(bf16[8,2,128,384]{3,2,1,0:T(8,128)(2,1)} %pack.1), calls=%async_computation | async-start | bytes 3145728 | tf_op jit(solution)/shard_map/all_to_all | solution.py:335
  15.3 9.3 %collective-permute-start.4 = (bf16[768,256]{1,0:T(8,128)(2,1)}, bf16[768,256]{1,0:T(8,128)(2,1)S(1)}, u32[]{:S(2)}, u32[]{:S(2)}) collective-permute-start(bf16[768,256]{1,0:T(8,128)(2,1)} %get-tuple-element.25), channel_id=1, source_target_pairs={{0,1},{1,2},{2,3},{3,0},{4,7},{5,4},{6,5},{7,6},{8,9},{9,10},{10,1... | collective-permute-start | bytes 1179656 | tf_op jit(solution)/shard_map/ppermute | solution.py:382
  21.8 29.7 %copy-start.8 = (bf16[256,768]{1,0:T(8,128)(2,1)}, bf16[256,768]{1,0:T(8,128)(2,1)S(1)}, u32[]{:S(2)}) copy-start(bf16[256,768]{1,0:T(8,128)(2,1)S(1)} %convolution_convert_fusion.refs_2_) | copy-start | bytes 1179652
  21.9 16.1 %collective-permute-start = (bf16[256,768]{1,0:T(8,128)(2,1)S(1)}, bf16[256,768]{1,0:T(8,128)(2,1)S(1)}, u32[]{:S(2)}, u32[]{:S(2)}) collective-permute-start(bf16[256,768]{1,0:T(8,128)(2,1)S(1)} %convolution_convert_fusion.refs_2_), channel_id=1, source_target_pairs={{0,1},{1,2},{2,3},{3,0},{4,5},{5,6},{6,7},{7,4},{8,9},{9,10},{10,1... | collective-permute-start | bytes 1179656 | tf_op jit(solution)/shard_map/ppermute | solution.py:27
  21.9 18.2 %collective-permute-start.1 = (bf16[256,768]{1,0:T(8,128)(2,1)S(1)}, bf16[256,768]{1,0:T(8,128)(2,1)S(1)}, u32[]{:S(2)}, u32[]{:S(2)}) collective-permute-start(bf16[256,768]{1,0:T(8,128)(2,1)S(1)} %convolution_convert_fusion.refs_2_), channel_id=1, source_target_pairs={{0,3},{1,0},{2,1},{3,2},{4,7},{5,4},{6,5},{7,6},{8,11},{9,8},{10,9... | collective-permute-start | bytes 1179656 | tf_op jit(solution)/shard_map/ppermute | solution.py:27
  24.6 11.7 %collective-permute-start.5 = (bf16[384,256]{1,0:T(8,128)(2,1)S(1)}, bf16[384,256]{1,0:T(8,128)(2,1)S(1)}, u32[]{:S(2)}, u32[]{:S(2)}) collective-permute-start(bf16[384,256]{1,0:T(8,128)(2,1)S(1)} %copy-done.14), channel_id=1, source_target_pairs={{0,2},{1,3},{2,0},{3,1},{4,6},{5,7},{6,4},{7,5},{8,10},{9,11},{10,... | collective-permute-start | bytes 589832 | tf_op jit(solution)/shard_map/ppermute | solution.py:27
  24.6 18.1 %copy-start.6 = (bf16[768,256]{1,0:T(8,128)(2,1)}, bf16[768,256]{1,0:T(8,128)(2,1)S(1)}, u32[]{:S(2)}) copy-start(bf16[768,256]{1,0:T(8,128)(2,1)S(1)} %collective-permute-done.4.near) | copy-start | bytes 1179652
  24.6 18.1 %collective-permute-start.6 = (bf16[768,256]{1,0:T(8,128)(2,1)S(1)}, bf16[768,256]{1,0:T(8,128)(2,1)S(1)}, u32[]{:S(2)}, u32[]{:S(2)}) collective-permute-start(bf16[768,256]{1,0:T(8,128)(2,1)S(1)} %collective-permute-done.4.near), channel_id=1, source_target_pairs={{0,4},{4,0},{8,12},{12,8},{16,20},{20,16},{24,28},{28,24},{1,5},{5... | collective-permute-start | bytes 1179656 | tf_op jit(solution)/shard_map/ppermute | solution.py:392
  36.3 5.8 %collective-permute-start.7 = (bf16[384,256]{1,0:T(8,128)(2,1)S(1)}, bf16[384,256]{1,0:T(8,128)(2,1)S(1)}, u32[]{:S(2)}, u32[]{:S(2)}) collective-permute-start(bf16[384,256]{1,0:T(8,128)(2,1)S(1)} %collective-permute-done.5.far), channel_id=1, source_target_pairs={{0,4},{4,0},{8,12},{12,8},{16,20},{20,16},{24,28},{28,24},{1,5},{5... | collective-permute-start | bytes 589832 | tf_op jit(solution)/shard_map/ppermute | solution.py:393
  38.7 12.8 %collective-permute-start.2 = (bf16[128,768]{1,0:T(8,128)(2,1)}, bf16[128,768]{1,0:T(8,128)(2,1)}, u32[]{:S(2)}, u32[]{:S(2)}) collective-permute-start(bf16[128,768]{1,0:T(8,128)(2,1)} %slice.40), channel_id=1, source_target_pairs={{0,1},{1,2},{2,3},{3,0},{4,5},{5,6},{6,7},{7,4},{8,9},{9,10},{10,1... | collective-permute-start | bytes 589832 | tf_op jit(solution)/shard_map/ppermute | solution.py:27
  40.9 10.6 %collective-permute-start.3 = (bf16[128,768]{1,0:T(8,128)(2,1)}, bf16[128,768]{1,0:T(8,128)(2,1)}, u32[]{:S(2)}, u32[]{:S(2)}) collective-permute-start(bf16[128,768]{1,0:T(8,128)(2,1)} %slice.41), channel_id=1, source_target_pairs={{0,3},{1,0},{2,1},{3,2},{4,7},{5,4},{6,5},{7,6},{8,11},{9,8},{10,9... | collective-permute-start | bytes 589832 | tf_op jit(solution)/shard_map/ppermute | solution.py:27
  45.9 53.2 %collective-permute-start.16 = (bf16[768,768]{1,0:T(8,128)(2,1)}, bf16[768,768]{1,0:T(8,128)(2,1)}, u32[]{:S(2)}, u32[]{:S(2)}) collective-permute-start(bf16[768,768]{1,0:T(8,128)(2,1)} %assemble.1.rest), channel_id=1, source_target_pairs={{0,32},{4,228},{8,40},{12,236},{16,48},{20,244},{24,56},{28,252},{... | collective-permute-start | bytes 3538952 | tf_op jit(solution)/shard_map/ppermute | solution.py:395
  58.0 13.0 %collective-permute-start.10 = (bf16[256,768]{1,0:T(8,128)(2,1)}, bf16[256,768]{1,0:T(8,128)(2,1)S(1)}, u32[]{:S(2)}, u32[]{:S(2)}) collective-permute-start(bf16[256,768]{1,0:T(8,128)(2,1)} %get-tuple-element.29), channel_id=1, source_target_pairs={{0,2},{1,3},{2,0},{3,1},{4,6},{5,7},{6,4},{7,5},{8,10},{9,11},{10,... | collective-permute-start | bytes 1179656 | tf_op jit(solution)/shard_map/ppermute | solution.py:27
  58.9 18.0 %collective-permute-start.11 = (bf16[256,768]{1,0:T(8,128)(2,1)}, bf16[256,768]{1,0:T(8,128)(2,1)S(1)}, u32[]{:S(2)}, u32[]{:S(2)}) collective-permute-start(bf16[256,768]{1,0:T(8,128)(2,1)} %get-tuple-element.30), channel_id=1, source_target_pairs={{0,3},{1,0},{2,1},{3,2},{4,7},{5,4},{6,5},{7,6},{8,11},{9,8},{10,9... | collective-permute-start | bytes 1179656 | tf_op jit(solution)/shard_map/ppermute | solution.py:27
  60.2 16.7 %collective-permute-start.9 = (bf16[256,768]{1,0:T(8,128)(2,1)}, bf16[256,768]{1,0:T(8,128)(2,1)}, u32[]{:S(2)}, u32[]{:S(2)}) collective-permute-start(bf16[256,768]{1,0:T(8,128)(2,1)} %get-tuple-element.28), channel_id=1, source_target_pairs={{0,1},{1,2},{2,3},{3,0},{4,5},{5,6},{6,7},{7,4},{8,9},{9,10},{10,1... | collective-permute-start | bytes 1179656 | tf_op jit(solution)/shard_map/ppermute | solution.py:27
  60.3 65.4 %all-to-all-start.1 = ((bf16[8,2,128,384]{3,2,1,0:T(8,128)(2,1)}), bf16[8,2,128,384]{3,2,1,0:T(8,128)(2,1)S(1)}, u32[]{:S(2)}, u32[]{:S(2)}) async-start(bf16[8,2,128,384]{3,2,1,0:T(8,128)(2,1)} %get-tuple-element.21), calls=%async_computation.1 | async-start | bytes 3145728 | tf_op jit(solution)/shard_map/all_to_all | solution.py:335
  65.4 20.1 %collective-permute-start.8 = (bf16[768,256]{1,0:T(8,128)(2,1)}, bf16[768,256]{1,0:T(8,128)(2,1)S(1)}, u32[]{:S(2)}, u32[]{:S(2)}) collective-permute-start(bf16[768,256]{1,0:T(8,128)(2,1)} %get-tuple-element.24.held), channel_id=1, source_target_pairs={{0,32},{4,228},{8,40},{12,236},{16,48},{20,244},{24,56},{28,252},{... | collective-permute-start | bytes 1179656 | tf_op jit(solution)/shard_map/ppermute | solution.py:384
  78.1 17.2 %copy-start.4 = (bf16[256,384]{1,0:T(8,128)(2,1)}, bf16[256,384]{1,0:T(8,128)(2,1)S(1)}, u32[]{:S(2)}) copy-start(bf16[256,384]{1,0:T(8,128)(2,1)S(1)} %get-tuple-element.45.refs_0_) | copy-start | bytes 589828
  78.1 8.1 %collective-permute-start.12 = (bf16[256,384]{1,0:T(8,128)(2,1)S(1)}, bf16[256,384]{1,0:T(8,128)(2,1)S(1)}, u32[]{:S(2)}, u32[]{:S(2)}) collective-permute-start(bf16[256,384]{1,0:T(8,128)(2,1)S(1)} %get-tuple-element.46), channel_id=1, source_target_pairs={{0,32},{4,228},{8,40},{12,236},{16,48},{20,244},{24,56},{28,252},{... | collective-permute-start | bytes 589832 | tf_op jit(solution)/shard_map/ppermute | solution.py:398
  81.5 8.9 %collective-permute-start.13 = (bf16[256,384]{1,0:T(8,128)(2,1)S(1)}, bf16[256,384]{1,0:T(8,128)(2,1)S(1)}, u32[]{:S(2)}, u32[]{:S(2)}) collective-permute-start(bf16[256,384]{1,0:T(8,128)(2,1)S(1)} %get-tuple-element.45.refs_0_), channel_id=1, source_target_pairs={{0,1},{1,2},{2,3},{3,0},{4,5},{5,6},{6,7},{7,4},{8,9},{9,10},{10,1... | collective-permute-start | bytes 589832 | tf_op jit(solution)/shard_map/ppermute | solution.py:27
  82.6 12.7 %collective-permute-start.14 = (bf16[256,384]{1,0:T(8,128)(2,1)S(1)}, bf16[256,384]{1,0:T(8,128)(2,1)S(1)}, u32[]{:S(2)}, u32[]{:S(2)}) collective-permute-start(bf16[256,384]{1,0:T(8,128)(2,1)S(1)} %get-tuple-element.45.refs_0_), channel_id=1, source_target_pairs={{0,2},{1,3},{2,0},{3,1},{4,6},{5,7},{6,4},{7,5},{8,10},{9,11},{10,... | collective-permute-start | bytes 589832 | tf_op jit(solution)/shard_map/ppermute | solution.py:27
  85.5 9.7 %collective-permute-start.15 = (bf16[256,384]{1,0:T(8,128)(2,1)S(1)}, bf16[256,384]{1,0:T(8,128)(2,1)S(1)}, u32[]{:S(2)}, u32[]{:S(2)}) collective-permute-start(bf16[256,384]{1,0:T(8,128)(2,1)S(1)} %get-tuple-element.45.refs_0_), channel_id=1, source_target_pairs={{0,3},{1,0},{2,1},{3,2},{4,7},{5,4},{6,5},{7,6},{8,11},{9,8},{10,9... | collective-permute-start | bytes 589832 | tf_op jit(solution)/shard_map/ppermute | solution.py:27
  86.1 13.0 %collective-permute-start.17 = (bf16[256,384]{1,0:T(8,128)(2,1)S(1)}, bf16[256,384]{1,0:T(8,128)(2,1)S(1)}, u32[]{:S(2)}, u32[]{:S(2)}) collective-permute-start(bf16[256,384]{1,0:T(8,128)(2,1)S(1)} %collective-permute-done.12.came), channel_id=1, source_target_pairs={{0,1},{1,2},{2,3},{3,0},{4,5},{5,6},{6,7},{7,4},{8,9},{9,10},{10,1... | collective-permute-start | bytes 589832 | tf_op jit(solution)/shard_map/ppermute | solution.py:27
  90.4 10.3 %collective-permute-start.18 = (bf16[256,384]{1,0:T(8,128)(2,1)S(1)}, bf16[256,384]{1,0:T(8,128)(2,1)S(1)}, u32[]{:S(2)}, u32[]{:S(2)}) collective-permute-start(bf16[256,384]{1,0:T(8,128)(2,1)S(1)} %collective-permute-done.12.came), channel_id=1, source_target_pairs={{0,2},{1,3},{2,0},{3,1},{4,6},{5,7},{6,4},{7,5},{8,10},{9,11},{10,... | collective-permute-start | bytes 589832 | tf_op jit(solution)/shard_map/ppermute | solution.py:27
  95.2 5.7 %collective-permute-start.19 = (bf16[256,384]{1,0:T(8,128)(2,1)S(1)}, bf16[256,384]{1,0:T(8,128)(2,1)S(1)}, u32[]{:S(2)}, u32[]{:S(2)}) collective-permute-start(bf16[256,384]{1,0:T(8,128)(2,1)S(1)} %collective-permute-done.12.came), channel_id=1, source_target_pairs={{0,3},{1,0},{2,1},{3,2},{4,7},{5,4},{6,5},{7,6},{8,11},{9,8},{10,9... | collective-permute-start | bytes 589832 | tf_op jit(solution)/shard_map/ppermute | solution.py:27
  104.2 8.6 %collective-permute-start.20 = (bf16[96,384]{1,0:T(8,128)(2,1)}, bf16[96,384]{1,0:T(8,128)(2,1)S(1)}, u32[]{:S(2)}, u32[]{:S(2)}) collective-permute-start(bf16[96,384]{1,0:T(8,128)(2,1)} %get-tuple-element.31), channel_id=1, source_target_pairs={{0,32},{32,64},{64,96},{96,128},{128,160},{160,192},{192,224},{224... | collective-permute-start | bytes 221192 | tf_op jit(solution)/shard_map/ppermute | solution.py:27
  104.2 10.7 %collective-permute-start.21 = (bf16[96,384]{1,0:T(8,128)(2,1)}, bf16[96,384]{1,0:T(8,128)(2,1)S(1)}, u32[]{:S(2)}, u32[]{:S(2)}) collective-permute-start(bf16[96,384]{1,0:T(8,128)(2,1)} %get-tuple-element.32), channel_id=1, source_target_pairs={{0,96},{32,128},{64,160},{96,192},{128,224},{160,0},{192,32},{224,... | collective-permute-start | bytes 221192 | tf_op jit(solution)/shard_map/ppermute | solution.py:27
  108.1 9.2 %collective-permute-start.22 = (bf16[96,384]{1,0:T(8,128)(2,1)}, bf16[96,384]{1,0:T(8,128)(2,1)S(1)}, u32[]{:S(2)}, u32[]{:S(2)}) collective-permute-start(bf16[96,384]{1,0:T(8,128)(2,1)} %get-tuple-element.33), channel_id=1, source_target_pairs={{0,160},{32,192},{64,224},{96,0},{128,32},{160,64},{192,96},{224,1... | collective-permute-start | bytes 221192 | tf_op jit(solution)/shard_map/ppermute | solution.py:27
  108.7 8.6 %collective-permute-start.23 = (bf16[96,384]{1,0:T(8,128)(2,1)}, bf16[96,384]{1,0:T(8,128)(2,1)S(1)}, u32[]{:S(2)}, u32[]{:S(2)}) collective-permute-start(bf16[96,384]{1,0:T(8,128)(2,1)} %get-tuple-element.34), channel_id=1, source_target_pairs={{0,224},{32,0},{64,32},{96,64},{128,96},{160,128},{192,160},{224,1... | collective-permute-start | bytes 221192 | tf_op jit(solution)/shard_map/ppermute | solution.py:27
  110.6 6.7 %collective-permute-start.24 = (bf16[96,384]{1,0:T(8,128)(2,1)}, bf16[96,384]{1,0:T(8,128)(2,1)S(1)}, u32[]{:S(2)}, u32[]{:S(2)}) collective-permute-start(bf16[96,384]{1,0:T(8,128)(2,1)} %get-tuple-element.36), channel_id=1, source_target_pairs={{0,64},{32,96},{64,128},{96,160},{128,192},{160,224},{192,0},{224,... | collective-permute-start | bytes 221192 | tf_op jit(solution)/shard_map/ppermute | solution.py:27
  112.7 10.2 %collective-permute-start.25 = (bf16[96,384]{1,0:T(8,128)(2,1)}, bf16[96,384]{1,0:T(8,128)(2,1)S(1)}, u32[]{:S(2)}, u32[]{:S(2)}) collective-permute-start(bf16[96,384]{1,0:T(8,128)(2,1)} %get-tuple-element.37), channel_id=1, source_target_pairs={{0,128},{32,160},{64,192},{96,224},{128,0},{160,32},{192,64},{224,... | collective-permute-start | bytes 221192 | tf_op jit(solution)/shard_map/ppermute | solution.py:27
  114.9 8.9 %collective-permute-start.26 = (bf16[96,384]{1,0:T(8,128)(2,1)}, bf16[96,384]{1,0:T(8,128)(2,1)S(1)}, u32[]{:S(2)}, u32[]{:S(2)}) collective-permute-start(bf16[96,384]{1,0:T(8,128)(2,1)} %get-tuple-element.38), channel_id=1, source_target_pairs={{0,192},{32,224},{64,0},{96,32},{128,64},{160,96},{192,128},{224,1... | collective-permute-start | bytes 221192 | tf_op jit(solution)/shard_map/ppermute | solution.py:27
  (12 other events, 77.3 us)
